TPU v7x, 32 devices: a whole 2x2x4 slice. The times are simulated.
32 devices in a mesh: groups: 2 (over x), strip: 16 (over z, y, core).
Axes of the slice: x: 2, y: 2, z: 4, core: 2. Of those that a mesh axis runs over, the one named last changes fastest.
Arguments:
- queries: bfloat16 [32, 3, 128, 2240], P(('groups', 'strip')), parts along dimension 0, may hold values from -6 to 6
- keys: bfloat16 [32, 3, 128, 2240], P(('groups', 'strip')), parts along dimension 0, may hold values from -6 to 6
- values: bfloat16 [32, 3, 128, 2240], P(('groups', 'strip')), parts along dimension 0, may hold values from -6 to 6
- norm_gain: float32 [2240], replicated, may hold values from 0.1 to 1.9
- conv_weight: bfloat16 [3, 2240, 1152], P(None, None, 'strip'), may hold values from -0.078125 to 0.078125
Outputs:
- convolved: bfloat16 [32, 3, 128, 1152], P(('groups', 'strip')), parts along dimension 0
There are 2 independent parts, one for each index of `groups`. A program takes and returns all parts, laid end to end along the dimension named above; an argument that names none is the same for every part. Nothing has to cross between parts.
All inputs are finite; a program needn't handle non-finite values.
Results may differ from a plain program's by a relative error of at most 0.0051.
Values may be sent and summed in bfloat16 or wider, within the bound.
No kernel may reach another device: no remote copies, remote signals or barrier semaphores. Data moves between devices by JAX's collectives and lax.ppermute only.
A program may use at most 128 MiB of HBM per device.

v0:
```python
import jax
import jax.numpy as jnp
from jax import lax
from jax.sharding import PartitionSpec as P

H = 20
DH = 112
TB = 4
FB = 3
P_SIZE = 128


def from_behind(block, axis, distance):
    devices = range(lax.axis_size(axis))
    route = [(i - distance, i) for i in devices if i - distance in devices]
    return lax.ppermute(block, axis, route)


def per_device(queries, keys, values, norm_gain, conv_weight):
    devices = lax.axis_size("strip")
    strips = devices // TB
    block_index = lax.axis_index("strip") // strips
    count = FB * P_SIZE
    width = H * DH
    key_heads = jax.nn.relu(keys).reshape(count, H, DH)
    value_heads = values.reshape(count, H, DH)
    key_value = jnp.einsum(
        "nhd,nhe->hde", key_heads, value_heads, preferred_element_type=jnp.float32
    )
    key_sums = jnp.sum(key_heads, axis=0, dtype=jnp.float32)
    state_len = H * DH * DH
    raw_len = state_len + width
    row_len = (raw_len + devices - 1) // devices * devices
    row = jnp.concatenate(
        [key_value.reshape(-1), key_sums.reshape(-1), jnp.zeros((row_len - raw_len,), jnp.float32)]
    )
    later_blocks = (jnp.arange(TB) >= block_index).astype(jnp.float32)[:, None]
    share = lax.psum_scatter(later_blocks * row[None, :], "strip", scatter_dimension=1, tiled=True)
    outgoing = jnp.broadcast_to(share[:, None, :], (TB, strips, share.shape[1])).reshape(
        devices, share.shape[1]
    )
    returned = lax.all_to_all(outgoing, "strip", split_axis=0, concat_axis=1, tiled=True).reshape(
        -1
    )
    state = returned[:state_len].reshape(H, DH, DH)
    summed = returned[state_len:raw_len].reshape(H, DH)
    state_rounded = state.astype(jnp.bfloat16)
    query_heads = jax.nn.relu(queries).reshape(count, H, DH)
    numer = jnp.einsum(
        "nhd,hde->nhe", query_heads, state_rounded, preferred_element_type=jnp.float32
    )
    denom = (
        jnp.einsum(
            "nhd,hd->nh", query_heads.astype(jnp.float32), summed, precision=lax.Precision.HIGHEST
        )
        + 1e-06
    )
    attended = (numer / denom[..., None]).reshape(count, width)
    scale = lax.rsqrt(jnp.mean(attended * attended, axis=-1, keepdims=True) + 1e-06)
    normed = (attended * scale * norm_gain).astype(jnp.bfloat16).reshape(FB, P_SIZE, width)
    rim = from_behind(normed[-2:], "strip", strips)
    extended = jnp.concatenate([rim, normed], axis=0)
    stacked = jnp.concatenate([normed, extended[1:-1], extended[:-2]], axis=-1).reshape(
        -1, 3 * width
    )
    full_taps = lax.all_gather(conv_weight, "strip", axis=2, tiled=True)
    mixed = jnp.dot(
        stacked, full_taps.reshape(3 * width, -1), preferred_element_type=jnp.float32
    ).astype(jnp.bfloat16)
    result = mixed.reshape(FB, P_SIZE, mixed.shape[-1])
    return result.reshape(1, FB, P_SIZE, result.shape[-1])


def solution(mesh):
    placed = (
        P(("groups", "strip"), None, None, None),
        P(("groups", "strip"), None, None, None),
        P(("groups", "strip"), None, None, None),
        P(),
        P(None, None, "strip"),
    )
    return jax.shard_map(
        per_device,
        mesh=mesh,
        in_specs=placed,
        out_specs=P(("groups", "strip"), None, None, None),
        check_vma=False,
    )
```

profile of v0, /device:TPU:18, one launch (start us, length us, event | category | flops | bytes accessed | tf_op | source)
XLA Modules:
  0.0 373.2 jit_solution(15843581912796238540)
XLA Ops:
  9.9 8.8 %copy.43 = bf16[1,3,128,2240]{2,1,3,0:T(4,128)(2,1)S(1)} copy(bf16[1,3,128,2240]{2,3,1,0:T(8,128)(2,1)} %broadcast_maximum_fusion.1) | data formatting | bytes 3440640 | tf_op jit(solution)/shard_map/reshape | solution.py:25
  18.7 3.1 reshape.96
  21.8 8.8 %copy.44 = bf16[1,3,128,2240]{2,1,3,0:T(4,128)(2,1)S(1)} copy(bf16[1,3,128,2240]{2,3,1,0:T(8,128)(2,1)} %param.7) | data formatting | bytes 3440640 | tf_op jit(solution)/shard_map/reshape | solution.py:26
  30.6 3.1 reshape.97
  33.7 2.7 fusion.5
  37.4 6.1 %broadcast_multiply_fusion = f32[4,253120]{1,0:T(4,128)} fusion(f32[253120]{0:T(1024)S(1)} %pad_maximum_fusion.1, f32[4]{0:T(128)S(1)} %compare_convert_fusion), kind=kLoop, calls=%fused_computation.8 | loop fusion | flops 1012480 | bytes 5062416 | tf_op jit(solution)/shard_map/mul | solution.py:38
  45.5 108.0 %all-reduce.3.cloned.1.call-done = f32[4,253120]{1,0:T(4,128)} async-done(((f32[4,253120]{1,0:T(4,128)}), f32[4,253120]{1,0:T(4,128)}) %all-reduce.3.cloned.1.call-update) | async-done | bytes 4049936
  157.2 5.5 %all-to-all-start = ((f32[16,1,15820]{2,1,0:T(1,128)}), f32[16,1,15820]{2,1,0:T(1,128)S(1)}, u32[]{:S(2)}, u32[]{:S(2)}) async-start(f32[16,1,15820]{2,1,0:T(1,128)} %all_to_all.10), calls=%async_computation | async-start | bytes 2031616 | tf_op jit(solution)/shard_map/all_to_all | solution.py:42
  162.8 12.2 %copy.45 = bf16[1,3,128,2240]{2,1,3,0:T(4,128)(2,1)S(1)} copy(bf16[1,3,128,2240]{2,3,1,0:T(8,128)(2,1)S(1)} %broadcast_maximum_fusion) | data formatting | bytes 3440640 | tf_op jit(solution)/shard_map/reshape | solution.py:48
  175.0 3.1 reshape.98
  178.1 33.8 %all-to-all-done = f32[16,1,15820]{2,1,0:T(1,128)S(1)} async-done(((f32[16,1,15820]{2,1,0:T(1,128)}), f32[16,1,15820]{2,1,0:T(1,128)S(1)}, u32[]{:S(2)}, u32[]{:S(2)}) %all-to-all-start) | async-done | bytes 1012512 | tf_op jit(solution)/shard_map/all_to_all | solution.py:42
  211.8 2.6 convert_reduce_fusion.1
  216.7 3.7 reduce.3
  220.3 2.4 slice.23
  223.8 3.6 multiply_reduce_fusion
  227.4 3.5 copy.35
  234.3 2.7 copy.36
  239.1 3.7 reshape.99
  242.8 4.5 %copy.47 = f32[3,128,2240]{2,1,0:T(8,128)S(1)} copy(f32[3,128,2240]{1,0,2:T(4,128)} %reshape.99) | data formatting | bytes 6881280 | tf_op jit(solution)/shard_map/reshape | solution.py:58
  248.9 65.8 %collective-permute-done = bf16[2,128,2240]{1,2,0:T(8,128)(2,1)} collective-permute-done((bf16[2,128,2240]{1,2,0:T(8,128)(2,1)}, bf16[2,128,2240]{1,2,0:T(8,128)(2,1)}, u32[]{:S(2)}, u32[]{:S(2)}) %collective-permute-start) | collective-permute-done | bytes 1146912 | tf_op jit(solution)/shard_map/ppermute | solution.py:16
  317.1 3.7 pad_maximum_fusion
  320.7 9.4 %concatenate.18 = bf16[384,6720]{1,0:T(8,128)(2,1)} concatenate(bf16[384,2240]{1,0:T(8,128)(2,1)S(1)} %copy-done.2, bf16[384,2240]{1,0:T(8,128)(2,1)} %bitcast.39, bf16[384,2240]{1,0:T(8,128)(2,1)} %bitcast.38), dimensions={1} | concatenate | bytes 10321920 | tf_op jit(solution)/shard_map/concatenate | solution.py:63
  330.1 22.1 %copy.39 = bf16[3,2240,1152]{2,1,0:T(8,128)(2,1)} copy(bf16[3,2240,1152]{1,2,0:T(8,128)(2,1)} %all-gather.2.cloned.1.call-done) | data formatting | bytes 30965760 | tf_op jit(solution)/shard_map/all_gather | solution.py:66
  352.2 14.1 %convolution_convert_fusion = bf16[384,1152]{1,0:T(8,128)(2,1)} fusion(bf16[384,6720]{1,0:T(8,128)(2,1)} %concatenate.18, bf16[6720,1152]{1,0:T(8,128)(2,1)} %bitcast.36), kind=kOutput, calls=%fused_computation.7 | convolution fusion | flops 5945868288 | bytes 21528576 | tf_op jit(solution)/shard_map/dot_general | solution.py:67
  (47 shorter events, 22.2 us)
Async XLA Ops:
  6.5 2.0 copy-start.4
  6.5 146.9 %all-reduce.3.cloned.1.call-start = ((), (), s32[]{:S(2)}) async-start(), calls=%async_computation.2 | async-start | bytes 8101888
  43.5 0.8 copy-start.9
  43.5 286.6 %all-gather.2.cloned.1.call-start = ((), (), s32[]{:S(2)}) async-start(), calls=%async_computation.1 | async-start | bytes 16920576 | tf_op jit(solution)/shard_map/all_gather | solution.py:66
  157.2 5.5 %copy-start.6 = (bf16[1,3,128,2240]{2,3,1,0:T(8,128)(2,1)S(1)}, bf16[1,3,128,2240]{2,3,1,0:T(8,128)(2,1)}, u32[]{:S(2)}) copy-start(bf16[1,3,128,2240]{2,3,1,0:T(8,128)(2,1)} %param.5) | copy-start | bytes 5160964
  157.2 54.6 %all-to-all-start = ((f32[16,1,15820]{2,1,0:T(1,128)}), f32[16,1,15820]{2,1,0:T(1,128)S(1)}, u32[]{:S(2)}, u32[]{:S(2)}) async-start(f32[16,1,15820]{2,1,0:T(1,128)} %all_to_all.10), calls=%async_computation | async-start | bytes 2031616 | tf_op jit(solution)/shard_map/all_to_all | solution.py:42
  216.7 6.1 %copy-start.5 = (bf16[384,20,112]{0,2,1:T(8,128)(2,1)S(1)}, bf16[384,20,112]{0,2,1:T(8,128)(2,1)}, u32[]{:S(2)}) copy-start(bf16[384,20,112]{0,2,1:T(8,128)(2,1)} %reshape.98) | copy-start | bytes 5160964
  220.3 3.5 copy-start.7
  227.4 4.2 %copy-start.8 = (f32[2240]{0:T(1024)S(1)}, f32[2240]{0:T(1024)}, u32[]{:S(2)}) copy-start(f32[2240]{0:T(1024)} %param.8) | copy-start | bytes 26884
  231.9 1.2 copy-start.1
  233.1 6.0 %copy-start = (f32[384,20,112]{0,2,1:T(8,128)S(1)}, f32[384,20,112]{0,2,1:T(8,128)}, u32[]{:S(2)}) copy-start(f32[384,20,112]{0,2,1:T(8,128)} %get-tuple-element.10) | copy-start | bytes 10321924
  237.0 77.7 %collective-permute-start = (bf16[2,128,2240]{1,2,0:T(8,128)(2,1)}, bf16[2,128,2240]{1,2,0:T(8,128)(2,1)}, u32[]{:S(2)}, u32[]{:S(2)}) collective-permute-start(bf16[2,128,2240]{1,2,0:T(8,128)(2,1)} %copy.36), channel_id=1, source_target_pairs={{0,4},{1,5},{2,6},{3,7},{4,8},{5,9},{6,10},{7,11},{8,12},{9,13},{1... | collective-permute-start | bytes 3440648 | tf_op jit(solution)/shard_map/ppermute | solution.py:16
  248.9 68.2 %copy-start.3 = (bf16[3,128,2240]{2,1,0:T(8,128)(2,1)S(1)}, bf16[3,128,2240]{2,1,0:T(8,128)(2,1)}, u32[]{:S(2)}) copy-start(bf16[3,128,2240]{2,1,0:T(8,128)(2,1)} %multiply_convert_fusion) | copy-start | bytes 5160964
  317.1 3.7 copy-start.2
Sparse Core Ops, SparseCore 0:
  43.6 109.7 all-reduce.2
  155.6 159.3 all-gather.1
where the time goes:
time: 375 us; the launch traced here: 373 us
  waiting for transfers between devices  208 us (55%)
  local copies, waits for them, and re-layouts  99.5 us (27%)
  other arithmetic  22.2 us (6%)
  matrix products  21.4 us (6%)
  between operations  14.2 us (4%)
  starting transfers between devices  7.64 us (2%)
    unnamed x3, waiting for transfers between devices  109 us
    ppermute x1, waiting for transfers between devices, from_behind(): return lax.ppermute(block, axis, route)  65.8 us
    all_to_all x1, waiting for transfers between devices, per_device(): lax.all_to_all(outgoing, 'strip', split_axis=0, concat_axis=1, tiled=True)  33.8 us
    all_gather x1, local copies, waits for them, and re-layouts, per_device(): full_taps = lax.all_gather(conv_weight, 'strip', axis=2, tiled=True)  22.1 us
    reshape x2, local copies, waits for them, and re-layouts, per_device(): query_heads = jax.nn.relu(queries).reshape(count, H, DH)  15.3 us
    dot_general x1, matrix products, per_device(): jnp.dot(stacked, full_taps.reshape(3 * width, -1), preferred_element_type...  14.1 us
    reshape x2, local copies, waits for them, and re-layouts, per_device(): key_heads = jax.nn.relu(keys).reshape(count, H, DH)  11.9 us
    reshape x2, local copies, waits for them, and re-layouts, per_device(): value_heads = values.reshape(count, H, DH)  11.9 us
  transfers between devices with their start and end apart: 4, of which 3 were waited for; matrix products, arithmetic and copies ran while one was open for 18% of the time, Pallas kernels for 0%

commit v1 on v0

--- a/solution.py
+++ b/solution.py
@@ -1,13 +1,21 @@
+import functools
+
 import jax
 import jax.numpy as jnp
 from jax import lax
+from jax.experimental import pallas as pl
+from jax.experimental.pallas import tpu as pltpu
 from jax.sharding import PartitionSpec as P
+
 
 H = 20
 DH = 112
 TB = 4
-FB = 3
-P_SIZE = 128
+EPS = 1e-06
+LANES = 128
+ANY = pl.BlockSpec(memory_space=pl.ANY)
+VMEM = pl.BlockSpec(memory_space=pltpu.VMEM)
+SMEM = pl.BlockSpec(memory_space=pltpu.SMEM)
 
 
 def from_behind(block, axis, distance):
@@ -16,12 +24,12 @@
     return lax.ppermute(block, axis, route)
 
 
-def per_device(queries, keys, values, norm_gain, conv_weight):
+def generic(queries, keys, values, norm_gain, conv_weight):
+    _, frames, pixels, width = queries.shape
     devices = lax.axis_size("strip")
     strips = devices // TB
     block_index = lax.axis_index("strip") // strips
-    count = FB * P_SIZE
-    width = H * DH
+    count = frames * pixels
     key_heads = jax.nn.relu(keys).reshape(count, H, DH)
     value_heads = values.reshape(count, H, DH)
     key_value = jnp.einsum(
@@ -53,11 +61,11 @@
         jnp.einsum(
             "nhd,hd->nh", query_heads.astype(jnp.float32), summed, precision=lax.Precision.HIGHEST
         )
-        + 1e-06
+        + EPS
     )
     attended = (numer / denom[..., None]).reshape(count, width)
-    scale = lax.rsqrt(jnp.mean(attended * attended, axis=-1, keepdims=True) + 1e-06)
-    normed = (attended * scale * norm_gain).astype(jnp.bfloat16).reshape(FB, P_SIZE, width)
+    scale = lax.rsqrt(jnp.mean(attended * attended, axis=-1, keepdims=True) + EPS)
+    normed = (attended * scale * norm_gain).astype(jnp.bfloat16).reshape(frames, pixels, width)
     rim = from_behind(normed[-2:], "strip", strips)
     extended = jnp.concatenate([rim, normed], axis=0)
     stacked = jnp.concatenate([normed, extended[1:-1], extended[:-2]], axis=-1).reshape(
@@ -67,8 +75,384 @@
     mixed = jnp.dot(
         stacked, full_taps.reshape(3 * width, -1), preferred_element_type=jnp.float32
     ).astype(jnp.bfloat16)
-    result = mixed.reshape(FB, P_SIZE, mixed.shape[-1])
-    return result.reshape(1, FB, P_SIZE, result.shape[-1])
+    return mixed.reshape(1, frames, pixels, mixed.shape[-1])
+
+
+def vm(value):
+    return pltpu.with_memory_space_constraint(value, pltpu.VMEM)
+
+
+def limit(mib):
+    return pltpu.CompilerParams(vmem_limit_bytes=mib * 2**20)
+
+
+def slice_kernel(step, x_ref, from_ref, to_ref, sem):
+    at = pl.ds(pl.multiple_of(x_ref[0] * step, 8), to_ref.shape[0])
+    copy = pltpu.make_async_copy(from_ref.at[at, :], to_ref, sem)
+    copy.start()
+    copy.wait()
+
+
+def half_of(x, whole, half):
+    rows, width = whole.shape
+    return pl.pallas_call(
+        functools.partial(slice_kernel, rows - half),
+        in_specs=[SMEM, ANY],
+        out_specs=VMEM,
+        out_shape=pltpu.VMEM((half, width), whole.dtype),
+        scratch_shapes=[pltpu.SemaphoreType.DMA],
+        compiler_params=limit(4),
+        name="half_of",
+    )(x, whole)
+
+
+def state_kernel(mine, k_ref, v_ref, *outs):
+    step = pl.program_id(0)
+    frames, rows, pixels = k_ref.shape
+    heads = rows // DH
+    fill = (lax.broadcasted_iota(jnp.int32, (LANES - DH, frames * pixels), 0) == 0).astype(
+        jnp.bfloat16
+    )
+
+    for head in range(heads):
+        part = pl.ds(head * DH, DH)
+        k = jnp.concatenate([k_ref[f, part, :] for f in range(frames)], axis=1)
+        v = jnp.concatenate([v_ref[f, part, :] for f in range(frames)], axis=1)
+        k = jnp.maximum(k, jnp.zeros_like(k))
+        v = jnp.concatenate([v, fill], axis=0)
+        both = lax.dot_general(
+            k, v, (((1,), (1,)), ((), ())), preferred_element_type=jnp.float32
+        ).astype(jnp.bfloat16)
+        for i, out in enumerate(outs):
+
+            @pl.when(step % 2 == i)
+            def _(out=out):
+                out[part, :] = both
+
+
+def local_state(mine, keys, values):
+    frames, width, pixels = keys.shape
+    quarter = width // 4
+    spec = pl.BlockSpec((frames, quarter, pixels), lambda r, m: (0, r ^ m[0], 0))
+    return pl.pallas_call(
+        state_kernel,
+        grid_spec=pltpu.PrefetchScalarGridSpec(
+            num_scalar_prefetch=1,
+            grid=(4,),
+            in_specs=[spec, spec],
+            out_specs=[pl.BlockSpec((quarter, LANES), lambda r, m: (r // 2, 0))] * 2,
+        ),
+        out_shape=[jax.ShapeDtypeStruct((2 * quarter, LANES), jnp.bfloat16)] * 2,
+        name="local_state",
+    )(mine, keys, values)
+
+
+def add_up(*parts):
+    total = parts[0].astype(jnp.float32)
+    for part in parts[1:]:
+        total = total + part.astype(jnp.float32)
+    return total.astype(parts[0].dtype)
+
+
+def attend_kernel(chosen, mine, q_ref, s0, s1, s2, s3, gain_ref, out_ref, attended):
+    heads = s0.shape[0] // DH
+    lanes = out_ref.shape[1]
+    squares = jnp.zeros((8, lanes), jnp.float32)
+    for r, state_ref in enumerate((s0, s1, s2, s3)):
+        first = (r ^ mine[0]) * heads
+        for i in range(heads):
+            at = pl.ds(pl.multiple_of((first + i) * DH, 16), DH)
+            q = jnp.concatenate([q_ref[f, at, :] for f in chosen], axis=1)
+            q = jnp.maximum(q, jnp.zeros_like(q))
+            s = state_ref[pl.ds(i * DH, DH), :]
+            both = lax.dot_general(
+                s, q, (((0,), (0,)), ((), ())), preferred_element_type=jnp.float32
+            )
+            a = both[:DH] * (1.0 / (both[DH : DH + 1] + EPS))
+            attended[at, :] = a
+            squares = squares + jnp.sum((a * a).reshape(DH // 8, 8, lanes), axis=0)
+    width = attended.shape[0]
+    mean = jnp.sum(squares, axis=0, keepdims=True) / width
+    scale = lax.rsqrt(mean + EPS)
+    for i in range(width // DH):
+        at = pl.ds(i * DH, DH)
+        gain = gain_ref[at, :]
+        gain = jnp.concatenate([gain] * (lanes // LANES), axis=1)
+        out_ref[at, :] = (attended[at, :] * scale * gain).astype(out_ref.dtype)
+
+
+def attend(chosen, mine, queries, states, gain):
+    _, width, pixels = queries.shape
+    lanes = len(chosen) * pixels
+    return pl.pallas_call(
+        functools.partial(attend_kernel, chosen),
+        in_specs=[SMEM] + [VMEM] * 6,
+        out_specs=VMEM,
+        out_shape=pltpu.VMEM((width, lanes), jnp.bfloat16),
+        scratch_shapes=[pltpu.VMEM((width, lanes), jnp.float32)],
+        compiler_params=limit(16),
+        name="attend",
+    )(mine, queries, *states, gain)
+
+
+def place(x, cols, half, taps, shards, refs, w, sems):
+    rows = 3 * cols
+
+    def plan(own_top):
+        copies = {t: [] for t in taps}
+        count = 0
+        spans = []
+        for kind, block, *which in shards:
+            if kind == "whole":
+                spans.append((refs[which[0]], block, 0, rows, 0))
+            else:
+                for ref, top in ((refs[which[0]], own_top), (refs[which[1]], not own_top)):
+                    if top:
+                        spans.append((ref, block, 0, half, 0))
+                    else:
+                        spans.append((ref, block, half, rows, rows - half))
+        for t in taps:
+            for ref, block, lo, hi, shift in spans:
+                a, b = max(lo, t * cols), min(hi, (t + 1) * cols)
+                if a < b:
+                    at = pl.ds(pl.multiple_of(block * cols + a - t * cols, 8), b - a)
+                    copies[t].append(
+                        pltpu.make_async_copy(
+                            ref.at[pl.ds(a - shift, b - a), :], w.at[t, at, :], sems.at[count]
+                        )
+                    )
+                    count += 1
+        return copies
+
+    def each(do, only):
+        for flag in (True, False):
+
+            @pl.when((x == 0) == flag)
+            def _(flag=flag):
+                copies = plan(flag)
+                for t in only:
+                    for c in copies[t]:
+                        do(c)
+
+    each(lambda c: c.start(), taps)
+    return lambda t: each(lambda c: c.wait(), (t,))
+
+
+def dot(a, b):
+    return lax.dot_general(a, b, (((1,), (0,)), ((), ())), preferred_element_type=jnp.float32)
+
+
+def where_of(code):
+    return code // (4 * TB), code // 4 % TB, code // 2 % 2, code % 2
+
+
+def shards_of(late, z, y):
+    if not late:
+        here, beside = z % 2, 1 - z % 2
+        return [
+            ("halves", beside * 2 + y, 3, 4),
+            ("halves", beside * 2 + 1 - y, 5, 6),
+            ("whole", here * 2 + y, 0),
+            ("halves", here * 2 + 1 - y, 1, 2),
+        ]
+    first = jnp.where(z < TB // 2, 0, 1)
+    return [
+        ("halves", first * 2 + y, 0, 1),
+        ("halves", first * 2 + 1 - y, 2, 3),
+        ("halves", (1 - first) * 2 + y, 4, 5),
+        ("halves", (1 - first) * 2 + 1 - y, 6, 7),
+    ]
+
+
+def both_cores(own, other, at):
+    return jnp.concatenate([own[:, at], other[:, at]], axis=1)
+
+
+def rim_kernel(cols, half, late, code, n_own, n_other, *refs):
+    pieces = refs[:-4]
+    keep, give, w, sems = refs[-4:]
+    x, z, y, _ = where_of(code[0])
+    wait = place(x, cols, half, (2, 1, 0), shards_of(late, z, y), pieces, w, sems)
+    p = n_own.shape[1] // 2
+    first = both_cores(n_own, n_other, pl.ds(0, p))
+    last = both_cores(n_own, n_other, pl.ds(p, p))
+    wait(2)
+    w2 = w[2]
+    two = dot(w2, last).astype(keep.dtype)
+    keep[:, p:], give[:, p:] = two[:, :p], two[:, p:]
+    one = dot(w2, first)
+    wait(1)
+    one = (one + dot(w[1], last)).astype(keep.dtype)
+    keep[:, :p], give[:, :p] = one[:, :p], one[:, p:]
+    wait(0)
+
+
+def own_kernel(n_own, n_other, z_own, z_other, w, keep, give):
+    p = n_own.shape[1] // 2
+    zero = jnp.concatenate([z_own[...], z_other[...]], axis=1)
+    first = both_cores(n_own, n_other, pl.ds(0, p))
+    last = both_cores(n_own, n_other, pl.ds(p, p))
+    totals = (
+        dot(w[0], zero),
+        dot(w[0], first) + dot(w[1], zero),
+        dot(w[0], last) + dot(w[1], first) + dot(w[2], zero),
+    )
+    for f, total in enumerate(totals):
+        at = pl.ds(f * p, p)
+        keep[:, at], give[:, at] = total[:, :p], total[:, p:]
+
+
+def out_kernel(cols, code, *refs):
+    sums, rims, (out, rows) = refs[:4], refs[4:8], refs[8:]
+    p = out.shape[1]
+    _, z, _, core = where_of(code[0])
+    odd = z % 2 == 1
+    for f in range(3):
+        for late in range(2):
+            pair = z // 2 if late == 0 else 1 - z // 2
+            for who in range(2):
+                total = sums[2 * late + who][:, pl.ds(f * p, p)]
+                if f < 2:
+                    at = pl.ds(f * p, p)
+                    same, flipped = rims[2 * late + who], rims[2 * (1 - late) + who]
+                    rim = jnp.where(odd, same[:, at], flipped[:, at])
+                    total = total + rim.astype(jnp.float32)
+                c = core if who == 0 else 1 - core
+                blocks = total.shape[0] // cols
+                for i in range(blocks):
+                    to = ((pair * blocks + i) * 2 + c) * cols
+                    rows[pl.ds(pl.multiple_of(to, 8), cols), :] = total[i * cols : (i + 1) * cols]
+        for j in range(rows.shape[0] // LANES):
+            tile = rows[pl.ds(j * LANES, LANES), :]
+            out[f, :, pl.ds(j * LANES, LANES)] = tile.T.astype(out.dtype)
+
+
+def tuned(queries, keys, values, norm_gain, conv_weight):
+    _, frames, pixels, width = queries.shape
+    cols = conv_weight.shape[2]
+    axes = ("groups", "strip")
+    groups, devices = lax.axis_size("groups"), lax.axis_size("strip")
+    strips = devices // TB
+    x, s = lax.axis_index("groups"), lax.axis_index("strip")
+    z, inside = s // strips, s % strips
+    y, core = inside // 2, inside % 2
+
+    def send(block, where):
+        route = []
+        for g in range(groups):
+            for d in range(devices):
+                to = where(g, d)
+                if to is not None:
+                    route.append((g * devices + d, to[0] * devices + to[1]))
+        return lax.ppermute(block, axes, route)
+
+    def to_core(g, d):
+        return g, d ^ 1
+
+    def to_y(g, d):
+        return g, d ^ 2
+
+    def to_x(g, d):
+        return 1 - g, d
+
+    def up(r):
+        return lambda g, d: (g, d + r * strips) if d + r * strips < devices else None
+
+    def up_across(g, d):
+        return (g, (d + strips) ^ 1) if d + strips < devices else None
+
+    def along(**pairs):
+        table = {int(a[1:]): b for a, b in pairs.items()}
+        return lambda g, d: (
+            (g, table[d // strips] * strips + d % strips) if d // strips in table else None
+        )
+
+    mine = inside.astype(jnp.int32).reshape(1)
+    side = x.astype(jnp.int32).reshape(1)
+    code = (x * devices // strips * 4 + z * 4 + y * 2 + core).astype(jnp.int32).reshape(1)
+    k = keys[0].transpose(0, 2, 1)
+    v = values[0].transpose(0, 2, 1)
+    q = queries[0].transpose(0, 2, 1)
+    q = vm(q)
+    gain = vm(jnp.broadcast_to(norm_gain[:, None], (width, LANES)))
+
+    rows = 3 * cols
+    half = -(-rows // 16) * 8
+    whole = conv_weight.transpose(0, 2, 1).reshape(rows, width)
+    piece = half_of(side, whole, half)
+    zp1 = send(piece, along(z0=1, z1=0, z2=3, z3=2))
+    zp2 = send(piece, along(z1=2, z2=1))
+    zp3 = send(zp1, along(z1=2, z2=1))
+    zp4 = send(zp2, along(z1=0, z2=3))
+    zp5 = send(zp3, along(z1=0, z2=3))
+    outer = (z == 0) | (z == TB - 1)
+    slot_b = jnp.where(outer, zp4, zp2)
+    slot_c = jnp.where(outer, zp5, zp3)
+    y0 = send(piece, to_y)
+    ya = send(zp1, to_y)
+    yb = send(slot_b, to_y)
+    yc = send(slot_c, to_y)
+    rest = half_of(1 - side, whole, half)
+    early_pieces = [whole, y0, send(rest, to_y), zp1, send(zp1, to_x), ya, send(ya, to_x)]
+    late_pieces = [
+        slot_b,
+        send(slot_b, to_x),
+        yb,
+        send(yb, to_x),
+        slot_c,
+        send(slot_c, to_x),
+        yc,
+        send(yc, to_x),
+    ]
+
+    quarter = width // 4
+    kept, given = local_state(mine, k, v)
+    chip = add_up(kept, send(given, to_core))
+    plane = add_up(chip[:quarter], send(chip[quarter:], to_y))
+    share = add_up(plane, *[send(plane, up(r)) for r in (1, 2, 3)])
+    beside = send(share, to_y)
+    states = [share, send(share, to_core), beside, send(beside, to_core)]
+    states = [vm(s) for s in states]
+
+    late = attend((1, 2), mine, q, states, gain)
+    late_other = vm(send(late, to_core))
+    early = attend((0,), mine, q, states, gain)
+    early_other = vm(send(early, to_core))
+
+    part_rows = cols * devices // 4
+    sums, rims = [], []
+    for name, pieces in (("a", early_pieces), ("b", late_pieces)):
+        keep, give, taps = pl.pallas_call(
+            functools.partial(rim_kernel, cols, half, name == "b"),
+            in_specs=[SMEM] + [VMEM] * (2 + len(pieces)),
+            out_specs=[VMEM] * 3,
+            out_shape=[pltpu.VMEM((part_rows, 2 * pixels), jnp.bfloat16)] * 2
+            + [pltpu.VMEM((3, part_rows, width), jnp.bfloat16)],
+            scratch_shapes=[pltpu.SemaphoreType.DMA((24,))],
+            compiler_params=limit(16),
+            name="rim",
+        )(code, late, late_other, *[vm(piece) for piece in pieces])
+        rims += [send(keep, up(1)), send(give, up_across)]
+        keep, give = pl.pallas_call(
+            own_kernel,
+            in_specs=[VMEM] * 5,
+            out_specs=[VMEM] * 2,
+            out_shape=[pltpu.VMEM((part_rows, 3 * pixels), jnp.float32)] * 2,
+            compiler_params=limit(16),
+            name="own",
+        )(late, late_other, early, early_other, taps)
+        sums += [keep, send(give, to_core)]
+
+    result = pl.pallas_call(
+        functools.partial(out_kernel, cols),
+        in_specs=[SMEM] + [VMEM] * 8,
+        out_specs=VMEM,
+        out_shape=jax.ShapeDtypeStruct((frames, pixels, 4 * part_rows), jnp.bfloat16),
+        scratch_shapes=[pltpu.VMEM((4 * part_rows, pixels), jnp.float32)],
+        compiler_params=limit(16),
+        name="out",
+    )(code, *[vm(part) for part in sums + rims])
+    return result[None]
 
 
 def solution(mesh):
@@ -79,6 +463,24 @@
         P(),
         P(None, None, "strip"),
     )
+
+    groups, devices = mesh.shape["groups"], mesh.shape["strip"]
+    square = groups == 2 and devices == 4 * TB
+
+    def per_device(queries, keys, values, norm_gain, conv_weight):
+        _, frames, pixels, width = queries.shape
+        cols = conv_weight.shape[2]
+        fits = (
+            square
+            and frames == 3
+            and pixels == LANES
+            and width == H * DH
+            and cols % 8 == 0
+            and cols * devices % LANES == 0
+        )
+        form = tuned if fits else generic
+        return form(queries, keys, values, norm_gain, conv_weight)
+
     return jax.shard_map(
         per_device,
         mesh=mesh,

time: 375 us -> 175 us (0.47)
  waiting for transfers between devices: 208 us -> 92.1 us
  local copies, waits for them, and re-layouts: 99.5 us -> 9.49 us
  Pallas kernels: 0 us -> 32.2 us
  starting transfers between devices: 7.64 us -> 33.2 us
  matrix products: 21.4 us -> 0 us
  other arithmetic: 22.2 us -> 4.97 us
  between operations: 14.2 us -> 0.34 us
    unnamed x3 -> x0, waiting for transfers between devices: 109 us -> none
    reshape x11 -> x0, local copies, waits for them, and re-layouts: 52.2 us -> none  [the longest x2 15.3 us: per_device(): query_heads = jax.nn.relu(queries).reshape(count, H, DH)]
    all_to_all x1 -> x0, waiting for transfers between devices: 33.8 us -> none  [per_device(): lax.all_to_all(outgoing, 'strip', split_axis=0, concat_axis=1, tiled=True)]
    pallas_call x0 -> x10, Pallas kernels: none -> 32.2 us  [the longest x2 13 us: tuned(): pl.pallas_call(functools.partial(rim_kernel, cols, half, name == 'b'), in...]
    ppermute x1 -> x32, starting transfers between devices: 2.13 us -> 33.2 us  [send(): return lax.ppermute(block, axes, route)]
    ppermute x1 -> x32, waiting for transfers between devices: 65.8 us -> 92.1 us  [send(): return lax.ppermute(block, axes, route)]
    all_gather x1 -> x0, local copies, waits for them, and re-layouts: 22.1 us -> none  [per_device(): full_taps = lax.all_gather(conv_weight, 'strip', axis=2, tiled=True)]
    dot_general x4 -> x0, matrix products: 21.4 us -> none  [the longest x1 14.1 us: per_device(): jnp.dot(stacked, full_taps.reshape(3 * width, -1), preferred_element_type...]
  transfers between devices with their start and end apart: 4 -> 32, of which waited for: 3 -> 16; matrix products, arithmetic and copies ran while one was open for 18% -> 2% of each run, Pallas kernels for 0% -> 14%
where the time goes in v1:
time: 175 us; the launch traced here: 172 us
  waiting for transfers between devices  92.1 us (53%)
  starting transfers between devices  33.2 us (19%)
  Pallas kernels  32.2 us (18%)
  local copies, waits for them, and re-layouts  9.49 us (5%)
  other arithmetic  4.97 us (3%)
    ppermute x32, waiting for transfers between devices, send(): return lax.ppermute(block, axes, route)  92.1 us
    ppermute x32, starting transfers between devices, send(): return lax.ppermute(block, axes, route)  33.2 us
    pallas_call x2, Pallas kernels, tuned(): pl.pallas_call(functools.partial(rim_kernel, cols, half, name == 'b'), in...  13 us
    unnamed x38, local copies, waits for them, and re-layouts  9.13 us
    pallas_call x2, Pallas kernels, tuned(): pl.pallas_call(own_kernel, in_specs=[VMEM] * 5, out_specs=[VMEM] * 2, out...  6.89 us
    pallas_call x1, Pallas kernels, local_state(): pl.pallas_call(state_kernel, grid_spec=pltpu.PrefetchScalarGridSpec(num_s...  6.39 us
  transfers between devices with their start and end apart: 32, of which 16 were waited for; matrix products, arithmetic and copies ran while one was open for 2% of the time, Pallas kernels for 14%

profile of v1, /device:TPU:18, one launch (start us, length us, event | category | flops | bytes accessed | tf_op | source)
XLA Modules:
  0.0 172.3 jit_solution(1917512637326324390)
XLA Ops:
  0.0 6.4 %local_state.1 = (bf16[1120,128]{1,0:T(8,128)(2,1)}, bf16[1120,128]{1,0:T(8,128)(2,1)}) custom-call(s32[1]{0:T(128)} %bitcast.1.mine, bf16[3,2240,128]{2,1,0:T(8,128)(2,1)} %bitcast.21, bf16[3,2240,128]{2,1,0:T(8,128)(2,1)} %bitcast.22), custom_call_target="tpu_custom_call" | custom-call | tf_op jit(solution)/shard_map/local_state/pallas_call | solution.py:137
  12.0 2.4 %collective-permute-start.17 = (bf16[112,2240]{1,0:T(8,128)(2,1)}, bf16[112,2240]{1,0:T(8,128)(2,1)}, u32[]{:S(2)}, u32[]{:S(2)}) collective-permute-start(bf16[112,2240]{1,0:T(8,128)(2,1)} %half_of.2), channel_id=1, source_target_pairs={{4,8},{5,9},{6,10},{7,11},{8,4},{9,5},{10,6},{11,7},{20,24},{21,25... | collective-permute-start | bytes 1505288 | tf_op jit(solution)/shard_map/ppermute | solution.py:347
  17.1 4.1 %collective-permute-start.2 = (bf16[560,128]{1,0:T(8,128)(2,1)S(1)}, bf16[560,128]{1,0:T(8,128)(2,1)S(1)}, u32[]{:S(2)}, u32[]{:S(2)}) collective-permute-start(bf16[560,128]{1,0:T(8,128)(2,1)S(1)} %add_convert_fusion.2), channel_id=1, source_target_pairs={{0,4},{1,5},{2,6},{3,7},{4,8},{5,9},{6,10},{7,11},{8,12},{9,13},{1... | collective-permute-start | bytes 430088 | tf_op jit(solution)/shard_map/ppermute | solution.py:347
  21.2 8.8 %collective-permute-done.17 = bf16[112,2240]{1,0:T(8,128)(2,1)} collective-permute-done((bf16[112,2240]{1,0:T(8,128)(2,1)}, bf16[112,2240]{1,0:T(8,128)(2,1)}, u32[]{:S(2)}, u32[]{:S(2)}) %collective-permute-start.17) | collective-permute-done | bytes 501792 | tf_op jit(solution)/shard_map/ppermute | solution.py:347
  30.0 2.1 %collective-permute-start.18 = (bf16[112,2240]{1,0:T(8,128)(2,1)}, bf16[112,2240]{1,0:T(8,128)(2,1)}, u32[]{:S(2)}, u32[]{:S(2)}) collective-permute-start(bf16[112,2240]{1,0:T(8,128)(2,1)} %collective-permute-done.17), channel_id=1, source_target_pairs={{4,0},{5,1},{6,2},{7,3},{8,12},{9,13},{10,14},{11,15},{20,16},{21,... | collective-permute-start | bytes 1505288 | tf_op jit(solution)/shard_map/ppermute | solution.py:347
  34.1 2.4 %collective-permute-done.3 = bf16[560,128]{1,0:T(8,128)(2,1)S(1)} collective-permute-done((bf16[560,128]{1,0:T(8,128)(2,1)S(1)}, bf16[560,128]{1,0:T(8,128)(2,1)S(1)}, u32[]{:S(2)}, u32[]{:S(2)}) %collective-permute-start.3) | collective-permute-done | bytes 143392 | tf_op jit(solution)/shard_map/ppermute | solution.py:347
  36.4 4.5 %collective-permute-done.2 = bf16[560,128]{1,0:T(8,128)(2,1)S(1)} collective-permute-done((bf16[560,128]{1,0:T(8,128)(2,1)S(1)}, bf16[560,128]{1,0:T(8,128)(2,1)S(1)}, u32[]{:S(2)}, u32[]{:S(2)}) %collective-permute-start.2) | collective-permute-done | bytes 143392 | tf_op jit(solution)/shard_map/ppermute | solution.py:347
  41.7 4.6 %collective-permute-done.6.s2 = bf16[560,128]{1,0:T(8,128)(2,1)S(1)} collective-permute-done((bf16[560,128]{1,0:T(8,128)(2,1)S(1)}, bf16[560,128]{1,0:T(8,128)(2,1)S(1)}, u32[]{:S(2)}, u32[]{:S(2)}) %collective-permute-start.6) | collective-permute-done | bytes 143392 | tf_op jit(solution)/shard_map/ppermute | solution.py:347
  56.6 4.5 %collective-permute-done.10.refs_1_ = bf16[112,2240]{1,0:T(8,128)(2,1)S(1)} collective-permute-done((bf16[112,2240]{1,0:T(8,128)(2,1)}, bf16[112,2240]{1,0:T(8,128)(2,1)S(1)}, u32[]{:S(2)}, u32[]{:S(2)}) %collective-permute-start.10) | collective-permute-done | bytes 501792 | tf_op jit(solution)/shard_map/ppermute | solution.py:347
  61.9 20.9 %collective-permute-done.14.refs_5_ = bf16[112,2240]{1,0:T(8,128)(2,1)S(1)} collective-permute-done((bf16[112,2240]{1,0:T(8,128)(2,1)}, bf16[112,2240]{1,0:T(8,128)(2,1)S(1)}, u32[]{:S(2)}, u32[]{:S(2)}) %collective-permute-start.14) | collective-permute-done | bytes 501792 | tf_op jit(solution)/shard_map/ppermute | solution.py:347
  89.4 6.9 %collective-permute-done.15.refs_6_ = bf16[112,2240]{1,0:T(8,128)(2,1)S(1)} collective-permute-done((bf16[112,2240]{1,0:T(8,128)(2,1)S(1)}, bf16[112,2240]{1,0:T(8,128)(2,1)S(1)}, u32[]{:S(2)}, u32[]{:S(2)}) %collective-permute-start.15) | collective-permute-done | bytes 501792 | tf_op jit(solution)/shard_map/ppermute | solution.py:347
  99.7 7.7 %collective-permute-done.25.refs_6_ = bf16[112,2240]{1,0:T(8,128)(2,1)} collective-permute-done((bf16[112,2240]{1,0:T(8,128)(2,1)}, bf16[112,2240]{1,0:T(8,128)(2,1)}, u32[]{:S(2)}, u32[]{:S(2)}) %collective-permute-start.25) | collective-permute-done | bytes 501792 | tf_op jit(solution)/shard_map/ppermute | solution.py:347
  113.2 5.7 %rim.2 = (bf16[288,256]{1,0:T(8,128)(2,1)S(1)}, bf16[288,256]{1,0:T(8,128)(2,1)S(1)}, bf16[3,288,2240]{2,1,0:T(8,128)(2,1)S(1)}) custom-call(s32[1]{0:T(128)} %bitcast.code, bf16[2240,256]{1,0:T(8,128)(2,1)S(1)} %attend.2.n_own, bf16[2240,256]{1,0:T(8,128)(2,1)S(1)} %collective-permute-done.8.n_other, bf16[216,2240]{1,0:T(8,128)(2,1)S(1)} %bitcast.18, ...), custom_call_target="tpu_custom_call" | custom-call | tf_op jit(solution)/shard_map/rim/pallas_call | solution.py:425
  118.9 3.4 %own.2 = (f32[288,384]{1,0:T(8,128)S(1)}, f32[288,384]{1,0:T(8,128)S(1)}) custom-call(bf16[2240,256]{1,0:T(8,128)(2,1)S(1)} %attend.2.n_own, bf16[2240,256]{1,0:T(8,128)(2,1)S(1)} %collective-permute-done.8.n_other, bf16[2240,128]{1,0:T(8,128)(2,1)} %attend.3.z_own, bf16[2240,128]{1,0:T(8,128)(2,1)} %collective-permute-done.9.z_other, ...), custom_call_target="tpu_custom_call" | custom-call | tf_op jit(solution)/shard_map/own/pallas_call | solution.py:436
  122.4 11.8 %collective-permute-done.21.refs_3_ = bf16[112,2240]{1,0:T(8,128)(2,1)} collective-permute-done((bf16[112,2240]{1,0:T(8,128)(2,1)}, bf16[112,2240]{1,0:T(8,128)(2,1)}, u32[]{:S(2)}, u32[]{:S(2)}) %collective-permute-start.21) | collective-permute-done | bytes 501792 | tf_op jit(solution)/shard_map/ppermute | solution.py:347
  134.2 8.7 %collective-permute-done.26.refs_7_ = bf16[112,2240]{1,0:T(8,128)(2,1)} collective-permute-done((bf16[112,2240]{1,0:T(8,128)(2,1)}, bf16[112,2240]{1,0:T(8,128)(2,1)}, u32[]{:S(2)}, u32[]{:S(2)}) %collective-permute-start.26) | collective-permute-done | bytes 501792 | tf_op jit(solution)/shard_map/ppermute | solution.py:347
  142.9 7.3 %rim.3 = (bf16[288,256]{1,0:T(8,128)(2,1)S(1)}, bf16[288,256]{1,0:T(8,128)(2,1)S(1)}, bf16[3,288,2240]{2,1,0:T(8,128)(2,1)S(1)}) custom-call(s32[1]{0:T(128)} %bitcast.code, bf16[2240,256]{1,0:T(8,128)(2,1)S(1)} %attend.2.n_own, bf16[2240,256]{1,0:T(8,128)(2,1)S(1)} %collective-permute-done.8.n_other, bf16[112,2240]{1,0:T(8,128)(2,1)} %broadcast_select_fusion.1.refs_0_, ...), custom_call_target="tpu_custom_call" | custom-call | tf_op jit(solution)/shard_map/rim/pallas_call | solution.py:425
  150.2 3.4 %own.3 = (f32[288,384]{1,0:T(8,128)S(1)}, f32[288,384]{1,0:T(8,128)S(1)}) custom-call(bf16[2240,256]{1,0:T(8,128)(2,1)S(1)} %attend.2.n_own, bf16[2240,256]{1,0:T(8,128)(2,1)S(1)} %collective-permute-done.8.n_other, bf16[2240,128]{1,0:T(8,128)(2,1)} %attend.3.z_own, bf16[2240,128]{1,0:T(8,128)(2,1)} %collective-permute-done.9.z_other, ...), custom_call_target="tpu_custom_call" | custom-call | tf_op jit(solution)/shard_map/own/pallas_call | solution.py:436
  153.7 1.9 %collective-permute-start.28 = (bf16[288,256]{1,0:T(8,128)(2,1)S(1)}, bf16[288,256]{1,0:T(8,128)(2,1)S(1)}, u32[]{:S(2)}, u32[]{:S(2)}) collective-permute-start(bf16[288,256]{1,0:T(8,128)(2,1)S(1)} %get-tuple-element.25), channel_id=1, source_target_pairs={{0,4},{1,5},{2,6},{3,7},{4,8},{5,9},{6,10},{7,11},{8,12},{9,13},{1... | collective-permute-start | bytes 442376 | tf_op jit(solution)/shard_map/ppermute | solution.py:347
  155.6 1.9 %collective-permute-start.29 = (bf16[288,256]{1,0:T(8,128)(2,1)S(1)}, bf16[288,256]{1,0:T(8,128)(2,1)S(1)}, u32[]{:S(2)}, u32[]{:S(2)}) collective-permute-start(bf16[288,256]{1,0:T(8,128)(2,1)S(1)} %get-tuple-element.26), channel_id=1, source_target_pairs={{0,5},{1,4},{2,7},{3,6},{4,9},{5,8},{6,11},{7,10},{8,13},{9,12},{1... | collective-permute-start | bytes 442376 | tf_op jit(solution)/shard_map/ppermute | solution.py:347
  157.6 1.9 %collective-permute-start.30 = (bf16[288,256]{1,0:T(8,128)(2,1)S(1)}, bf16[288,256]{1,0:T(8,128)(2,1)S(1)}, u32[]{:S(2)}, u32[]{:S(2)}) collective-permute-start(bf16[288,256]{1,0:T(8,128)(2,1)S(1)} %get-tuple-element.27), channel_id=1, source_target_pairs={{0,4},{1,5},{2,6},{3,7},{4,8},{5,9},{6,10},{7,11},{8,12},{9,13},{1... | collective-permute-start | bytes 442376 | tf_op jit(solution)/shard_map/ppermute | solution.py:347
  159.5 2.8 %collective-permute-done.28.refs_4_ = bf16[288,256]{1,0:T(8,128)(2,1)S(1)} collective-permute-done((bf16[288,256]{1,0:T(8,128)(2,1)S(1)}, bf16[288,256]{1,0:T(8,128)(2,1)S(1)}, u32[]{:S(2)}, u32[]{:S(2)}) %collective-permute-start.28) | collective-permute-done | bytes 147488 | tf_op jit(solution)/shard_map/ppermute | solution.py:347
  164.5 4.1 %collective-permute-done.30.refs_6_ = bf16[288,256]{1,0:T(8,128)(2,1)S(1)} collective-permute-done((bf16[288,256]{1,0:T(8,128)(2,1)S(1)}, bf16[288,256]{1,0:T(8,128)(2,1)S(1)}, u32[]{:S(2)}, u32[]{:S(2)}) %collective-permute-start.30) | collective-permute-done | bytes 147488 | tf_op jit(solution)/shard_map/ppermute | solution.py:347
  168.7 2.2 %collective-permute-done.31.refs_7_ = bf16[288,256]{1,0:T(8,128)(2,1)S(1)} collective-permute-done((bf16[288,256]{1,0:T(8,128)(2,1)S(1)}, bf16[288,256]{1,0:T(8,128)(2,1)S(1)}, u32[]{:S(2)}, u32[]{:S(2)}) %collective-permute-start.31) | collective-permute-done | bytes 147488 | tf_op jit(solution)/shard_map/ppermute | solution.py:347
  (95 shorter events, 41.6 us)
Async XLA Ops:
  12.0 18.1 %collective-permute-start.17 = (bf16[112,2240]{1,0:T(8,128)(2,1)}, bf16[112,2240]{1,0:T(8,128)(2,1)}, u32[]{:S(2)}, u32[]{:S(2)}) collective-permute-start(bf16[112,2240]{1,0:T(8,128)(2,1)} %half_of.2), channel_id=1, source_target_pairs={{4,8},{5,9},{6,10},{7,11},{8,4},{9,5},{10,6},{11,7},{20,24},{21,25... | collective-permute-start | bytes 1505288 | tf_op jit(solution)/shard_map/ppermute | solution.py:347
  14.3 17.8 %collective-permute-start.12 = (bf16[112,2240]{1,0:T(8,128)(2,1)}, bf16[112,2240]{1,0:T(8,128)(2,1)}, u32[]{:S(2)}, u32[]{:S(2)}) collective-permute-start(bf16[112,2240]{1,0:T(8,128)(2,1)} %half_of.2), channel_id=1, source_target_pairs={{0,4},{1,5},{2,6},{3,7},{4,0},{5,1},{6,2},{7,3},{8,12},{9,13},{10,... | collective-permute-start | bytes 1505288 | tf_op jit(solution)/shard_map/ppermute | solution.py:347
  15.2 18.9 %collective-permute-start.4 = (bf16[560,128]{1,0:T(8,128)(2,1)S(1)}, bf16[560,128]{1,0:T(8,128)(2,1)S(1)}, u32[]{:S(2)}, u32[]{:S(2)}) collective-permute-start(bf16[560,128]{1,0:T(8,128)(2,1)S(1)} %add_convert_fusion.2), channel_id=1, source_target_pairs={{0,12},{1,13},{2,14},{3,15},{16,28},{17,29},{18,30},{19,31}} | collective-permute-start | bytes 430088 | tf_op jit(solution)/shard_map/ppermute | solution.py:347
  15.8 20.6 %collective-permute-start.3 = (bf16[560,128]{1,0:T(8,128)(2,1)S(1)}, bf16[560,128]{1,0:T(8,128)(2,1)S(1)}, u32[]{:S(2)}, u32[]{:S(2)}) collective-permute-start(bf16[560,128]{1,0:T(8,128)(2,1)S(1)} %add_convert_fusion.2), channel_id=1, source_target_pairs={{0,8},{1,9},{2,10},{3,11},{4,12},{5,13},{6,14},{7,15},{16,24},{17,... | collective-permute-start | bytes 430088 | tf_op jit(solution)/shard_map/ppermute | solution.py:347
  17.1 23.9 %collective-permute-start.2 = (bf16[560,128]{1,0:T(8,128)(2,1)S(1)}, bf16[560,128]{1,0:T(8,128)(2,1)S(1)}, u32[]{:S(2)}, u32[]{:S(2)}) collective-permute-start(bf16[560,128]{1,0:T(8,128)(2,1)S(1)} %add_convert_fusion.2), channel_id=1, source_target_pairs={{0,4},{1,5},{2,6},{3,7},{4,8},{5,9},{6,10},{7,11},{8,12},{9,13},{1... | collective-permute-start | bytes 430088 | tf_op jit(solution)/shard_map/ppermute | solution.py:347
  30.0 22.7 %collective-permute-start.18 = (bf16[112,2240]{1,0:T(8,128)(2,1)}, bf16[112,2240]{1,0:T(8,128)(2,1)}, u32[]{:S(2)}, u32[]{:S(2)}) collective-permute-start(bf16[112,2240]{1,0:T(8,128)(2,1)} %collective-permute-done.17), channel_id=1, source_target_pairs={{4,0},{5,1},{6,2},{7,3},{8,12},{9,13},{10,14},{11,15},{20,16},{21,... | collective-permute-start | bytes 1505288 | tf_op jit(solution)/shard_map/ppermute | solution.py:347
  32.1 21.2 %collective-permute-start.22 = (bf16[112,2240]{1,0:T(8,128)(2,1)}, bf16[112,2240]{1,0:T(8,128)(2,1)}, u32[]{:S(2)}, u32[]{:S(2)}) collective-permute-start(bf16[112,2240]{1,0:T(8,128)(2,1)} %collective-permute-done.12.refs_3_), channel_id=1, source_target_pairs={{4,8},{5,9},{6,10},{7,11},{8,4},{9,5},{10,6},{11,7},{20,24},{21,25... | collective-permute-start | bytes 1505288 | tf_op jit(solution)/shard_map/ppermute | solution.py:347
  46.2 14.8 %collective-permute-start.10 = (bf16[112,2240]{1,0:T(8,128)(2,1)}, bf16[112,2240]{1,0:T(8,128)(2,1)S(1)}, u32[]{:S(2)}, u32[]{:S(2)}) collective-permute-start(bf16[112,2240]{1,0:T(8,128)(2,1)} %half_of.2), channel_id=1, source_target_pairs={{0,2},{1,3},{2,0},{3,1},{4,6},{5,7},{6,4},{7,5},{8,10},{9,11},{10,... | collective-permute-start | bytes 1505288 | tf_op jit(solution)/shard_map/ppermute | solution.py:347
  47.9 37.8 %collective-permute-start.11 = (bf16[112,2240]{1,0:T(8,128)(2,1)}, bf16[112,2240]{1,0:T(8,128)(2,1)S(1)}, u32[]{:S(2)}, u32[]{:S(2)}) collective-permute-start(bf16[112,2240]{1,0:T(8,128)(2,1)} %half_of.3), channel_id=1, source_target_pairs={{0,2},{1,3},{2,0},{3,1},{4,6},{5,7},{6,4},{7,5},{8,10},{9,11},{10,... | collective-permute-start | bytes 1505288 | tf_op jit(solution)/shard_map/ppermute | solution.py:347
  49.5 39.1 %collective-permute-start.13 = (bf16[112,2240]{1,0:T(8,128)(2,1)}, bf16[112,2240]{1,0:T(8,128)(2,1)S(1)}, u32[]{:S(2)}, u32[]{:S(2)}) collective-permute-start(bf16[112,2240]{1,0:T(8,128)(2,1)} %collective-permute-done.12.refs_3_), channel_id=1, source_target_pairs={{0,16},{1,17},{2,18},{3,19},{4,20},{5,21},{6,22},{7,23},{8,24},{9,... | collective-permute-start | bytes 1505288 | tf_op jit(solution)/shard_map/ppermute | solution.py:347
  52.8 29.9 %collective-permute-start.14 = (bf16[112,2240]{1,0:T(8,128)(2,1)}, bf16[112,2240]{1,0:T(8,128)(2,1)S(1)}, u32[]{:S(2)}, u32[]{:S(2)}) collective-permute-start(bf16[112,2240]{1,0:T(8,128)(2,1)} %collective-permute-done.12.refs_3_), channel_id=1, source_target_pairs={{0,2},{1,3},{2,0},{3,1},{4,6},{5,7},{6,4},{7,5},{8,10},{9,11},{10,... | collective-permute-start | bytes 1505288 | tf_op jit(solution)/shard_map/ppermute | solution.py:347
  53.4 29.9 %collective-permute-start.23 = (bf16[112,2240]{1,0:T(8,128)(2,1)}, bf16[112,2240]{1,0:T(8,128)(2,1)S(1)}, u32[]{:S(2)}, u32[]{:S(2)}) collective-permute-start(bf16[112,2240]{1,0:T(8,128)(2,1)} %collective-permute-done.22), channel_id=1, source_target_pairs={{4,0},{5,1},{6,2},{7,3},{8,12},{9,13},{10,14},{11,15},{20,16},{21,... | collective-permute-start | bytes 1505288 | tf_op jit(solution)/shard_map/ppermute | solution.py:347
  61.9 37.3 %collective-permute-start.8 = (bf16[2240,256]{1,0:T(8,128)(2,1)S(1)}, bf16[2240,256]{1,0:T(8,128)(2,1)S(1)}, u32[]{:S(2)}, u32[]{:S(2)}) collective-permute-start(bf16[2240,256]{1,0:T(8,128)(2,1)S(1)} %attend.2.n_own), channel_id=1, source_target_pairs={{0,1},{1,0},{2,3},{3,2},{4,5},{5,4},{6,7},{7,6},{8,9},{9,8},{10,11... | collective-permute-start | bytes 3440648 | tf_op jit(solution)/shard_map/ppermute | solution.py:347
  82.7 14.9 %collective-permute-start.20 = (bf16[112,2240]{1,0:T(8,128)(2,1)}, bf16[112,2240]{1,0:T(8,128)(2,1)}, u32[]{:S(2)}, u32[]{:S(2)}) collective-permute-start(bf16[112,2240]{1,0:T(8,128)(2,1)} %broadcast_select_fusion.1.refs_0_), channel_id=1, source_target_pairs={{0,2},{1,3},{2,0},{3,1},{4,6},{5,7},{6,4},{7,5},{8,10},{9,11},{10,... | collective-permute-start | bytes 1505288 | tf_op jit(solution)/shard_map/ppermute | solution.py:347
  83.3 13.0 %collective-permute-start.15 = (bf16[112,2240]{1,0:T(8,128)(2,1)S(1)}, bf16[112,2240]{1,0:T(8,128)(2,1)S(1)}, u32[]{:S(2)}, u32[]{:S(2)}) collective-permute-start(bf16[112,2240]{1,0:T(8,128)(2,1)S(1)} %collective-permute-done.14.refs_5_), channel_id=1, source_target_pairs={{0,16},{1,17},{2,18},{3,19},{4,20},{5,21},{6,22},{7,23},{8,24},{9,... | collective-permute-start | bytes 1505288 | tf_op jit(solution)/shard_map/ppermute | solution.py:347
  85.7 21.7 %collective-permute-start.25 = (bf16[112,2240]{1,0:T(8,128)(2,1)}, bf16[112,2240]{1,0:T(8,128)(2,1)}, u32[]{:S(2)}, u32[]{:S(2)}) collective-permute-start(bf16[112,2240]{1,0:T(8,128)(2,1)} %broadcast_select_fusion.refs_4_), channel_id=1, source_target_pairs={{0,2},{1,3},{2,0},{3,1},{4,6},{5,7},{6,4},{7,5},{8,10},{9,11},{10,... | collective-permute-start | bytes 1505288 | tf_op jit(solution)/shard_map/ppermute | solution.py:347
  89.4 29.4 %collective-permute-start.9 = (bf16[2240,128]{1,0:T(8,128)(2,1)}, bf16[2240,128]{1,0:T(8,128)(2,1)}, u32[]{:S(2)}, u32[]{:S(2)}) collective-permute-start(bf16[2240,128]{1,0:T(8,128)(2,1)} %attend.3.z_own), channel_id=1, source_target_pairs={{0,1},{1,0},{2,3},{3,2},{4,5},{5,4},{6,7},{7,6},{8,9},{9,8},{10,11... | collective-permute-start | bytes 1720328 | tf_op jit(solution)/shard_map/ppermute | solution.py:347
  97.1 25.3 %collective-permute-start.19 = (bf16[112,2240]{1,0:T(8,128)(2,1)}, bf16[112,2240]{1,0:T(8,128)(2,1)}, u32[]{:S(2)}, u32[]{:S(2)}) collective-permute-start(bf16[112,2240]{1,0:T(8,128)(2,1)} %broadcast_select_fusion.1.refs_0_), channel_id=1, source_target_pairs={{0,16},{1,17},{2,18},{3,19},{4,20},{5,21},{6,22},{7,23},{8,24},{9,... | collective-permute-start | bytes 1505288 | tf_op jit(solution)/shard_map/ppermute | solution.py:347
  97.7 36.5 %collective-permute-start.24 = (bf16[112,2240]{1,0:T(8,128)(2,1)}, bf16[112,2240]{1,0:T(8,128)(2,1)}, u32[]{:S(2)}, u32[]{:S(2)}) collective-permute-start(bf16[112,2240]{1,0:T(8,128)(2,1)} %broadcast_select_fusion.refs_4_), channel_id=1, source_target_pairs={{0,16},{1,17},{2,18},{3,19},{4,20},{5,21},{6,22},{7,23},{8,24},{9,... | collective-permute-start | bytes 1505288 | tf_op jit(solution)/shard_map/ppermute | solution.py:347
  99.2 35.0 %collective-permute-start.21 = (bf16[112,2240]{1,0:T(8,128)(2,1)}, bf16[112,2240]{1,0:T(8,128)(2,1)}, u32[]{:S(2)}, u32[]{:S(2)}) collective-permute-start(bf16[112,2240]{1,0:T(8,128)(2,1)} %collective-permute-done.20.refs_2_), channel_id=1, source_target_pairs={{0,16},{1,17},{2,18},{3,19},{4,20},{5,21},{6,22},{7,23},{8,24},{9,... | collective-permute-start | bytes 1505288 | tf_op jit(solution)/shard_map/ppermute | solution.py:347
  107.4 35.5 %collective-permute-start.26 = (bf16[112,2240]{1,0:T(8,128)(2,1)}, bf16[112,2240]{1,0:T(8,128)(2,1)}, u32[]{:S(2)}, u32[]{:S(2)}) collective-permute-start(bf16[112,2240]{1,0:T(8,128)(2,1)} %collective-permute-done.25.refs_6_), channel_id=1, source_target_pairs={{0,16},{1,17},{2,18},{3,19},{4,20},{5,21},{6,22},{7,23},{8,24},{9,... | collective-permute-start | bytes 1505288 | tf_op jit(solution)/shard_map/ppermute | solution.py:347
  122.3 42.2 %collective-permute-start.16 = (f32[288,384]{1,0:T(8,128)S(1)}, f32[288,384]{1,0:T(8,128)S(1)}, u32[]{:S(2)}, u32[]{:S(2)}) collective-permute-start(f32[288,384]{1,0:T(8,128)S(1)} %get-tuple-element.21), channel_id=1, source_target_pairs={{0,1},{1,0},{2,3},{3,2},{4,5},{5,4},{6,7},{7,6},{8,9},{9,8},{10,11... | collective-permute-start | bytes 1327112 | tf_op jit(solution)/shard_map/ppermute | solution.py:347
  153.6 17.2 %collective-permute-start.27 = (f32[288,384]{1,0:T(8,128)S(1)}, f32[288,384]{1,0:T(8,128)S(1)}, u32[]{:S(2)}, u32[]{:S(2)}) collective-permute-start(f32[288,384]{1,0:T(8,128)S(1)} %get-tuple-element.24), channel_id=1, source_target_pairs={{0,1},{1,0},{2,3},{3,2},{4,5},{5,4},{6,7},{7,6},{8,9},{9,8},{10,11... | collective-permute-start | bytes 1327112 | tf_op jit(solution)/shard_map/ppermute | solution.py:347
  157.6 11.1 %collective-permute-start.30 = (bf16[288,256]{1,0:T(8,128)(2,1)S(1)}, bf16[288,256]{1,0:T(8,128)(2,1)S(1)}, u32[]{:S(2)}, u32[]{:S(2)}) collective-permute-start(bf16[288,256]{1,0:T(8,128)(2,1)S(1)} %get-tuple-element.27), channel_id=1, source_target_pairs={{0,4},{1,5},{2,6},{3,7},{4,8},{5,9},{6,10},{7,11},{8,12},{9,13},{1... | collective-permute-start | bytes 442376 | tf_op jit(solution)/shard_map/ppermute | solution.py:347
  (27 other events, 234.2 us)

commit v2 on v1

--- a/solution.py
+++ b/solution.py
@@ -82,15 +82,28 @@
     return pltpu.with_memory_space_constraint(value, pltpu.VMEM)
 
 
+def hbm(value):
+    return pltpu.with_memory_space_constraint(value, pltpu.HBM)
+
+
 def limit(mib):
     return pltpu.CompilerParams(vmem_limit_bytes=mib * 2**20)
 
 
-def slice_kernel(step, x_ref, from_ref, to_ref, sem):
-    at = pl.ds(pl.multiple_of(x_ref[0] * step, 8), to_ref.shape[0])
-    copy = pltpu.make_async_copy(from_ref.at[at, :], to_ref, sem)
-    copy.start()
-    copy.wait()
+def slice_kernel(step, x_ref, from_ref, to_ref, sems):
+    count = to_ref.shape[0] // sems.shape[0]
+    copies = []
+    for i in range(sems.shape[0]):
+        at = pl.ds(pl.multiple_of(x_ref[0] * step + i * count, 8), count)
+        copies.append(
+            pltpu.make_async_copy(
+                from_ref.at[at, :], to_ref.at[pl.ds(i * count, count), :], sems.at[i]
+            )
+        )
+    for copy in copies:
+        copy.start()
+    for copy in copies:
+        copy.wait()
 
 
 def half_of(x, whole, half):
@@ -100,10 +113,10 @@
         in_specs=[SMEM, ANY],
         out_specs=VMEM,
         out_shape=pltpu.VMEM((half, width), whole.dtype),
-        scratch_shapes=[pltpu.SemaphoreType.DMA],
+        scratch_shapes=[pltpu.SemaphoreType.DMA((half // 8,))],
         compiler_params=limit(4),
         name="half_of",
-    )(x, whole)
+    )(x, hbm(whole))
 
 
 def state_kernel(mine, k_ref, v_ref, *outs):
@@ -195,47 +208,35 @@
     )(mine, queries, *states, gain)
 
 
-def place(x, cols, half, taps, shards, refs, w, sems):
+def place(x, outer, cols, half, tap, shards, refs, w):
     rows = 3 * cols
-
-    def plan(own_top):
-        copies = {t: [] for t in taps}
-        count = 0
-        spans = []
-        for kind, block, *which in shards:
-            if kind == "whole":
-                spans.append((refs[which[0]], block, 0, rows, 0))
+    lo_tap, hi_tap = tap * cols, (tap + 1) * cols
+
+    def put(ref, block, lo, hi, shift):
+        a, b = max(lo, lo_tap), min(hi, hi_tap)
+        if a < b:
+            at = pl.ds(pl.multiple_of(block * cols + a - lo_tap, 8), b - a)
+            part = pl.ds(a - shift, b - a)
+            if isinstance(ref, tuple):
+                w[at, :] = jnp.where(outer, ref[0][part, :], ref[1][part, :])
             else:
-                for ref, top in ((refs[which[0]], own_top), (refs[which[1]], not own_top)):
-                    if top:
-                        spans.append((ref, block, 0, half, 0))
-                    else:
-                        spans.append((ref, block, half, rows, rows - half))
-        for t in taps:
-            for ref, block, lo, hi, shift in spans:
-                a, b = max(lo, t * cols), min(hi, (t + 1) * cols)
-                if a < b:
-                    at = pl.ds(pl.multiple_of(block * cols + a - t * cols, 8), b - a)
-                    copies[t].append(
-                        pltpu.make_async_copy(
-                            ref.at[pl.ds(a - shift, b - a), :], w.at[t, at, :], sems.at[count]
-                        )
-                    )
-                    count += 1
-        return copies
-
-    def each(do, only):
-        for flag in (True, False):
-
-            @pl.when((x == 0) == flag)
-            def _(flag=flag):
-                copies = plan(flag)
-                for t in only:
-                    for c in copies[t]:
-                        do(c)
-
-    each(lambda c: c.start(), taps)
-    return lambda t: each(lambda c: c.wait(), (t,))
+                w[at, :] = ref[part, :]
+
+    for kind, block, *which in shards:
+        if kind == "whole":
+            put(refs[which[0]], block, 0, rows, 0)
+
+    for flag in (True, False):
+
+        @pl.when((x == 0) == flag)
+        def _(flag=flag):
+            for kind, block, *which in shards:
+                if kind == "halves":
+                    for ref, top in ((refs[which[0]], flag), (refs[which[1]], not flag)):
+                        if top:
+                            put(ref, block, 0, half, 0)
+                        else:
+                            put(ref, block, half, rows, rows - half)
 
 
 def dot(a, b):
@@ -246,8 +247,12 @@
     return code // (4 * TB), code // 4 % TB, code // 2 % 2, code % 2
 
 
-def shards_of(late, z, y):
-    if not late:
+def first_late(z):
+    return jnp.where(z < TB // 2, 0, 1)
+
+
+def shards_of(part, z, y):
+    if part == 0:
         here, beside = z % 2, 1 - z % 2
         return [
             ("halves", beside * 2 + y, 3, 4),
@@ -255,73 +260,81 @@
             ("whole", here * 2 + y, 0),
             ("halves", here * 2 + 1 - y, 1, 2),
         ]
-    first = jnp.where(z < TB // 2, 0, 1)
-    return [
-        ("halves", first * 2 + y, 0, 1),
-        ("halves", first * 2 + 1 - y, 2, 3),
-        ("halves", (1 - first) * 2 + y, 4, 5),
-        ("halves", (1 - first) * 2 + 1 - y, 6, 7),
-    ]
+    return [("halves", y, 0, 1), ("halves", 1 - y, 2, 3)]
 
 
 def both_cores(own, other, at):
     return jnp.concatenate([own[:, at], other[:, at]], axis=1)
 
 
-def rim_kernel(cols, half, late, code, n_own, n_other, *refs):
-    pieces = refs[:-4]
-    keep, give, w, sems = refs[-4:]
+def rim_kernel(cols, half, part, code, n_own, n_other, *refs):
+    pieces, (out, w) = list(refs[:-2]), refs[-2:]
     x, z, y, _ = where_of(code[0])
-    wait = place(x, cols, half, (2, 1, 0), shards_of(late, z, y), pieces, w, sems)
+    outer = (z == 0) | (z == TB - 1)
+    if part == 1:
+        pieces[1:3] = [(pieces[1], pieces[2])]
+    for tap in (2, 1, 0):
+        place(x, outer, cols, half, tap, shards_of(part, z, y), pieces, w.at[tap])
     p = n_own.shape[1] // 2
     first = both_cores(n_own, n_other, pl.ds(0, p))
     last = both_cores(n_own, n_other, pl.ds(p, p))
-    wait(2)
-    w2 = w[2]
-    two = dot(w2, last).astype(keep.dtype)
-    keep[:, p:], give[:, p:] = two[:, :p], two[:, p:]
-    one = dot(w2, first)
-    wait(1)
-    one = (one + dot(w[1], last)).astype(keep.dtype)
-    keep[:, :p], give[:, :p] = one[:, :p], one[:, p:]
-    wait(0)
-
-
-def own_kernel(n_own, n_other, z_own, z_other, w, keep, give):
+    out[:, 2 * p :] = dot(w[2], last).astype(out.dtype)
+    out[:, : 2 * p] = (dot(w[2], first) + dot(w[1], last)).astype(out.dtype)
+
+
+def own_kernel(late, code, n_own, n_other, z_own, z_other, *refs):
+    taps, (keep, give) = refs[:-2], refs[-2:]
+    _, z, _, _ = where_of(code[0])
     p = n_own.shape[1] // 2
     zero = jnp.concatenate([z_own[...], z_other[...]], axis=1)
     first = both_cores(n_own, n_other, pl.ds(0, p))
     last = both_cores(n_own, n_other, pl.ds(p, p))
-    totals = (
-        dot(w[0], zero),
-        dot(w[0], first) + dot(w[1], zero),
-        dot(w[0], last) + dot(w[1], first) + dot(w[2], zero),
-    )
-    for f, total in enumerate(totals):
-        at = pl.ds(f * p, p)
-        keep[:, at], give[:, at] = total[:, :p], total[:, p:]
+    for i, w in enumerate(taps):
+        count = w.shape[1]
+        to = i * count
+        if late:
+            nearer = first_late(z)
+            to = (nearer if i == 0 else 1 - nearer) * count
+        rows = pl.ds(pl.multiple_of(to, 8), count)
+        totals = (
+            dot(w[0], zero),
+            dot(w[0], first) + dot(w[1], zero),
+            dot(w[0], last) + dot(w[1], first) + dot(w[2], zero),
+        )
+        for f, total in enumerate(totals):
+            at = pl.ds(f * p, p)
+            keep[rows, at], give[rows, at] = total[:, :p], total[:, p:]
 
 
 def out_kernel(cols, code, *refs):
-    sums, rims, (out, rows) = refs[:4], refs[4:8], refs[8:]
+    sums, rims, (out, rows) = refs[:4], refs[4:10], refs[10:]
     p = out.shape[1]
     _, z, _, core = where_of(code[0])
-    odd = z % 2 == 1
+    behind = z - 1
+    behind_pair = behind // 2
+    nearer = first_late(behind)
+    count = 2 * cols
     for f in range(3):
         for late in range(2):
             pair = z // 2 if late == 0 else 1 - z // 2
-            for who in range(2):
-                total = sums[2 * late + who][:, pl.ds(f * p, p)]
-                if f < 2:
-                    at = pl.ds(f * p, p)
-                    same, flipped = rims[2 * late + who], rims[2 * (1 - late) + who]
-                    rim = jnp.where(odd, same[:, at], flipped[:, at])
-                    total = total + rim.astype(jnp.float32)
-                c = core if who == 0 else 1 - core
-                blocks = total.shape[0] // cols
-                for i in range(blocks):
-                    to = ((pair * blocks + i) * 2 + c) * cols
-                    rows[pl.ds(pl.multiple_of(to, 8), cols), :] = total[i * cols : (i + 1) * cols]
+            for j in range(2):
+                for who in range(2):
+                    total = sums[2 * late + who][pl.ds(j * count, count), pl.ds(f * p, p)]
+                    if f < 2:
+                        at = pl.ds((2 * f + who) * p, p)
+                        near, mid, far = rims[who], rims[2 + who], rims[4 + who]
+                        rim = jnp.where(
+                            pair == behind_pair,
+                            near[pl.ds(j * count, count), at],
+                            jnp.where(nearer == j, mid[:, at], far[:, at]),
+                        )
+                        total = total + rim.astype(jnp.float32)
+                    c = core if who == 0 else 1 - core
+                    for i in range(2):
+                        to = (((pair * 2 + j) * 2 + i) * 2 + c) * cols
+                        rows[pl.ds(pl.multiple_of(to, 8), cols), :] = total[
+                            i * cols : (i + 1) * cols
+                        ]
         for j in range(rows.shape[0] // LANES):
             tile = rows[pl.ds(j * LANES, LANES), :]
             out[f, :, pl.ds(j * LANES, LANES)] = tile.T.astype(out.dtype)
@@ -358,9 +371,6 @@
     def up(r):
         return lambda g, d: (g, d + r * strips) if d + r * strips < devices else None
 
-    def up_across(g, d):
-        return (g, (d + strips) ^ 1) if d + strips < devices else None
-
     def along(**pairs):
         table = {int(a[1:]): b for a, b in pairs.items()}
         return lambda g, d: (
@@ -380,11 +390,14 @@
     half = -(-rows // 16) * 8
     whole = conv_weight.transpose(0, 2, 1).reshape(rows, width)
     piece = half_of(side, whole, half)
+    rest = half_of(1 - side, whole, half)
     zp1 = send(piece, along(z0=1, z1=0, z2=3, z3=2))
     zp2 = send(piece, along(z1=2, z2=1))
     zp3 = send(zp1, along(z1=2, z2=1))
     zp4 = send(zp2, along(z1=0, z2=3))
     zp5 = send(zp3, along(z1=0, z2=3))
+    zr2 = send(rest, along(z1=2, z2=1))
+    zr4 = send(zr2, along(z1=0, z2=3))
     outer = (z == 0) | (z == TB - 1)
     slot_b = jnp.where(outer, zp4, zp2)
     slot_c = jnp.where(outer, zp5, zp3)
@@ -392,24 +405,26 @@
     ya = send(zp1, to_y)
     yb = send(slot_b, to_y)
     yc = send(slot_c, to_y)
-    rest = half_of(1 - side, whole, half)
     early_pieces = [whole, y0, send(rest, to_y), zp1, send(zp1, to_x), ya, send(ya, to_x)]
-    late_pieces = [
+    mid_pieces = [
         slot_b,
-        send(slot_b, to_x),
+        zr4,
+        zr2,
         yb,
         send(yb, to_x),
-        slot_c,
-        send(slot_c, to_x),
-        yc,
-        send(yc, to_x),
     ]
+    late_pieces = [slot_c, send(slot_c, to_x), yc, send(yc, to_x)]
 
     quarter = width // 4
     kept, given = local_state(mine, k, v)
-    chip = add_up(kept, send(given, to_core))
-    plane = add_up(chip[:quarter], send(chip[quarter:], to_y))
-    share = add_up(plane, *[send(plane, up(r)) for r in (1, 2, 3)])
+    from_core = send(given, to_core)
+    chip = add_up(kept, from_core)
+    from_y = send(chip[quarter:], to_y)
+    plane = add_up(chip[:quarter], from_y)
+    below = send(plane, up(1))
+    two = add_up(plane, below)
+    below = send(two, up(2))
+    share = add_up(two, below)
     beside = send(share, to_y)
     states = [share, send(share, to_core), beside, send(beside, to_core)]
     states = [vm(s) for s in states]
@@ -419,39 +434,45 @@
     early = attend((0,), mine, q, states, gain)
     early_other = vm(send(early, to_core))
 
-    part_rows = cols * devices // 4
-    sums, rims = [], []
-    for name, pieces in (("a", early_pieces), ("b", late_pieces)):
-        keep, give, taps = pl.pallas_call(
-            functools.partial(rim_kernel, cols, half, name == "b"),
+    pair_rows = cols * devices // 4
+    rims, taps = [], []
+    for name, pieces in (("a", early_pieces), ("b", mid_pieces), ("c", late_pieces)):
+        count = pair_rows if name == "a" else pair_rows // 2
+        rim, w = pl.pallas_call(
+            functools.partial(rim_kernel, cols, half, "abc".index(name)),
             in_specs=[SMEM] + [VMEM] * (2 + len(pieces)),
-            out_specs=[VMEM] * 3,
-            out_shape=[pltpu.VMEM((part_rows, 2 * pixels), jnp.bfloat16)] * 2
-            + [pltpu.VMEM((3, part_rows, width), jnp.bfloat16)],
-            scratch_shapes=[pltpu.SemaphoreType.DMA((24,))],
+            out_specs=[VMEM] * 2,
+            out_shape=[
+                pltpu.VMEM((count, 4 * pixels), jnp.bfloat16),
+                pltpu.VMEM((3, count, width), jnp.bfloat16),
+            ],
             compiler_params=limit(16),
             name="rim",
-        )(code, late, late_other, *[vm(piece) for piece in pieces])
-        rims += [send(keep, up(1)), send(give, up_across)]
+        )(code, late, late_other, *[p if p is whole else vm(p) for p in pieces])
+        rim = send(rim, up(1))
+        rims += [rim, send(rim, to_core)]
+        taps.append(w)
+    sums = []
+    for name, parts in (("a", taps[:1]), ("b", taps[1:])):
         keep, give = pl.pallas_call(
-            own_kernel,
-            in_specs=[VMEM] * 5,
+            functools.partial(own_kernel, name == "b"),
+            in_specs=[SMEM] + [VMEM] * (4 + len(parts)),
             out_specs=[VMEM] * 2,
-            out_shape=[pltpu.VMEM((part_rows, 3 * pixels), jnp.float32)] * 2,
+            out_shape=[pltpu.VMEM((pair_rows, 3 * pixels), jnp.float32)] * 2,
             compiler_params=limit(16),
             name="own",
-        )(late, late_other, early, early_other, taps)
-        sums += [keep, send(give, to_core)]
+        )(code, late, late_other, early, early_other, *parts)
+        sums += [keep, vm(send(give, to_core))]
 
     result = pl.pallas_call(
         functools.partial(out_kernel, cols),
-        in_specs=[SMEM] + [VMEM] * 8,
+        in_specs=[SMEM] + [VMEM] * 10,
         out_specs=VMEM,
-        out_shape=jax.ShapeDtypeStruct((frames, pixels, 4 * part_rows), jnp.bfloat16),
-        scratch_shapes=[pltpu.VMEM((4 * part_rows, pixels), jnp.float32)],
+        out_shape=jax.ShapeDtypeStruct((frames, pixels, 4 * pair_rows), jnp.bfloat16),
+        scratch_shapes=[pltpu.VMEM((4 * pair_rows, pixels), jnp.float32)],
         compiler_params=limit(16),
         name="out",
-    )(code, *[vm(part) for part in sums + rims])
+    )(code, *sums, *[vm(rim) for rim in rims])
     return result[None]
 
 

time: 175 us -> 161 us (0.920)
  waiting for transfers between devices: 92.1 us -> 78.6 us
  starting transfers between devices: 33.2 us -> 38.2 us
  Pallas kernels: 32.2 us -> 28.6 us
    ppermute x32 -> x34, waiting for transfers between devices: 92.1 us -> 78.6 us  [send(): return lax.ppermute(block, axes, route)]
    pallas_call x4 -> x5, Pallas kernels: 19.9 us -> 14.7 us  [the longest x3 7.58 us: tuned(): pl.pallas_call(functools.partial(rim_kernel, cols, half, 'abc'.index(name...]
    ppermute x32 -> x34, starting transfers between devices: 33.2 us -> 38.2 us  [send(): return lax.ppermute(block, axes, route)]
    unnamed x38 -> x42, local copies, waits for them, and re-layouts: 9.13 us -> 7.5 us
  transfers between devices with their start and end apart: 32 -> 34, of which waited for: 16 -> 14; matrix products, arithmetic and copies ran while one was open for 2% -> 2% of each run, Pallas kernels for 14% -> 13%
where the time goes in v2:
time: 161 us; the launch traced here: 158 us
  waiting for transfers between devices  78.6 us (49%)
  starting transfers between devices  38.2 us (24%)
  Pallas kernels  28.6 us (18%)
  local copies, waits for them, and re-layouts  7.86 us (5%)
  other arithmetic  4.14 us (3%)
    ppermute x34, waiting for transfers between devices, send(): return lax.ppermute(block, axes, route)  78.6 us
    ppermute x34, starting transfers between devices, send(): return lax.ppermute(block, axes, route)  38.2 us
    pallas_call x3, Pallas kernels, tuned(): pl.pallas_call(functools.partial(rim_kernel, cols, half, 'abc'.index(name...  7.58 us
    unnamed x42, local copies, waits for them, and re-layouts  7.5 us
    pallas_call x2, Pallas kernels, tuned(): pl.pallas_call(functools.partial(own_kernel, name == 'b'), in_specs=[SMEM...  7.13 us
    pallas_call x1, Pallas kernels, local_state(): pl.pallas_call(state_kernel, grid_spec=pltpu.PrefetchScalarGridSpec(num_s...  6.29 us
    pallas_call x2, Pallas kernels, half_of(): pl.pallas_call(functools.partial(slice_kernel, rows - half), in_specs=[SM...  3.83 us
  transfers between devices with their start and end apart: 34, of which 14 were waited for; matrix products, arithmetic and copies ran while one was open for 2% of the time, Pallas kernels for 13%

profile of v2, /device:TPU:18, one launch (start us, length us, event | category | flops | bytes accessed | tf_op | source)
XLA Modules:
  0.0 157.8 jit_solution(15587797247981684627)
XLA Ops:
  0.0 6.3 %local_state.1 = (bf16[1120,128]{1,0:T(8,128)(2,1)}, bf16[1120,128]{1,0:T(8,128)(2,1)}) custom-call(s32[1]{0:T(128)} %bitcast.1.mine, bf16[3,2240,128]{2,1,0:T(8,128)(2,1)} %bitcast.21, bf16[3,2240,128]{2,1,0:T(8,128)(2,1)} %bitcast.22), custom_call_target="tpu_custom_call" | custom-call | tf_op jit(solution)/shard_map/local_state/pallas_call | solution.py:150
  10.7 4.3 %collective-permute-done.1 = bf16[560,128]{1,0:T(8,128)(2,1)S(1)} collective-permute-done((bf16[560,128]{1,0:T(8,128)(2,1)S(1)}, bf16[560,128]{1,0:T(8,128)(2,1)S(1)}, u32[]{:S(2)}, u32[]{:S(2)}) %collective-permute-start.1) | collective-permute-done | bytes 143392 | tf_op jit(solution)/shard_map/ppermute | solution.py:360
  15.0 3.5 %collective-permute-start.2 = (bf16[560,128]{1,0:T(8,128)(2,1)S(1)}, bf16[560,128]{1,0:T(8,128)(2,1)S(1)}, u32[]{:S(2)}, u32[]{:S(2)}) collective-permute-start(bf16[560,128]{1,0:T(8,128)(2,1)S(1)} %add_convert_fusion.3), channel_id=1, source_target_pairs={{0,4},{1,5},{2,6},{3,7},{4,8},{5,9},{6,10},{7,11},{8,12},{9,13},{1... | collective-permute-start | bytes 430088 | tf_op jit(solution)/shard_map/ppermute | solution.py:360
  18.6 1.9 %half_of.2 = bf16[112,2240]{1,0:T(8,128)(2,1)} custom-call(s32[1]{0:T(128)} %bitcast.11.x_ref, bf16[216,2240]{1,0:T(8,128)(2,1)} %bitcast.16), custom_call_target="tpu_custom_call" | custom-call | tf_op jit(solution)/shard_map/half_of/pallas_call | solution.py:111
  20.5 2.5 %collective-permute-start.16 = (bf16[112,2240]{1,0:T(8,128)(2,1)}, bf16[112,2240]{1,0:T(8,128)(2,1)}, u32[]{:S(2)}, u32[]{:S(2)}) collective-permute-start(bf16[112,2240]{1,0:T(8,128)(2,1)} %half_of.2), channel_id=1, source_target_pairs={{4,8},{5,9},{6,10},{7,11},{8,4},{9,5},{10,6},{11,7},{20,24},{21,25... | collective-permute-start | bytes 1505288 | tf_op jit(solution)/shard_map/ppermute | solution.py:360
  24.4 15.7 %collective-permute-done.16 = bf16[112,2240]{1,0:T(8,128)(2,1)} collective-permute-done((bf16[112,2240]{1,0:T(8,128)(2,1)}, bf16[112,2240]{1,0:T(8,128)(2,1)}, u32[]{:S(2)}, u32[]{:S(2)}) %collective-permute-start.16) | collective-permute-done | bytes 501792 | tf_op jit(solution)/shard_map/ppermute | solution.py:360
  40.1 2.1 %collective-permute-start.17 = (bf16[112,2240]{1,0:T(8,128)(2,1)}, bf16[112,2240]{1,0:T(8,128)(2,1)}, u32[]{:S(2)}, u32[]{:S(2)}) collective-permute-start(bf16[112,2240]{1,0:T(8,128)(2,1)} %collective-permute-done.16), channel_id=1, source_target_pairs={{4,0},{5,1},{6,2},{7,3},{8,12},{9,13},{10,14},{11,15},{20,16},{21,... | collective-permute-start | bytes 1505288 | tf_op jit(solution)/shard_map/ppermute | solution.py:360
  45.8 3.6 %collective-permute-done.5.s2 = bf16[560,128]{1,0:T(8,128)(2,1)S(1)} collective-permute-done((bf16[560,128]{1,0:T(8,128)(2,1)S(1)}, bf16[560,128]{1,0:T(8,128)(2,1)S(1)}, u32[]{:S(2)}, u32[]{:S(2)}) %collective-permute-start.5) | collective-permute-done | bytes 143392 | tf_op jit(solution)/shard_map/ppermute | solution.py:360
  54.1 3.9 %collective-permute-start.18 = (bf16[112,2240]{1,0:T(8,128)(2,1)}, bf16[112,2240]{1,0:T(8,128)(2,1)}, u32[]{:S(2)}, u32[]{:S(2)}) collective-permute-start(bf16[112,2240]{1,0:T(8,128)(2,1)} %half_of.3), channel_id=1, source_target_pairs={{4,8},{5,9},{6,10},{7,11},{8,4},{9,5},{10,6},{11,7},{20,24},{21,25... | collective-permute-start | bytes 1505288 | tf_op jit(solution)/shard_map/ppermute | solution.py:360
  65.8 7.5 %collective-permute-done.23 = bf16[112,2240]{1,0:T(8,128)(2,1)S(1)} collective-permute-done((bf16[112,2240]{1,0:T(8,128)(2,1)}, bf16[112,2240]{1,0:T(8,128)(2,1)S(1)}, u32[]{:S(2)}, u32[]{:S(2)}) %collective-permute-start.23) | collective-permute-done | bytes 501792 | tf_op jit(solution)/shard_map/ppermute | solution.py:360
  75.2 10.6 %collective-permute-done.13.refs_5_ = bf16[112,2240]{1,0:T(8,128)(2,1)S(1)} collective-permute-done((bf16[112,2240]{1,0:T(8,128)(2,1)}, bf16[112,2240]{1,0:T(8,128)(2,1)S(1)}, u32[]{:S(2)}, u32[]{:S(2)}) %collective-permute-start.13) | collective-permute-done | bytes 501792 | tf_op jit(solution)/shard_map/ppermute | solution.py:360
  90.7 8.5 %collective-permute-done.14.refs_6_ = bf16[112,2240]{1,0:T(8,128)(2,1)S(1)} collective-permute-done((bf16[112,2240]{1,0:T(8,128)(2,1)S(1)}, bf16[112,2240]{1,0:T(8,128)(2,1)S(1)}, u32[]{:S(2)}, u32[]{:S(2)}) %collective-permute-start.14) | collective-permute-done | bytes 501792 | tf_op jit(solution)/shard_map/ppermute | solution.py:360
  100.0 2.6 %collective-permute-start.19 = (bf16[112,2240]{1,0:T(8,128)(2,1)}, bf16[112,2240]{1,0:T(8,128)(2,1)}, u32[]{:S(2)}, u32[]{:S(2)}) collective-permute-start(bf16[112,2240]{1,0:T(8,128)(2,1)} %collective-permute-done.18.refs_2_), channel_id=1, source_target_pairs={{4,0},{5,1},{6,2},{7,3},{8,12},{9,13},{10,14},{11,15},{20,16},{21,... | collective-permute-start | bytes 1505288 | tf_op jit(solution)/shard_map/ppermute | solution.py:360
  103.2 7.4 %collective-permute-done.25.refs_2_ = bf16[112,2240]{1,0:T(8,128)(2,1)} collective-permute-done((bf16[112,2240]{1,0:T(8,128)(2,1)}, bf16[112,2240]{1,0:T(8,128)(2,1)}, u32[]{:S(2)}, u32[]{:S(2)}) %collective-permute-start.25) | collective-permute-done | bytes 501792 | tf_op jit(solution)/shard_map/ppermute | solution.py:360
  116.8 2.7 %rim.3 = (bf16[288,512]{1,0:T(8,128)(2,1)S(1)}, bf16[3,288,2240]{2,1,0:T(8,128)(2,1)S(1)}) custom-call(s32[1]{0:T(128)} %bitcast.code, bf16[2240,256]{1,0:T(8,128)(2,1)S(1)} %attend.2.n_own, bf16[2240,256]{1,0:T(8,128)(2,1)S(1)} %collective-permute-done.7.n_other, bf16[216,2240]{1,0:T(8,128)(2,1)S(1)} %bitcast.18, ...), custom_call_target="tpu_custom_call" | custom-call | tf_op jit(solution)/shard_map/rim/pallas_call | solution.py:441
  119.5 1.9 %collective-permute-start.28 = (bf16[288,512]{1,0:T(8,128)(2,1)S(1)}, bf16[288,512]{1,0:T(8,128)(2,1)S(1)}, u32[]{:S(2)}, u32[]{:S(2)}) collective-permute-start(bf16[288,512]{1,0:T(8,128)(2,1)S(1)} %get-tuple-element.26), channel_id=1, source_target_pairs={{0,4},{1,5},{2,6},{3,7},{4,8},{5,9},{6,10},{7,11},{8,12},{9,13},{1... | collective-permute-start | bytes 884744 | tf_op jit(solution)/shard_map/ppermute | solution.py:360
  121.4 3.6 %own.2 = (f32[288,384]{1,0:T(8,128)S(1)}, f32[288,384]{1,0:T(8,128)S(1)}) custom-call(s32[1]{0:T(128)} %bitcast.code, bf16[2240,256]{1,0:T(8,128)(2,1)S(1)} %attend.2.n_own, bf16[2240,256]{1,0:T(8,128)(2,1)S(1)} %collective-permute-done.7.n_other, bf16[2240,128]{1,0:T(8,128)(2,1)} %attend.3.z_own, bf16[2240,128]{1,0:T(8,128)(2,1)} %collective-permute-done.8.z_other, ...), custom_call_target="tpu_custom_call" | custom-call | tf_op jit(solution)/shard_map/own/pallas_call | solution.py:457
  125.1 2.4 %rim.4 = (bf16[144,512]{1,0:T(8,128)(2,1)S(1)}, bf16[3,144,2240]{2,1,0:T(8,128)(2,1)S(1)}) custom-call(s32[1]{0:T(128)} %bitcast.code, bf16[2240,256]{1,0:T(8,128)(2,1)S(1)} %attend.2.n_own, bf16[2240,256]{1,0:T(8,128)(2,1)S(1)} %collective-permute-done.7.n_other, bf16[112,2240]{1,0:T(8,128)(2,1)S(1)} %copy-done.4, ...), custom_call_target="tpu_custom_call" | custom-call | tf_op jit(solution)/shard_map/rim/pallas_call | solution.py:441
  128.7 8.7 %collective-permute-done.26.refs_3_ = bf16[112,2240]{1,0:T(8,128)(2,1)} collective-permute-done((bf16[112,2240]{1,0:T(8,128)(2,1)}, bf16[112,2240]{1,0:T(8,128)(2,1)}, u32[]{:S(2)}, u32[]{:S(2)}) %collective-permute-start.26) | collective-permute-done | bytes 501792 | tf_op jit(solution)/shard_map/ppermute | solution.py:360
  137.4 2.5 %rim.5 = (bf16[144,512]{1,0:T(8,128)(2,1)S(1)}, bf16[3,144,2240]{2,1,0:T(8,128)(2,1)S(1)}) custom-call(s32[1]{0:T(128)} %bitcast.code, bf16[2240,256]{1,0:T(8,128)(2,1)S(1)} %attend.2.n_own, bf16[2240,256]{1,0:T(8,128)(2,1)S(1)} %collective-permute-done.7.n_other, bf16[112,2240]{1,0:T(8,128)(2,1)} %broadcast_select_fusion.refs_0_, ...), custom_call_target="tpu_custom_call" | custom-call | tf_op jit(solution)/shard_map/rim/pallas_call | solution.py:441
  139.9 3.6 %own.3 = (f32[288,384]{1,0:T(8,128)S(1)}, f32[288,384]{1,0:T(8,128)S(1)}) custom-call(s32[1]{0:T(128)} %bitcast.code, bf16[2240,256]{1,0:T(8,128)(2,1)S(1)} %attend.2.n_own, bf16[2240,256]{1,0:T(8,128)(2,1)S(1)} %collective-permute-done.7.n_other, bf16[2240,128]{1,0:T(8,128)(2,1)} %attend.3.z_own, bf16[2240,128]{1,0:T(8,128)(2,1)} %collective-permute-done.8.z_other, ...), custom_call_target="tpu_custom_call" | custom-call | tf_op jit(solution)/shard_map/own/pallas_call | solution.py:457
  143.6 1.9 %collective-permute-start.30 = (bf16[144,512]{1,0:T(8,128)(2,1)S(1)}, bf16[144,512]{1,0:T(8,128)(2,1)S(1)}, u32[]{:S(2)}, u32[]{:S(2)}) collective-permute-start(bf16[144,512]{1,0:T(8,128)(2,1)S(1)} %get-tuple-element.27), channel_id=1, source_target_pairs={{0,4},{1,5},{2,6},{3,7},{4,8},{5,9},{6,10},{7,11},{8,12},{9,13},{1... | collective-permute-start | bytes 442376 | tf_op jit(solution)/shard_map/ppermute | solution.py:360
  148.0 4.2 %collective-permute-done.30.refs_6_ = bf16[144,512]{1,0:T(8,128)(2,1)S(1)} collective-permute-done((bf16[144,512]{1,0:T(8,128)(2,1)S(1)}, bf16[144,512]{1,0:T(8,128)(2,1)S(1)}, u32[]{:S(2)}, u32[]{:S(2)}) %collective-permute-start.30) | collective-permute-done | bytes 147488 | tf_op jit(solution)/shard_map/ppermute | solution.py:360
  152.2 2.7 %collective-permute-done.32.refs_8_ = bf16[144,512]{1,0:T(8,128)(2,1)S(1)} collective-permute-done((bf16[144,512]{1,0:T(8,128)(2,1)S(1)}, bf16[144,512]{1,0:T(8,128)(2,1)S(1)}, u32[]{:S(2)}, u32[]{:S(2)}) %collective-permute-start.32) | collective-permute-done | bytes 147488 | tf_op jit(solution)/shard_map/ppermute | solution.py:360
  (105 shorter events, 42.8 us)
Async XLA Ops:
  20.5 19.6 %collective-permute-start.16 = (bf16[112,2240]{1,0:T(8,128)(2,1)}, bf16[112,2240]{1,0:T(8,128)(2,1)}, u32[]{:S(2)}, u32[]{:S(2)}) collective-permute-start(bf16[112,2240]{1,0:T(8,128)(2,1)} %half_of.2), channel_id=1, source_target_pairs={{4,8},{5,9},{6,10},{7,11},{8,4},{9,5},{10,6},{11,7},{20,24},{21,25... | collective-permute-start | bytes 1505288 | tf_op jit(solution)/shard_map/ppermute | solution.py:360
  23.0 19.2 %collective-permute-start.11 = (bf16[112,2240]{1,0:T(8,128)(2,1)}, bf16[112,2240]{1,0:T(8,128)(2,1)}, u32[]{:S(2)}, u32[]{:S(2)}) collective-permute-start(bf16[112,2240]{1,0:T(8,128)(2,1)} %half_of.2), channel_id=1, source_target_pairs={{0,4},{1,5},{2,6},{3,7},{4,0},{5,1},{6,2},{7,3},{8,12},{9,13},{10,... | collective-permute-start | bytes 1505288 | tf_op jit(solution)/shard_map/ppermute | solution.py:360
  23.1 21.0 %collective-permute-start.3 = (bf16[560,128]{1,0:T(8,128)(2,1)S(1)}, bf16[560,128]{1,0:T(8,128)(2,1)S(1)}, u32[]{:S(2)}, u32[]{:S(2)}) collective-permute-start(bf16[560,128]{1,0:T(8,128)(2,1)S(1)} %add_convert_fusion.2), channel_id=1, source_target_pairs={{0,8},{1,9},{2,10},{3,11},{4,12},{5,13},{6,14},{7,15},{16,24},{17,... | collective-permute-start | bytes 430088 | tf_op jit(solution)/shard_map/ppermute | solution.py:360
  40.1 20.1 %collective-permute-start.17 = (bf16[112,2240]{1,0:T(8,128)(2,1)}, bf16[112,2240]{1,0:T(8,128)(2,1)}, u32[]{:S(2)}, u32[]{:S(2)}) collective-permute-start(bf16[112,2240]{1,0:T(8,128)(2,1)} %collective-permute-done.16), channel_id=1, source_target_pairs={{4,0},{5,1},{6,2},{7,3},{8,12},{9,13},{10,14},{11,15},{20,16},{21,... | collective-permute-start | bytes 1505288 | tf_op jit(solution)/shard_map/ppermute | solution.py:360
  42.2 18.6 %collective-permute-start.22 = (bf16[112,2240]{1,0:T(8,128)(2,1)}, bf16[112,2240]{1,0:T(8,128)(2,1)}, u32[]{:S(2)}, u32[]{:S(2)}) collective-permute-start(bf16[112,2240]{1,0:T(8,128)(2,1)} %collective-permute-done.11.refs_3_), channel_id=1, source_target_pairs={{4,8},{5,9},{6,10},{7,11},{8,4},{9,5},{10,6},{11,7},{20,24},{21,25... | collective-permute-start | bytes 1505288 | tf_op jit(solution)/shard_map/ppermute | solution.py:360
  49.3 14.9 %collective-permute-start.9 = (bf16[112,2240]{1,0:T(8,128)(2,1)}, bf16[112,2240]{1,0:T(8,128)(2,1)}, u32[]{:S(2)}, u32[]{:S(2)}) collective-permute-start(bf16[112,2240]{1,0:T(8,128)(2,1)} %half_of.2), channel_id=1, source_target_pairs={{0,2},{1,3},{2,0},{3,1},{4,6},{5,7},{6,4},{7,5},{8,10},{9,11},{10,... | collective-permute-start | bytes 1505288 | tf_op jit(solution)/shard_map/ppermute | solution.py:360
  52.8 33.6 %collective-permute-start.10 = (bf16[112,2240]{1,0:T(8,128)(2,1)}, bf16[112,2240]{1,0:T(8,128)(2,1)S(1)}, u32[]{:S(2)}, u32[]{:S(2)}) collective-permute-start(bf16[112,2240]{1,0:T(8,128)(2,1)} %half_of.3), channel_id=1, source_target_pairs={{0,2},{1,3},{2,0},{3,1},{4,6},{5,7},{6,4},{7,5},{8,10},{9,11},{10,... | collective-permute-start | bytes 1505288 | tf_op jit(solution)/shard_map/ppermute | solution.py:360
  54.1 33.8 %collective-permute-start.18 = (bf16[112,2240]{1,0:T(8,128)(2,1)}, bf16[112,2240]{1,0:T(8,128)(2,1)}, u32[]{:S(2)}, u32[]{:S(2)}) collective-permute-start(bf16[112,2240]{1,0:T(8,128)(2,1)} %half_of.3), channel_id=1, source_target_pairs={{4,8},{5,9},{6,10},{7,11},{8,4},{9,5},{10,6},{11,7},{20,24},{21,25... | collective-permute-start | bytes 1505288 | tf_op jit(solution)/shard_map/ppermute | solution.py:360
  60.2 29.6 %collective-permute-start.12 = (bf16[112,2240]{1,0:T(8,128)(2,1)}, bf16[112,2240]{1,0:T(8,128)(2,1)S(1)}, u32[]{:S(2)}, u32[]{:S(2)}) collective-permute-start(bf16[112,2240]{1,0:T(8,128)(2,1)} %collective-permute-done.11.refs_3_), channel_id=1, source_target_pairs={{0,16},{1,17},{2,18},{3,19},{4,20},{5,21},{6,22},{7,23},{8,24},{9,... | collective-permute-start | bytes 1505288 | tf_op jit(solution)/shard_map/ppermute | solution.py:360
  60.8 12.6 %collective-permute-start.23 = (bf16[112,2240]{1,0:T(8,128)(2,1)}, bf16[112,2240]{1,0:T(8,128)(2,1)S(1)}, u32[]{:S(2)}, u32[]{:S(2)}) collective-permute-start(bf16[112,2240]{1,0:T(8,128)(2,1)} %collective-permute-done.22), channel_id=1, source_target_pairs={{4,0},{5,1},{6,2},{7,3},{8,12},{9,13},{10,14},{11,15},{20,16},{21,... | collective-permute-start | bytes 1505288 | tf_op jit(solution)/shard_map/ppermute | solution.py:360
  64.3 21.6 %collective-permute-start.13 = (bf16[112,2240]{1,0:T(8,128)(2,1)}, bf16[112,2240]{1,0:T(8,128)(2,1)S(1)}, u32[]{:S(2)}, u32[]{:S(2)}) collective-permute-start(bf16[112,2240]{1,0:T(8,128)(2,1)} %collective-permute-done.11.refs_3_), channel_id=1, source_target_pairs={{0,2},{1,3},{2,0},{3,1},{4,6},{5,7},{6,4},{7,5},{8,10},{9,11},{10,... | collective-permute-start | bytes 1505288 | tf_op jit(solution)/shard_map/ppermute | solution.py:360
  73.3 38.7 %collective-permute-start.7 = (bf16[2240,256]{1,0:T(8,128)(2,1)S(1)}, bf16[2240,256]{1,0:T(8,128)(2,1)S(1)}, u32[]{:S(2)}, u32[]{:S(2)}) collective-permute-start(bf16[2240,256]{1,0:T(8,128)(2,1)S(1)} %attend.2.n_own), channel_id=1, source_target_pairs={{0,1},{1,0},{2,3},{3,2},{4,5},{5,4},{6,7},{7,6},{8,9},{9,8},{10,11... | collective-permute-start | bytes 3440648 | tf_op jit(solution)/shard_map/ppermute | solution.py:360
  85.8 13.3 %collective-permute-start.14 = (bf16[112,2240]{1,0:T(8,128)(2,1)S(1)}, bf16[112,2240]{1,0:T(8,128)(2,1)S(1)}, u32[]{:S(2)}, u32[]{:S(2)}) collective-permute-start(bf16[112,2240]{1,0:T(8,128)(2,1)S(1)} %collective-permute-done.13.refs_5_), channel_id=1, source_target_pairs={{0,16},{1,17},{2,18},{3,19},{4,20},{5,21},{6,22},{7,23},{8,24},{9,... | collective-permute-start | bytes 1505288 | tf_op jit(solution)/shard_map/ppermute | solution.py:360
  86.4 16.3 %collective-permute-start.20 = (bf16[112,2240]{1,0:T(8,128)(2,1)S(1)}, bf16[112,2240]{1,0:T(8,128)(2,1)}, u32[]{:S(2)}, u32[]{:S(2)}) collective-permute-start(bf16[112,2240]{1,0:T(8,128)(2,1)S(1)} %broadcast_select_fusion.1.refs_0_), channel_id=1, source_target_pairs={{0,2},{1,3},{2,0},{3,1},{4,6},{5,7},{6,4},{7,5},{8,10},{9,11},{10,... | collective-permute-start | bytes 1505288 | tf_op jit(solution)/shard_map/ppermute | solution.py:360
  87.9 22.7 %collective-permute-start.25 = (bf16[112,2240]{1,0:T(8,128)(2,1)}, bf16[112,2240]{1,0:T(8,128)(2,1)}, u32[]{:S(2)}, u32[]{:S(2)}) collective-permute-start(bf16[112,2240]{1,0:T(8,128)(2,1)} %broadcast_select_fusion.refs_0_), channel_id=1, source_target_pairs={{0,2},{1,3},{2,0},{3,1},{4,6},{5,7},{6,4},{7,5},{8,10},{9,11},{10,... | collective-permute-start | bytes 1505288 | tf_op jit(solution)/shard_map/ppermute | solution.py:360
  90.7 28.8 %collective-permute-start.8 = (bf16[2240,128]{1,0:T(8,128)(2,1)}, bf16[2240,128]{1,0:T(8,128)(2,1)}, u32[]{:S(2)}, u32[]{:S(2)}) collective-permute-start(bf16[2240,128]{1,0:T(8,128)(2,1)} %attend.3.z_own), channel_id=1, source_target_pairs={{0,1},{1,0},{2,3},{3,2},{4,5},{5,4},{6,7},{7,6},{8,9},{9,8},{10,11... | collective-permute-start | bytes 1720328 | tf_op jit(solution)/shard_map/ppermute | solution.py:360
  100.0 25.0 %collective-permute-start.19 = (bf16[112,2240]{1,0:T(8,128)(2,1)}, bf16[112,2240]{1,0:T(8,128)(2,1)}, u32[]{:S(2)}, u32[]{:S(2)}) collective-permute-start(bf16[112,2240]{1,0:T(8,128)(2,1)} %collective-permute-done.18.refs_2_), channel_id=1, source_target_pairs={{4,0},{5,1},{6,2},{7,3},{8,12},{9,13},{10,14},{11,15},{20,16},{21,... | collective-permute-start | bytes 1505288 | tf_op jit(solution)/shard_map/ppermute | solution.py:360
  102.7 22.4 %collective-permute-start.21 = (bf16[112,2240]{1,0:T(8,128)(2,1)}, bf16[112,2240]{1,0:T(8,128)(2,1)}, u32[]{:S(2)}, u32[]{:S(2)}) collective-permute-start(bf16[112,2240]{1,0:T(8,128)(2,1)} %collective-permute-done.20.refs_3_), channel_id=1, source_target_pairs={{0,16},{1,17},{2,18},{3,19},{4,20},{5,21},{6,22},{7,23},{8,24},{9,... | collective-permute-start | bytes 1505288 | tf_op jit(solution)/shard_map/ppermute | solution.py:360
  110.6 18.1 %collective-permute-start.24 = (bf16[112,2240]{1,0:T(8,128)(2,1)}, bf16[112,2240]{1,0:T(8,128)(2,1)}, u32[]{:S(2)}, u32[]{:S(2)}) collective-permute-start(bf16[112,2240]{1,0:T(8,128)(2,1)} %broadcast_select_fusion.refs_0_), channel_id=1, source_target_pairs={{0,16},{1,17},{2,18},{3,19},{4,20},{5,21},{6,22},{7,23},{8,24},{9,... | collective-permute-start | bytes 1505288 | tf_op jit(solution)/shard_map/ppermute | solution.py:360
  112.1 25.3 %collective-permute-start.26 = (bf16[112,2240]{1,0:T(8,128)(2,1)}, bf16[112,2240]{1,0:T(8,128)(2,1)}, u32[]{:S(2)}, u32[]{:S(2)}) collective-permute-start(bf16[112,2240]{1,0:T(8,128)(2,1)} %collective-permute-done.25.refs_2_), channel_id=1, source_target_pairs={{0,16},{1,17},{2,18},{3,19},{4,20},{5,21},{6,22},{7,23},{8,24},{9,... | collective-permute-start | bytes 1505288 | tf_op jit(solution)/shard_map/ppermute | solution.py:360
  119.5 26.0 %collective-permute-start.28 = (bf16[288,512]{1,0:T(8,128)(2,1)S(1)}, bf16[288,512]{1,0:T(8,128)(2,1)S(1)}, u32[]{:S(2)}, u32[]{:S(2)}) collective-permute-start(bf16[288,512]{1,0:T(8,128)(2,1)S(1)} %get-tuple-element.26), channel_id=1, source_target_pairs={{0,4},{1,5},{2,6},{3,7},{4,8},{5,9},{6,10},{7,11},{8,12},{9,13},{1... | collective-permute-start | bytes 884744 | tf_op jit(solution)/shard_map/ppermute | solution.py:360
  125.0 29.9 %collective-permute-start.15 = (f32[288,384]{1,0:T(8,128)S(1)}, f32[288,384]{1,0:T(8,128)S(1)}, u32[]{:S(2)}, u32[]{:S(2)}) collective-permute-start(f32[288,384]{1,0:T(8,128)S(1)} %get-tuple-element.21), channel_id=1, source_target_pairs={{0,1},{1,0},{2,3},{3,2},{4,5},{5,4},{6,7},{7,6},{8,9},{9,8},{10,11... | collective-permute-start | bytes 1327112 | tf_op jit(solution)/shard_map/ppermute | solution.py:360
  143.5 12.7 %collective-permute-start.27 = (f32[288,384]{1,0:T(8,128)S(1)}, f32[288,384]{1,0:T(8,128)S(1)}, u32[]{:S(2)}, u32[]{:S(2)}) collective-permute-start(f32[288,384]{1,0:T(8,128)S(1)} %get-tuple-element.25), channel_id=1, source_target_pairs={{0,1},{1,0},{2,3},{3,2},{4,5},{5,4},{6,7},{7,6},{8,9},{9,8},{10,11... | collective-permute-start | bytes 1327112 | tf_op jit(solution)/shard_map/ppermute | solution.py:360
  145.5 9.4 %collective-permute-start.29 = (bf16[288,512]{1,0:T(8,128)(2,1)S(1)}, bf16[288,512]{1,0:T(8,128)(2,1)S(1)}, u32[]{:S(2)}, u32[]{:S(2)}) collective-permute-start(bf16[288,512]{1,0:T(8,128)(2,1)S(1)} %collective-permute-done.28.refs_4_), channel_id=1, source_target_pairs={{0,1},{1,0},{2,3},{3,2},{4,5},{5,4},{6,7},{7,6},{8,9},{9,8},{10,11... | collective-permute-start | bytes 884744 | tf_op jit(solution)/shard_map/ppermute | solution.py:360
  (31 other events, 344.4 us)

commit v3 on v2

--- a/solution.py
+++ b/solution.py
@@ -208,35 +208,32 @@
     )(mine, queries, *states, gain)
 
 
-def place(x, outer, cols, half, tap, shards, refs, w):
+def place(x, cols, half, tap, shards, w):
     rows = 3 * cols
     lo_tap, hi_tap = tap * cols, (tap + 1) * cols
 
-    def put(ref, block, lo, hi, shift):
+    def put(ref, slot, lo, hi, shift):
         a, b = max(lo, lo_tap), min(hi, hi_tap)
         if a < b:
-            at = pl.ds(pl.multiple_of(block * cols + a - lo_tap, 8), b - a)
+            at = pl.ds(slot * cols + a - lo_tap, b - a)
             part = pl.ds(a - shift, b - a)
-            if isinstance(ref, tuple):
-                w[at, :] = jnp.where(outer, ref[0][part, :], ref[1][part, :])
-            else:
-                w[at, :] = ref[part, :]
-
-    for kind, block, *which in shards:
-        if kind == "whole":
-            put(refs[which[0]], block, 0, rows, 0)
+            w[at, :] = ref[part, :]
+
+    for slot, shard in enumerate(shards):
+        if len(shard) == 1:
+            put(shard[0], slot, 0, rows, 0)
 
     for flag in (True, False):
 
         @pl.when((x == 0) == flag)
         def _(flag=flag):
-            for kind, block, *which in shards:
-                if kind == "halves":
-                    for ref, top in ((refs[which[0]], flag), (refs[which[1]], not flag)):
+            for slot, shard in enumerate(shards):
+                if len(shard) == 2:
+                    for ref, top in ((shard[0], flag), (shard[1], not flag)):
                         if top:
-                            put(ref, block, 0, half, 0)
+                            put(ref, slot, 0, half, 0)
                         else:
-                            put(ref, block, half, rows, rows - half)
+                            put(ref, slot, half, rows, rows - half)
 
 
 def dot(a, b):
@@ -247,20 +244,14 @@
     return code // (4 * TB), code // 4 % TB, code // 2 % 2, code % 2
 
 
-def first_late(z):
-    return jnp.where(z < TB // 2, 0, 1)
-
-
-def shards_of(part, z, y):
+def blocks_of(part, z, y):
+    low = z < TB // 2
+    near = z ^ 1
+    nearer = jnp.where(low, TB // 2, TB // 2 - 1)
+    farther = jnp.where(low, TB - 1, 0)
     if part == 0:
-        here, beside = z % 2, 1 - z % 2
-        return [
-            ("halves", beside * 2 + y, 3, 4),
-            ("halves", beside * 2 + 1 - y, 5, 6),
-            ("whole", here * 2 + y, 0),
-            ("halves", here * 2 + 1 - y, 1, 2),
-        ]
-    return [("halves", y, 0, 1), ("halves", 1 - y, 2, 3)]
+        return [(z, y), (z, 1 - y), (near, y), (near, 1 - y), (nearer, y)]
+    return [(nearer, 1 - y), (farther, y), (farther, 1 - y)]
 
 
 def both_cores(own, other, at):
@@ -268,13 +259,14 @@
 
 
 def rim_kernel(cols, half, part, code, n_own, n_other, *refs):
-    pieces, (out, w) = list(refs[:-2]), refs[-2:]
-    x, z, y, _ = where_of(code[0])
-    outer = (z == 0) | (z == TB - 1)
-    if part == 1:
-        pieces[1:3] = [(pieces[1], pieces[2])]
+    pieces, (out, w) = refs[:-2], refs[-2:]
+    x, _, _, _ = where_of(code[0])
+    shards = []
+    if part == 0:
+        shards, pieces = [pieces[:1]], pieces[1:]
+    shards += [pieces[i : i + 2] for i in range(0, len(pieces), 2)]
     for tap in (2, 1, 0):
-        place(x, outer, cols, half, tap, shards_of(part, z, y), pieces, w.at[tap])
+        place(x, cols, half, tap, shards, w.at[tap])
     p = n_own.shape[1] // 2
     first = both_cores(n_own, n_other, pl.ds(0, p))
     last = both_cores(n_own, n_other, pl.ds(p, p))
@@ -282,59 +274,45 @@
     out[:, : 2 * p] = (dot(w[2], first) + dot(w[1], last)).astype(out.dtype)
 
 
-def own_kernel(late, code, n_own, n_other, z_own, z_other, *refs):
-    taps, (keep, give) = refs[:-2], refs[-2:]
-    _, z, _, _ = where_of(code[0])
+def own_kernel(n_own, n_other, z_own, z_other, w, keep, give):
     p = n_own.shape[1] // 2
     zero = jnp.concatenate([z_own[...], z_other[...]], axis=1)
     first = both_cores(n_own, n_other, pl.ds(0, p))
     last = both_cores(n_own, n_other, pl.ds(p, p))
-    for i, w in enumerate(taps):
-        count = w.shape[1]
-        to = i * count
-        if late:
-            nearer = first_late(z)
-            to = (nearer if i == 0 else 1 - nearer) * count
-        rows = pl.ds(pl.multiple_of(to, 8), count)
-        totals = (
-            dot(w[0], zero),
-            dot(w[0], first) + dot(w[1], zero),
-            dot(w[0], last) + dot(w[1], first) + dot(w[2], zero),
-        )
-        for f, total in enumerate(totals):
-            at = pl.ds(f * p, p)
-            keep[rows, at], give[rows, at] = total[:, :p], total[:, p:]
+    totals = (
+        dot(w[0], zero),
+        dot(w[0], first) + dot(w[1], zero),
+        dot(w[0], last) + dot(w[1], first) + dot(w[2], zero),
+    )
+    for f, total in enumerate(totals):
+        at = pl.ds(f * p, p)
+        keep[:, at], give[:, at] = total[:, :p], total[:, p:]
 
 
 def out_kernel(cols, code, *refs):
-    sums, rims, (out, rows) = refs[:4], refs[4:10], refs[10:]
+    sums, rims, (out, rows) = refs[:4], refs[4:8], refs[8:]
     p = out.shape[1]
-    _, z, _, core = where_of(code[0])
-    behind = z - 1
-    behind_pair = behind // 2
-    nearer = first_late(behind)
-    count = 2 * cols
+    _, z, y, core = where_of(code[0])
+
+    def at(block, who):
+        c = core if who == 0 else 1 - core
+        return pl.ds(pl.multiple_of(((block[0] * 2 + block[1]) * 2 + c) * cols, 8), cols)
+
     for f in range(3):
-        for late in range(2):
-            pair = z // 2 if late == 0 else 1 - z // 2
-            for j in range(2):
+        for part in range(2):
+            for i, block in enumerate(blocks_of(part, z, y)):
                 for who in range(2):
-                    total = sums[2 * late + who][pl.ds(j * count, count), pl.ds(f * p, p)]
-                    if f < 2:
-                        at = pl.ds((2 * f + who) * p, p)
-                        near, mid, far = rims[who], rims[2 + who], rims[4 + who]
-                        rim = jnp.where(
-                            pair == behind_pair,
-                            near[pl.ds(j * count, count), at],
-                            jnp.where(nearer == j, mid[:, at], far[:, at]),
-                        )
-                        total = total + rim.astype(jnp.float32)
-                    c = core if who == 0 else 1 - core
-                    for i in range(2):
-                        to = (((pair * 2 + j) * 2 + i) * 2 + c) * cols
-                        rows[pl.ds(pl.multiple_of(to, 8), cols), :] = total[
-                            i * cols : (i + 1) * cols
+                    total = sums[2 * part + who][pl.ds(i * cols, cols), pl.ds(f * p, p)]
+                    rows[at(block, who), :] = total
+        if f < 2:
+            for part in range(2):
+                for i, block in enumerate(blocks_of(part, jnp.maximum(z - 1, 0), y)):
+                    for who in range(2):
+                        to = at(block, who)
+                        rim = rims[2 * part + who][
+                            pl.ds(i * cols, cols), pl.ds((2 * f + who) * p, p)
                         ]
+                        rows[to, :] = rows[to, :] + rim.astype(jnp.float32)
         for j in range(rows.shape[0] // LANES):
             tile = rows[pl.ds(j * LANES, LANES), :]
             out[f, :, pl.ds(j * LANES, LANES)] = tile.T.astype(out.dtype)
@@ -400,20 +378,16 @@
     zr4 = send(zr2, along(z1=0, z2=3))
     outer = (z == 0) | (z == TB - 1)
     slot_b = jnp.where(outer, zp4, zp2)
+    rest_b = jnp.where(outer, zr4, zr2)
     slot_c = jnp.where(outer, zp5, zp3)
     y0 = send(piece, to_y)
     ya = send(zp1, to_y)
     yb = send(slot_b, to_y)
     yc = send(slot_c, to_y)
-    early_pieces = [whole, y0, send(rest, to_y), zp1, send(zp1, to_x), ya, send(ya, to_x)]
-    mid_pieces = [
-        slot_b,
-        zr4,
-        zr2,
-        yb,
-        send(yb, to_x),
+    early_pieces = [
+        whole, y0, send(y0, to_x), zp1, send(zp1, to_x), ya, send(ya, to_x), slot_b, rest_b
     ]
-    late_pieces = [slot_c, send(slot_c, to_x), yc, send(yc, to_x)]
+    late_pieces = [yb, send(rest_b, to_y), slot_c, send(slot_c, to_x), yc, send(yc, to_x)]
 
     quarter = width // 4
     kept, given = local_state(mine, k, v)
@@ -434,12 +408,11 @@
     early = attend((0,), mine, q, states, gain)
     early_other = vm(send(early, to_core))
 
-    pair_rows = cols * devices // 4
-    rims, taps = [], []
-    for name, pieces in (("a", early_pieces), ("b", mid_pieces), ("c", late_pieces)):
-        count = pair_rows if name == "a" else pair_rows // 2
+    sums, rims = [], []
+    for name, pieces in (("a", early_pieces), ("b", late_pieces)):
+        count = cols * len(blocks_of("ab".index(name), z, y))
         rim, w = pl.pallas_call(
-            functools.partial(rim_kernel, cols, half, "abc".index(name)),
+            functools.partial(rim_kernel, cols, half, "ab".index(name)),
             in_specs=[SMEM] + [VMEM] * (2 + len(pieces)),
             out_specs=[VMEM] * 2,
             out_shape=[
@@ -451,25 +424,22 @@
         )(code, late, late_other, *[p if p is whole else vm(p) for p in pieces])
         rim = send(rim, up(1))
         rims += [rim, send(rim, to_core)]
-        taps.append(w)
-    sums = []
-    for name, parts in (("a", taps[:1]), ("b", taps[1:])):
         keep, give = pl.pallas_call(
-            functools.partial(own_kernel, name == "b"),
-            in_specs=[SMEM] + [VMEM] * (4 + len(parts)),
+            own_kernel,
+            in_specs=[VMEM] * 5,
             out_specs=[VMEM] * 2,
-            out_shape=[pltpu.VMEM((pair_rows, 3 * pixels), jnp.float32)] * 2,
+            out_shape=[pltpu.VMEM((count, 3 * pixels), jnp.float32)] * 2,
             compiler_params=limit(16),
             name="own",
-        )(code, late, late_other, early, early_other, *parts)
+        )(late, late_other, early, early_other, w)
         sums += [keep, vm(send(give, to_core))]
 
     result = pl.pallas_call(
         functools.partial(out_kernel, cols),
-        in_specs=[SMEM] + [VMEM] * 10,
+        in_specs=[SMEM] + [VMEM] * 8,
         out_specs=VMEM,
-        out_shape=jax.ShapeDtypeStruct((frames, pixels, 4 * pair_rows), jnp.bfloat16),
-        scratch_shapes=[pltpu.VMEM((4 * pair_rows, pixels), jnp.float32)],
+        out_shape=jax.ShapeDtypeStruct((frames, pixels, cols * devices), jnp.bfloat16),
+        scratch_shapes=[pltpu.VMEM((cols * devices, pixels), jnp.float32)],
         compiler_params=limit(16),
         name="out",
     )(code, *sums, *[vm(rim) for rim in rims])

time: 161 us -> 152 us (0.944)
  waiting for transfers between devices: 78.6 us -> 66.1 us
  starting transfers between devices: 38.2 us -> 43.2 us
  other arithmetic: 4.14 us -> 6.87 us
  local copies, waits for them, and re-layouts: 7.86 us -> 5.38 us
    ppermute x34 -> x32, waiting for transfers between devices: 78.6 us -> 66.1 us  [send(): return lax.ppermute(block, axes, route)]
    ppermute x34 -> x32, starting transfers between devices: 38.2 us -> 43.2 us  [send(): return lax.ppermute(block, axes, route)]
    unnamed x42 -> x22, local copies, waits for them, and re-layouts: 7.5 us -> 5.02 us
    select_n x0 -> x1, other arithmetic: none -> 1.91 us  [tuned(): rest_b = jnp.where(outer, zr4, zr2)]
    pallas_call x5 -> x4, Pallas kernels: 14.7 us -> 13.4 us  [the longest x2 7.11 us: tuned(): pl.pallas_call(own_kernel, in_specs=[VMEM] * 5, out_specs=[VMEM] * 2, out...]
  transfers between devices with their start and end apart: 34 -> 32, of which waited for: 14 -> 14; matrix products, arithmetic and copies ran while one was open for 2% -> 4% of each run, Pallas kernels for 13% -> 13%
where the time goes in v3:
time: 152 us; the launch traced here: 149 us
  waiting for transfers between devices  66.1 us (43%)
  starting transfers between devices  43.2 us (28%)
  Pallas kernels  27.3 us (18%)
  other arithmetic  6.87 us (5%)
  local copies, waits for them, and re-layouts  5.38 us (4%)
    ppermute x32, waiting for transfers between devices, send(): return lax.ppermute(block, axes, route)  66.1 us
    ppermute x32, starting transfers between devices, send(): return lax.ppermute(block, axes, route)  43.2 us
    pallas_call x2, Pallas kernels, tuned(): pl.pallas_call(own_kernel, in_specs=[VMEM] * 5, out_specs=[VMEM] * 2, out...  7.11 us
    pallas_call x2, Pallas kernels, tuned(): pl.pallas_call(functools.partial(rim_kernel, cols, half, 'ab'.index(name)...  6.31 us
    pallas_call x1, Pallas kernels, local_state(): pl.pallas_call(state_kernel, grid_spec=pltpu.PrefetchScalarGridSpec(num_s...  6.29 us
    unnamed x22, local copies, waits for them, and re-layouts  5.02 us
    pallas_call x2, Pallas kernels, half_of(): pl.pallas_call(functools.partial(slice_kernel, rows - half), in_specs=[SM...  3.85 us
  transfers between devices with their start and end apart: 32, of which 14 were waited for; matrix products, arithmetic and copies ran while one was open for 4% of the time, Pallas kernels for 13%

profile of v3, /device:TPU:18, one launch (start us, length us, event | category | flops | bytes accessed | tf_op | source)
XLA Modules:
  0.0 149.1 jit_solution(2153236534347322739)
XLA Ops:
  0.0 6.3 %local_state.1 = (bf16[1120,128]{1,0:T(8,128)(2,1)}, bf16[1120,128]{1,0:T(8,128)(2,1)}) custom-call(s32[1]{0:T(128)} %bitcast.1.mine, bf16[3,2240,128]{2,1,0:T(8,128)(2,1)} %bitcast.21, bf16[3,2240,128]{2,1,0:T(8,128)(2,1)} %bitcast.22), custom_call_target="tpu_custom_call" | custom-call | tf_op jit(solution)/shard_map/local_state/pallas_call | solution.py:150
  10.7 4.3 %collective-permute-done.1 = bf16[560,128]{1,0:T(8,128)(2,1)S(1)} collective-permute-done((bf16[560,128]{1,0:T(8,128)(2,1)S(1)}, bf16[560,128]{1,0:T(8,128)(2,1)S(1)}, u32[]{:S(2)}, u32[]{:S(2)}) %collective-permute-start.1) | collective-permute-done | bytes 143392 | tf_op jit(solution)/shard_map/ppermute | solution.py:338
  15.0 3.5 %collective-permute-start.2 = (bf16[560,128]{1,0:T(8,128)(2,1)S(1)}, bf16[560,128]{1,0:T(8,128)(2,1)S(1)}, u32[]{:S(2)}, u32[]{:S(2)}) collective-permute-start(bf16[560,128]{1,0:T(8,128)(2,1)S(1)} %add_convert_fusion.3), channel_id=1, source_target_pairs={{0,4},{1,5},{2,6},{3,7},{4,8},{5,9},{6,10},{7,11},{8,12},{9,13},{1... | collective-permute-start | bytes 430088 | tf_op jit(solution)/shard_map/ppermute | solution.py:338
  18.6 1.9 %half_of.2 = bf16[112,2240]{1,0:T(8,128)(2,1)} custom-call(s32[1]{0:T(128)} %bitcast.11.x_ref, bf16[216,2240]{1,0:T(8,128)(2,1)} %bitcast.16), custom_call_target="tpu_custom_call" | custom-call | tf_op jit(solution)/shard_map/half_of/pallas_call | solution.py:111
  20.5 2.5 %collective-permute-start.15 = (bf16[112,2240]{1,0:T(8,128)(2,1)}, bf16[112,2240]{1,0:T(8,128)(2,1)}, u32[]{:S(2)}, u32[]{:S(2)}) collective-permute-start(bf16[112,2240]{1,0:T(8,128)(2,1)} %half_of.2), channel_id=1, source_target_pairs={{4,8},{5,9},{6,10},{7,11},{8,4},{9,5},{10,6},{11,7},{20,24},{21,25... | collective-permute-start | bytes 1505288 | tf_op jit(solution)/shard_map/ppermute | solution.py:338
  26.0 1.9 %half_of.3 = bf16[112,2240]{1,0:T(8,128)(2,1)} custom-call(s32[1]{0:T(128)S(6)} %sub.16.x_ref, bf16[216,2240]{1,0:T(8,128)(2,1)} %bitcast.17), custom_call_target="tpu_custom_call" | custom-call | tf_op jit(solution)/shard_map/half_of/pallas_call | solution.py:111
  28.0 6.0 %collective-permute-start.17 = (bf16[112,2240]{1,0:T(8,128)(2,1)}, bf16[112,2240]{1,0:T(8,128)(2,1)}, u32[]{:S(2)}, u32[]{:S(2)}) collective-permute-start(bf16[112,2240]{1,0:T(8,128)(2,1)} %half_of.3), channel_id=1, source_target_pairs={{4,8},{5,9},{6,10},{7,11},{8,4},{9,5},{10,6},{11,7},{20,24},{21,25... | collective-permute-start | bytes 1505288 | tf_op jit(solution)/shard_map/ppermute | solution.py:338
  34.0 6.6 %collective-permute-done.15 = bf16[112,2240]{1,0:T(8,128)(2,1)} collective-permute-done((bf16[112,2240]{1,0:T(8,128)(2,1)}, bf16[112,2240]{1,0:T(8,128)(2,1)}, u32[]{:S(2)}, u32[]{:S(2)}) %collective-permute-start.15) | collective-permute-done | bytes 501792 | tf_op jit(solution)/shard_map/ppermute | solution.py:338
  40.5 2.1 %collective-permute-start.16 = (bf16[112,2240]{1,0:T(8,128)(2,1)}, bf16[112,2240]{1,0:T(8,128)(2,1)}, u32[]{:S(2)}, u32[]{:S(2)}) collective-permute-start(bf16[112,2240]{1,0:T(8,128)(2,1)} %collective-permute-done.15), channel_id=1, source_target_pairs={{4,0},{5,1},{6,2},{7,3},{8,12},{9,13},{10,14},{11,15},{20,16},{21,... | collective-permute-start | bytes 1505288 | tf_op jit(solution)/shard_map/ppermute | solution.py:338
  42.6 1.9 %collective-permute-start.22 = (bf16[112,2240]{1,0:T(8,128)(2,1)}, bf16[112,2240]{1,0:T(8,128)(2,1)}, u32[]{:S(2)}, u32[]{:S(2)}) collective-permute-start(bf16[112,2240]{1,0:T(8,128)(2,1)} %collective-permute-done.11.refs_3_), channel_id=1, source_target_pairs={{4,8},{5,9},{6,10},{7,11},{8,4},{9,5},{10,6},{11,7},{20,24},{21,25... | collective-permute-start | bytes 1505288 | tf_op jit(solution)/shard_map/ppermute | solution.py:338
  47.6 4.3 %collective-permute-done.5.s2 = bf16[560,128]{1,0:T(8,128)(2,1)S(1)} collective-permute-done((bf16[560,128]{1,0:T(8,128)(2,1)S(1)}, bf16[560,128]{1,0:T(8,128)(2,1)S(1)}, u32[]{:S(2)}, u32[]{:S(2)}) %collective-permute-start.5) | collective-permute-done | bytes 143392 | tf_op jit(solution)/shard_map/ppermute | solution.py:338
  59.4 2.3 %collective-permute-start.18 = (bf16[112,2240]{1,0:T(8,128)(2,1)}, bf16[112,2240]{1,0:T(8,128)(2,1)S(1)}, u32[]{:S(2)}, u32[]{:S(2)}) collective-permute-start(bf16[112,2240]{1,0:T(8,128)(2,1)} %collective-permute-done.17), channel_id=1, source_target_pairs={{4,0},{5,1},{6,2},{7,3},{8,12},{9,13},{10,14},{11,15},{20,16},{21,... | collective-permute-start | bytes 1505288 | tf_op jit(solution)/shard_map/ppermute | solution.py:338
  61.7 2.1 %collective-permute-done.22 = bf16[112,2240]{1,0:T(8,128)(2,1)} collective-permute-done((bf16[112,2240]{1,0:T(8,128)(2,1)}, bf16[112,2240]{1,0:T(8,128)(2,1)}, u32[]{:S(2)}, u32[]{:S(2)}) %collective-permute-start.22) | collective-permute-done | bytes 501792 | tf_op jit(solution)/shard_map/ppermute | solution.py:338
  65.1 1.9 %broadcast_select_fusion.2.refs_7_ = bf16[112,2240]{1,0:T(8,128)(2,1)} fusion(bf16[112,2240]{1,0:T(8,128)(2,1)} %collective-permute-done.16, bf16[112,2240]{1,0:T(8,128)(2,1)} %collective-permute-done.15, pred[]{:T(512)S(6)} %or.3), kind=kLoop, calls=%fused_computation.3 | loop fusion | flops 250880 | bytes 1505281 | tf_op jit(solution)/shard_map/jit(_where)/select_n | solution.py:380
  67.0 16.5 %collective-permute-done.23 = bf16[112,2240]{1,0:T(8,128)(2,1)S(1)} collective-permute-done((bf16[112,2240]{1,0:T(8,128)(2,1)}, bf16[112,2240]{1,0:T(8,128)(2,1)S(1)}, u32[]{:S(2)}, u32[]{:S(2)}) %collective-permute-start.23) | collective-permute-done | bytes 501792 | tf_op jit(solution)/shard_map/ppermute | solution.py:338
  90.4 9.5 %collective-permute-done.14.refs_6_ = bf16[112,2240]{1,0:T(8,128)(2,1)S(1)} collective-permute-done((bf16[112,2240]{1,0:T(8,128)(2,1)S(1)}, bf16[112,2240]{1,0:T(8,128)(2,1)S(1)}, u32[]{:S(2)}, u32[]{:S(2)}) %collective-permute-start.14) | collective-permute-done | bytes 501792 | tf_op jit(solution)/shard_map/ppermute | solution.py:338
  102.3 9.7 %collective-permute-done.25.refs_4_ = bf16[112,2240]{1,0:T(8,128)(2,1)} collective-permute-done((bf16[112,2240]{1,0:T(8,128)(2,1)}, bf16[112,2240]{1,0:T(8,128)(2,1)}, u32[]{:S(2)}, u32[]{:S(2)}) %collective-permute-start.25) | collective-permute-done | bytes 501792 | tf_op jit(solution)/shard_map/ppermute | solution.py:338
  118.2 3.3 %rim.2 = (bf16[360,512]{1,0:T(8,128)(2,1)S(1)}, bf16[3,360,2240]{2,1,0:T(8,128)(2,1)S(1)}) custom-call(s32[1]{0:T(128)} %bitcast.code, bf16[2240,256]{1,0:T(8,128)(2,1)S(1)} %attend.2.n_own, bf16[2240,256]{1,0:T(8,128)(2,1)S(1)} %collective-permute-done.7.n_other, bf16[216,2240]{1,0:T(8,128)(2,1)S(1)} %bitcast.18, ...), custom_call_target="tpu_custom_call" | custom-call | tf_op jit(solution)/shard_map/rim/pallas_call | solution.py:414
  121.5 3.2 %collective-permute-start.28 = (bf16[360,512]{1,0:T(8,128)(2,1)S(1)}, bf16[360,512]{1,0:T(8,128)(2,1)S(1)}, u32[]{:S(2)}, u32[]{:S(2)}) collective-permute-start(bf16[360,512]{1,0:T(8,128)(2,1)S(1)} %get-tuple-element.23), channel_id=1, source_target_pairs={{0,4},{1,5},{2,6},{3,7},{4,8},{5,9},{6,10},{7,11},{8,12},{9,13},{1... | collective-permute-start | bytes 1105928 | tf_op jit(solution)/shard_map/ppermute | solution.py:338
  124.8 4.1 %own.2 = (f32[360,384]{1,0:T(8,128)S(1)}, f32[360,384]{1,0:T(8,128)S(1)}) custom-call(bf16[2240,256]{1,0:T(8,128)(2,1)S(1)} %attend.2.n_own, bf16[2240,256]{1,0:T(8,128)(2,1)S(1)} %collective-permute-done.7.n_other, bf16[2240,128]{1,0:T(8,128)(2,1)} %attend.3.z_own, bf16[2240,128]{1,0:T(8,128)(2,1)} %collective-permute-done.8.z_other, ...), custom_call_target="tpu_custom_call" | custom-call | tf_op jit(solution)/shard_map/own/pallas_call | solution.py:427
  129.0 6.3 %collective-permute-done.26.refs_5_ = bf16[112,2240]{1,0:T(8,128)(2,1)} collective-permute-done((bf16[112,2240]{1,0:T(8,128)(2,1)}, bf16[112,2240]{1,0:T(8,128)(2,1)}, u32[]{:S(2)}, u32[]{:S(2)}) %collective-permute-start.26) | collective-permute-done | bytes 501792 | tf_op jit(solution)/shard_map/ppermute | solution.py:338
  135.3 3.0 %rim.3 = (bf16[216,512]{1,0:T(8,128)(2,1)S(1)}, bf16[3,216,2240]{2,1,0:T(8,128)(2,1)S(1)}) custom-call(s32[1]{0:T(128)} %bitcast.code, bf16[2240,256]{1,0:T(8,128)(2,1)S(1)} %attend.2.n_own, bf16[2240,256]{1,0:T(8,128)(2,1)S(1)} %collective-permute-done.7.n_other, bf16[112,2240]{1,0:T(8,128)(2,1)} %collective-permute-done.20.refs_0_, ...), custom_call_target="tpu_custom_call" | custom-call | tf_op jit(solution)/shard_map/rim/pallas_call | solution.py:414
  138.3 3.2 %collective-permute-start.30 = (bf16[216,512]{1,0:T(8,128)(2,1)S(1)}, bf16[216,512]{1,0:T(8,128)(2,1)S(1)}, u32[]{:S(2)}, u32[]{:S(2)}) collective-permute-start(bf16[216,512]{1,0:T(8,128)(2,1)S(1)} %get-tuple-element.24), channel_id=1, source_target_pairs={{0,4},{1,5},{2,6},{3,7},{4,8},{5,9},{6,10},{7,11},{8,12},{9,13},{1... | collective-permute-start | bytes 663560 | tf_op jit(solution)/shard_map/ppermute | solution.py:338
  141.6 3.1 %own.3 = (f32[216,384]{1,0:T(8,128)S(1)}, f32[216,384]{1,0:T(8,128)S(1)}) custom-call(bf16[2240,256]{1,0:T(8,128)(2,1)S(1)} %attend.2.n_own, bf16[2240,256]{1,0:T(8,128)(2,1)S(1)} %collective-permute-done.7.n_other, bf16[2240,128]{1,0:T(8,128)(2,1)} %attend.3.z_own, bf16[2240,128]{1,0:T(8,128)(2,1)} %collective-permute-done.8.z_other, ...), custom_call_target="tpu_custom_call" | custom-call | tf_op jit(solution)/shard_map/own/pallas_call | solution.py:427
  (81 shorter events, 39.3 us)
Async XLA Ops:
  15.0 8.0 %collective-permute-start.2 = (bf16[560,128]{1,0:T(8,128)(2,1)S(1)}, bf16[560,128]{1,0:T(8,128)(2,1)S(1)}, u32[]{:S(2)}, u32[]{:S(2)}) collective-permute-start(bf16[560,128]{1,0:T(8,128)(2,1)S(1)} %add_convert_fusion.3), channel_id=1, source_target_pairs={{0,4},{1,5},{2,6},{3,7},{4,8},{5,9},{6,10},{7,11},{8,12},{9,13},{1... | collective-permute-start | bytes 430088 | tf_op jit(solution)/shard_map/ppermute | solution.py:338
  20.5 20.0 %collective-permute-start.15 = (bf16[112,2240]{1,0:T(8,128)(2,1)}, bf16[112,2240]{1,0:T(8,128)(2,1)}, u32[]{:S(2)}, u32[]{:S(2)}) collective-permute-start(bf16[112,2240]{1,0:T(8,128)(2,1)} %half_of.2), channel_id=1, source_target_pairs={{4,8},{5,9},{6,10},{7,11},{8,4},{9,5},{10,6},{11,7},{20,24},{21,25... | collective-permute-start | bytes 1505288 | tf_op jit(solution)/shard_map/ppermute | solution.py:338
  23.0 19.6 %collective-permute-start.11 = (bf16[112,2240]{1,0:T(8,128)(2,1)}, bf16[112,2240]{1,0:T(8,128)(2,1)}, u32[]{:S(2)}, u32[]{:S(2)}) collective-permute-start(bf16[112,2240]{1,0:T(8,128)(2,1)} %half_of.2), channel_id=1, source_target_pairs={{0,4},{1,5},{2,6},{3,7},{4,0},{5,1},{6,2},{7,3},{8,12},{9,13},{10,... | collective-permute-start | bytes 1505288 | tf_op jit(solution)/shard_map/ppermute | solution.py:338
  23.1 21.4 %collective-permute-start.3 = (bf16[560,128]{1,0:T(8,128)(2,1)S(1)}, bf16[560,128]{1,0:T(8,128)(2,1)S(1)}, u32[]{:S(2)}, u32[]{:S(2)}) collective-permute-start(bf16[560,128]{1,0:T(8,128)(2,1)S(1)} %add_convert_fusion.2), channel_id=1, source_target_pairs={{0,8},{1,9},{2,10},{3,11},{4,12},{5,13},{6,14},{7,15},{16,24},{17,... | collective-permute-start | bytes 430088 | tf_op jit(solution)/shard_map/ppermute | solution.py:338
  24.4 31.9 %collective-permute-start.9 = (bf16[112,2240]{1,0:T(8,128)(2,1)}, bf16[112,2240]{1,0:T(8,128)(2,1)}, u32[]{:S(2)}, u32[]{:S(2)}) collective-permute-start(bf16[112,2240]{1,0:T(8,128)(2,1)} %half_of.2), channel_id=1, source_target_pairs={{0,2},{1,3},{2,0},{3,1},{4,6},{5,7},{6,4},{7,5},{8,10},{9,11},{10,... | collective-permute-start | bytes 1505288 | tf_op jit(solution)/shard_map/ppermute | solution.py:338
  28.0 29.9 %collective-permute-start.17 = (bf16[112,2240]{1,0:T(8,128)(2,1)}, bf16[112,2240]{1,0:T(8,128)(2,1)}, u32[]{:S(2)}, u32[]{:S(2)}) collective-permute-start(bf16[112,2240]{1,0:T(8,128)(2,1)} %half_of.3), channel_id=1, source_target_pairs={{4,8},{5,9},{6,10},{7,11},{8,4},{9,5},{10,6},{11,7},{20,24},{21,25... | collective-permute-start | bytes 1505288 | tf_op jit(solution)/shard_map/ppermute | solution.py:338
  40.5 18.8 %collective-permute-start.16 = (bf16[112,2240]{1,0:T(8,128)(2,1)}, bf16[112,2240]{1,0:T(8,128)(2,1)}, u32[]{:S(2)}, u32[]{:S(2)}) collective-permute-start(bf16[112,2240]{1,0:T(8,128)(2,1)} %collective-permute-done.15), channel_id=1, source_target_pairs={{4,0},{5,1},{6,2},{7,3},{8,12},{9,13},{10,14},{11,15},{20,16},{21,... | collective-permute-start | bytes 1505288 | tf_op jit(solution)/shard_map/ppermute | solution.py:338
  42.6 21.1 %collective-permute-start.22 = (bf16[112,2240]{1,0:T(8,128)(2,1)}, bf16[112,2240]{1,0:T(8,128)(2,1)}, u32[]{:S(2)}, u32[]{:S(2)}) collective-permute-start(bf16[112,2240]{1,0:T(8,128)(2,1)} %collective-permute-done.11.refs_3_), channel_id=1, source_target_pairs={{4,8},{5,9},{6,10},{7,11},{8,4},{9,5},{10,6},{11,7},{20,24},{21,25... | collective-permute-start | bytes 1505288 | tf_op jit(solution)/shard_map/ppermute | solution.py:338
  53.2 32.7 %collective-permute-start.12 = (bf16[112,2240]{1,0:T(8,128)(2,1)}, bf16[112,2240]{1,0:T(8,128)(2,1)S(1)}, u32[]{:S(2)}, u32[]{:S(2)}) collective-permute-start(bf16[112,2240]{1,0:T(8,128)(2,1)} %collective-permute-done.11.refs_3_), channel_id=1, source_target_pairs={{0,16},{1,17},{2,18},{3,19},{4,20},{5,21},{6,22},{7,23},{8,24},{9,... | collective-permute-start | bytes 1505288 | tf_op jit(solution)/shard_map/ppermute | solution.py:338
  56.3 30.1 %collective-permute-start.13 = (bf16[112,2240]{1,0:T(8,128)(2,1)}, bf16[112,2240]{1,0:T(8,128)(2,1)S(1)}, u32[]{:S(2)}, u32[]{:S(2)}) collective-permute-start(bf16[112,2240]{1,0:T(8,128)(2,1)} %collective-permute-done.11.refs_3_), channel_id=1, source_target_pairs={{0,2},{1,3},{2,0},{3,1},{4,6},{5,7},{6,4},{7,5},{8,10},{9,11},{10,... | collective-permute-start | bytes 1505288 | tf_op jit(solution)/shard_map/ppermute | solution.py:338
  57.9 27.5 %collective-permute-start.10 = (bf16[112,2240]{1,0:T(8,128)(2,1)}, bf16[112,2240]{1,0:T(8,128)(2,1)S(1)}, u32[]{:S(2)}, u32[]{:S(2)}) collective-permute-start(bf16[112,2240]{1,0:T(8,128)(2,1)} %collective-permute-done.9.refs_1_), channel_id=1, source_target_pairs={{0,16},{1,17},{2,18},{3,19},{4,20},{5,21},{6,22},{7,23},{8,24},{9,... | collective-permute-start | bytes 1505288 | tf_op jit(solution)/shard_map/ppermute | solution.py:338
  59.4 27.6 %collective-permute-start.18 = (bf16[112,2240]{1,0:T(8,128)(2,1)}, bf16[112,2240]{1,0:T(8,128)(2,1)S(1)}, u32[]{:S(2)}, u32[]{:S(2)}) collective-permute-start(bf16[112,2240]{1,0:T(8,128)(2,1)} %collective-permute-done.17), channel_id=1, source_target_pairs={{4,0},{5,1},{6,2},{7,3},{8,12},{9,13},{10,14},{11,15},{20,16},{21,... | collective-permute-start | bytes 1505288 | tf_op jit(solution)/shard_map/ppermute | solution.py:338
  63.8 19.7 %collective-permute-start.23 = (bf16[112,2240]{1,0:T(8,128)(2,1)}, bf16[112,2240]{1,0:T(8,128)(2,1)S(1)}, u32[]{:S(2)}, u32[]{:S(2)}) collective-permute-start(bf16[112,2240]{1,0:T(8,128)(2,1)} %collective-permute-done.22), channel_id=1, source_target_pairs={{4,0},{5,1},{6,2},{7,3},{8,12},{9,13},{10,14},{11,15},{20,16},{21,... | collective-permute-start | bytes 1505288 | tf_op jit(solution)/shard_map/ppermute | solution.py:338
  83.5 29.0 %collective-permute-start.7 = (bf16[2240,256]{1,0:T(8,128)(2,1)S(1)}, bf16[2240,256]{1,0:T(8,128)(2,1)S(1)}, u32[]{:S(2)}, u32[]{:S(2)}) collective-permute-start(bf16[2240,256]{1,0:T(8,128)(2,1)S(1)} %attend.2.n_own), channel_id=1, source_target_pairs={{0,1},{1,0},{2,3},{3,2},{4,5},{5,4},{6,7},{7,6},{8,9},{9,8},{10,11... | collective-permute-start | bytes 3440648 | tf_op jit(solution)/shard_map/ppermute | solution.py:338
  85.4 36.1 %collective-permute-start.8 = (bf16[2240,128]{1,0:T(8,128)(2,1)}, bf16[2240,128]{1,0:T(8,128)(2,1)}, u32[]{:S(2)}, u32[]{:S(2)}) collective-permute-start(bf16[2240,128]{1,0:T(8,128)(2,1)} %attend.3.z_own), channel_id=1, source_target_pairs={{0,1},{1,0},{2,3},{3,2},{4,5},{5,4},{6,7},{7,6},{8,9},{9,8},{10,11... | collective-permute-start | bytes 1720328 | tf_op jit(solution)/shard_map/ppermute | solution.py:338
  85.9 42.9 %collective-permute-start.20 = (bf16[112,2240]{1,0:T(8,128)(2,1)}, bf16[112,2240]{1,0:T(8,128)(2,1)}, u32[]{:S(2)}, u32[]{:S(2)}) collective-permute-start(bf16[112,2240]{1,0:T(8,128)(2,1)} %broadcast_select_fusion.2.refs_7_), channel_id=1, source_target_pairs={{0,2},{1,3},{2,0},{3,1},{4,6},{5,7},{6,4},{7,5},{8,10},{9,11},{10,... | collective-permute-start | bytes 1505288 | tf_op jit(solution)/shard_map/ppermute | solution.py:338
  86.4 13.5 %collective-permute-start.14 = (bf16[112,2240]{1,0:T(8,128)(2,1)S(1)}, bf16[112,2240]{1,0:T(8,128)(2,1)S(1)}, u32[]{:S(2)}, u32[]{:S(2)}) collective-permute-start(bf16[112,2240]{1,0:T(8,128)(2,1)S(1)} %collective-permute-done.13.refs_5_), channel_id=1, source_target_pairs={{0,16},{1,17},{2,18},{3,19},{4,20},{5,21},{6,22},{7,23},{8,24},{9,... | collective-permute-start | bytes 1505288 | tf_op jit(solution)/shard_map/ppermute | solution.py:338
  87.0 24.9 %collective-permute-start.25 = (bf16[112,2240]{1,0:T(8,128)(2,1)}, bf16[112,2240]{1,0:T(8,128)(2,1)}, u32[]{:S(2)}, u32[]{:S(2)}) collective-permute-start(bf16[112,2240]{1,0:T(8,128)(2,1)} %broadcast_select_fusion.refs_2_), channel_id=1, source_target_pairs={{0,2},{1,3},{2,0},{3,1},{4,6},{5,7},{6,4},{7,5},{8,10},{9,11},{10,... | collective-permute-start | bytes 1505288 | tf_op jit(solution)/shard_map/ppermute | solution.py:338
  100.7 28.2 %collective-permute-start.21 = (bf16[112,2240]{1,0:T(8,128)(2,1)}, bf16[112,2240]{1,0:T(8,128)(2,1)}, u32[]{:S(2)}, u32[]{:S(2)}) collective-permute-start(bf16[112,2240]{1,0:T(8,128)(2,1)} %broadcast_select_fusion.1.refs_8_), channel_id=1, source_target_pairs={{0,2},{1,3},{2,0},{3,1},{4,6},{5,7},{6,4},{7,5},{8,10},{9,11},{10,... | collective-permute-start | bytes 1505288 | tf_op jit(solution)/shard_map/ppermute | solution.py:338
  111.9 17.0 %collective-permute-start.24 = (bf16[112,2240]{1,0:T(8,128)(2,1)}, bf16[112,2240]{1,0:T(8,128)(2,1)}, u32[]{:S(2)}, u32[]{:S(2)}) collective-permute-start(bf16[112,2240]{1,0:T(8,128)(2,1)} %broadcast_select_fusion.refs_2_), channel_id=1, source_target_pairs={{0,16},{1,17},{2,18},{3,19},{4,20},{5,21},{6,22},{7,23},{8,24},{9,... | collective-permute-start | bytes 1505288 | tf_op jit(solution)/shard_map/ppermute | solution.py:338
  112.5 22.8 %collective-permute-start.26 = (bf16[112,2240]{1,0:T(8,128)(2,1)}, bf16[112,2240]{1,0:T(8,128)(2,1)}, u32[]{:S(2)}, u32[]{:S(2)}) collective-permute-start(bf16[112,2240]{1,0:T(8,128)(2,1)} %collective-permute-done.25.refs_4_), channel_id=1, source_target_pairs={{0,16},{1,17},{2,18},{3,19},{4,20},{5,21},{6,22},{7,23},{8,24},{9,... | collective-permute-start | bytes 1505288 | tf_op jit(solution)/shard_map/ppermute | solution.py:338
  121.5 20.0 %collective-permute-start.28 = (bf16[360,512]{1,0:T(8,128)(2,1)S(1)}, bf16[360,512]{1,0:T(8,128)(2,1)S(1)}, u32[]{:S(2)}, u32[]{:S(2)}) collective-permute-start(bf16[360,512]{1,0:T(8,128)(2,1)S(1)} %get-tuple-element.23), channel_id=1, source_target_pairs={{0,4},{1,5},{2,6},{3,7},{4,8},{5,9},{6,10},{7,11},{8,12},{9,13},{1... | collective-permute-start | bytes 1105928 | tf_op jit(solution)/shard_map/ppermute | solution.py:338
  128.9 17.3 %collective-permute-start.19 = (f32[360,384]{1,0:T(8,128)S(1)}, f32[360,384]{1,0:T(8,128)S(1)}, u32[]{:S(2)}, u32[]{:S(2)}) collective-permute-start(f32[360,384]{1,0:T(8,128)S(1)} %get-tuple-element.19), channel_id=1, source_target_pairs={{0,1},{1,0},{2,3},{3,2},{4,5},{5,4},{6,7},{7,6},{8,9},{9,8},{10,11... | collective-permute-start | bytes 1658888 | tf_op jit(solution)/shard_map/ppermute | solution.py:338
  138.3 7.8 %collective-permute-start.30 = (bf16[216,512]{1,0:T(8,128)(2,1)S(1)}, bf16[216,512]{1,0:T(8,128)(2,1)S(1)}, u32[]{:S(2)}, u32[]{:S(2)}) collective-permute-start(bf16[216,512]{1,0:T(8,128)(2,1)S(1)} %get-tuple-element.24), channel_id=1, source_target_pairs={{0,4},{1,5},{2,6},{3,7},{4,8},{5,9},{6,10},{7,11},{8,12},{9,13},{1... | collective-permute-start | bytes 663560 | tf_op jit(solution)/shard_map/ppermute | solution.py:338
  (19 other events, 225.0 us)

commit v4 on v3

--- a/solution.py
+++ b/solution.py
@@ -117,6 +117,27 @@
         compiler_params=limit(4),
         name="half_of",
     )(x, hbm(whole))
+
+
+def pick_kernel(flag, a, b, out):
+    @pl.when(flag[0] == 1)
+    def _():
+        out[...] = a[...]
+
+    @pl.when(flag[0] == 0)
+    def _():
+        out[...] = b[...]
+
+
+def pick(flag, a, b):
+    return pl.pallas_call(
+        pick_kernel,
+        in_specs=[SMEM, VMEM, VMEM],
+        out_specs=VMEM,
+        out_shape=pltpu.VMEM(a.shape, a.dtype),
+        compiler_params=limit(4),
+        name="pick",
+    )(flag, a, b)
 
 
 def state_kernel(mine, k_ref, v_ref, *outs):
@@ -250,8 +271,8 @@
     nearer = jnp.where(low, TB // 2, TB // 2 - 1)
     farther = jnp.where(low, TB - 1, 0)
     if part == 0:
-        return [(z, y), (z, 1 - y), (near, y), (near, 1 - y), (nearer, y)]
-    return [(nearer, 1 - y), (farther, y), (farther, 1 - y)]
+        return [(z, y), (z, 1 - y), (near, y), (near, 1 - y), (nearer, y), (farther, y)]
+    return [(nearer, 1 - y), (farther, 1 - y)]
 
 
 def both_cores(own, other, at):
@@ -335,7 +356,8 @@
                 to = where(g, d)
                 if to is not None:
                     route.append((g * devices + d, to[0] * devices + to[1]))
-        return lax.ppermute(block, axes, route)
+        moved = lax.ppermute(block, axes, route)
+        return vm(moved) if block.shape[1] == width else moved
 
     def to_core(g, d):
         return g, d ^ 1
@@ -376,18 +398,28 @@
     zp5 = send(zp3, along(z1=0, z2=3))
     zr2 = send(rest, along(z1=2, z2=1))
     zr4 = send(zr2, along(z1=0, z2=3))
-    outer = (z == 0) | (z == TB - 1)
-    slot_b = jnp.where(outer, zp4, zp2)
-    rest_b = jnp.where(outer, zr4, zr2)
-    slot_c = jnp.where(outer, zp5, zp3)
+    outer = ((z == 0) | (z == TB - 1)).astype(jnp.int32).reshape(1)
+    slot_b = pick(outer, zp4, zp2)
+    rest_b = pick(outer, zr4, zr2)
+    slot_c = pick(outer, zp5, zp3)
     y0 = send(piece, to_y)
     ya = send(zp1, to_y)
     yb = send(slot_b, to_y)
     yc = send(slot_c, to_y)
     early_pieces = [
-        whole, y0, send(y0, to_x), zp1, send(zp1, to_x), ya, send(ya, to_x), slot_b, rest_b
+        whole,
+        y0,
+        send(y0, to_x),
+        zp1,
+        send(zp1, to_x),
+        ya,
+        send(ya, to_x),
+        slot_b,
+        rest_b,
+        slot_c,
+        send(slot_c, to_x),
     ]
-    late_pieces = [yb, send(rest_b, to_y), slot_c, send(slot_c, to_x), yc, send(yc, to_x)]
+    late_pieces = [yb, send(rest_b, to_y), yc, send(yc, to_x)]
 
     quarter = width // 4
     kept, given = local_state(mine, k, v)
@@ -421,7 +453,7 @@
             ],
             compiler_params=limit(16),
             name="rim",
-        )(code, late, late_other, *[p if p is whole else vm(p) for p in pieces])
+        )(code, late, late_other, *pieces)
         rim = send(rim, up(1))
         rims += [rim, send(rim, to_core)]
         keep, give = pl.pallas_call(

time: 152 us -> 152 us (level)
  the two profiles are of different devices: /device:TPU:18 before, /device:TPU:0 now
where the time goes in v4:
time: 152 us; the launch traced here: 151 us
  waiting for transfers between devices  65 us (43%)
  starting transfers between devices  46.6 us (31%)
  Pallas kernels  28.5 us (19%)
  local copies, waits for them, and re-layouts  9.15 us (6%)
    ppermute x32, waiting for transfers between devices, send(): moved = lax.ppermute(block, axes, route)  65 us
    ppermute x32, starting transfers between devices, send(): moved = lax.ppermute(block, axes, route)  46.6 us
    unnamed x40, local copies, waits for them, and re-layouts  8.79 us
    pallas_call x2, Pallas kernels, tuned(): pl.pallas_call(own_kernel, in_specs=[VMEM] * 5, out_specs=[VMEM] * 2, out...  7.05 us
    pallas_call x1, Pallas kernels, local_state(): pl.pallas_call(state_kernel, grid_spec=pltpu.PrefetchScalarGridSpec(num_s...  6.29 us
    pallas_call x2, Pallas kernels, tuned(): pl.pallas_call(functools.partial(rim_kernel, cols, half, 'ab'.index(name)...  5.8 us
    pallas_call x3, Pallas kernels, pick(): pl.pallas_call(pick_kernel, in_specs=[SMEM, VMEM, VMEM], out_specs=VMEM,...  3.39 us
  transfers between devices with their start and end apart: 32, of which 16 were waited for; matrix products, arithmetic and copies ran while one was open for 0% of the time, Pallas kernels for 14%

profile of v4, /device:TPU:0, one launch (start us, length us, event | category | flops | bytes accessed | tf_op | source)
XLA Modules:
  0.0 150.8 jit_solution(6970057444565068331)
XLA Ops:
  0.0 6.3 %local_state.1 = (bf16[1120,128]{1,0:T(8,128)(2,1)}, bf16[1120,128]{1,0:T(8,128)(2,1)}) custom-call(s32[1]{0:T(128)} %bitcast.1.mine, bf16[3,2240,128]{2,1,0:T(8,128)(2,1)} %bitcast.22, bf16[3,2240,128]{2,1,0:T(8,128)(2,1)} %bitcast.23), custom_call_target="tpu_custom_call" | custom-call | tf_op jit(solution)/shard_map/local_state/pallas_call | solution.py:171
  9.3 2.9 %collective-permute-start.1 = (bf16[560,128]{1,0:T(8,128)(2,1)S(1)}, bf16[560,128]{1,0:T(8,128)(2,1)S(1)}, u32[]{:S(2)}, u32[]{:S(2)}) collective-permute-start(bf16[560,128]{1,0:T(8,128)(2,1)S(1)} %slice.9), channel_id=1, source_target_pairs={{0,2},{1,3},{2,0},{3,1},{4,6},{5,7},{6,4},{7,5},{8,10},{9,11},{10,... | collective-permute-start | bytes 430088 | tf_op jit(solution)/shard_map/ppermute | solution.py:359
  13.3 1.6 %collective-permute-start.11 = (bf16[112,2240]{1,0:T(8,128)(2,1)S(1)}, bf16[112,2240]{1,0:T(8,128)(2,1)}, u32[]{:S(2)}, u32[]{:S(2)}) collective-permute-start(bf16[112,2240]{1,0:T(8,128)(2,1)S(1)} %half_of.2), channel_id=1, source_target_pairs={{0,4},{1,5},{2,6},{3,7},{4,0},{5,1},{6,2},{7,3},{8,12},{9,13},{10,... | collective-permute-start | bytes 1505288 | tf_op jit(solution)/shard_map/ppermute | solution.py:359
  16.3 3.8 %collective-permute-start.2 = (bf16[560,128]{1,0:T(8,128)(2,1)S(1)}, bf16[560,128]{1,0:T(8,128)(2,1)S(1)}, u32[]{:S(2)}, u32[]{:S(2)}) collective-permute-start(bf16[560,128]{1,0:T(8,128)(2,1)S(1)} %add_convert_fusion.3), channel_id=1, source_target_pairs={{0,4},{1,5},{2,6},{3,7},{4,8},{5,9},{6,10},{7,11},{8,12},{9,13},{1... | collective-permute-start | bytes 430088 | tf_op jit(solution)/shard_map/ppermute | solution.py:359
  20.2 8.9 %collective-permute-done.2 = bf16[560,128]{1,0:T(8,128)(2,1)S(1)} collective-permute-done((bf16[560,128]{1,0:T(8,128)(2,1)S(1)}, bf16[560,128]{1,0:T(8,128)(2,1)S(1)}, u32[]{:S(2)}, u32[]{:S(2)}) %collective-permute-start.2) | collective-permute-done | bytes 143392 | tf_op jit(solution)/shard_map/ppermute | solution.py:359
  29.1 4.5 %collective-permute-start.3 = (bf16[560,128]{1,0:T(8,128)(2,1)S(1)}, bf16[560,128]{1,0:T(8,128)(2,1)S(1)}, u32[]{:S(2)}, u32[]{:S(2)}) collective-permute-start(bf16[560,128]{1,0:T(8,128)(2,1)S(1)} %add_convert_fusion.2), channel_id=1, source_target_pairs={{0,8},{1,9},{2,10},{3,11},{4,12},{5,13},{6,14},{7,15},{16,24},{17,... | collective-permute-start | bytes 430088 | tf_op jit(solution)/shard_map/ppermute | solution.py:359
  40.4 5.6 %collective-permute-done.9.refs_1_ = bf16[112,2240]{1,0:T(8,128)(2,1)S(1)} collective-permute-done((bf16[112,2240]{1,0:T(8,128)(2,1)S(1)}, bf16[112,2240]{1,0:T(8,128)(2,1)S(1)}, u32[]{:S(2)}, u32[]{:S(2)}) %collective-permute-start.9) | collective-permute-done | bytes 501792 | tf_op jit(solution)/shard_map/ppermute | solution.py:359
  46.6 1.5 collective-permute-start.10
  49.4 1.8 %collective-permute-done.5.s2 = bf16[560,128]{1,0:T(8,128)(2,1)S(1)} collective-permute-done((bf16[560,128]{1,0:T(8,128)(2,1)S(1)}, bf16[560,128]{1,0:T(8,128)(2,1)S(1)}, u32[]{:S(2)}, u32[]{:S(2)}) %collective-permute-start.5) | collective-permute-done | bytes 143392 | tf_op jit(solution)/shard_map/ppermute | solution.py:359
  56.0 2.2 %collective-permute-done.10.refs_2_ = bf16[112,2240]{1,0:T(8,128)(2,1)S(1)} collective-permute-done((bf16[112,2240]{1,0:T(8,128)(2,1)S(1)}, bf16[112,2240]{1,0:T(8,128)(2,1)S(1)}, u32[]{:S(2)}, u32[]{:S(2)}) %collective-permute-start.10) | collective-permute-done | bytes 501792 | tf_op jit(solution)/shard_map/ppermute | solution.py:359
  60.3 4.0 %collective-permute-done.20.a = bf16[112,2240]{1,0:T(8,128)(2,1)S(1)} collective-permute-done((bf16[112,2240]{1,0:T(8,128)(2,1)S(1)}, bf16[112,2240]{1,0:T(8,128)(2,1)S(1)}, u32[]{:S(2)}, u32[]{:S(2)}) %collective-permute-start.20) | collective-permute-done | bytes 501792 | tf_op jit(solution)/shard_map/ppermute | solution.py:359
  69.4 1.5 collective-permute-start.14
  71.4 18.6 %collective-permute-done.16.a = bf16[112,2240]{1,0:T(8,128)(2,1)} collective-permute-done((bf16[112,2240]{1,0:T(8,128)(2,1)}, bf16[112,2240]{1,0:T(8,128)(2,1)}, u32[]{:S(2)}, u32[]{:S(2)}) %collective-permute-start.16) | collective-permute-done | bytes 501792 | tf_op jit(solution)/shard_map/ppermute | solution.py:359
  97.5 2.2 %collective-permute-done.18.a = bf16[112,2240]{1,0:T(8,128)(2,1)} collective-permute-done((bf16[112,2240]{1,0:T(8,128)(2,1)}, bf16[112,2240]{1,0:T(8,128)(2,1)}, u32[]{:S(2)}, u32[]{:S(2)}) %collective-permute-start.18) | collective-permute-done | bytes 501792 | tf_op jit(solution)/shard_map/ppermute | solution.py:359
  102.4 3.9 %rim.2 = (bf16[432,512]{1,0:T(8,128)(2,1)S(1)}, bf16[3,432,2240]{2,1,0:T(8,128)(2,1)S(1)}) custom-call(s32[1]{0:T(128)} %bitcast.code, bf16[2240,256]{1,0:T(8,128)(2,1)S(1)} %attend.2.n_own, bf16[2240,256]{1,0:T(8,128)(2,1)S(1)} %collective-permute-done.7.n_other, bf16[216,2240]{1,0:T(8,128)(2,1)S(1)} %bitcast.19, bf16[112,2240]{1,0:T(8,128)(2,1)S(1)} %copy-done.12, ...), custom_call_target="tpu_custom_call" | custom-call | tf_op jit(solution)/shard_map/rim/pallas_call | solution.py:446
  106.3 8.8 %collective-permute-start.28 = (bf16[432,512]{1,0:T(8,128)(2,1)S(1)}, bf16[432,512]{1,0:T(8,128)(2,1)S(1)}, u32[]{:S(2)}, u32[]{:S(2)}) collective-permute-start(bf16[432,512]{1,0:T(8,128)(2,1)S(1)} %get-tuple-element.23), channel_id=1, source_target_pairs={{0,4},{1,5},{2,6},{3,7},{4,8},{5,9},{6,10},{7,11},{8,12},{9,13},{1... | collective-permute-start | bytes 1327112 | tf_op jit(solution)/shard_map/ppermute | solution.py:359
  115.6 1.6 %collective-permute-start.24 = (bf16[112,2240]{1,0:T(8,128)(2,1)S(1)}, bf16[112,2240]{1,0:T(8,128)(2,1)S(1)}, u32[]{:S(2)}, u32[]{:S(2)}) collective-permute-start(bf16[112,2240]{1,0:T(8,128)(2,1)S(1)} %pick.4.refs_8_), channel_id=1, source_target_pairs={{0,2},{1,3},{2,0},{3,1},{4,6},{5,7},{6,4},{7,5},{8,10},{9,11},{10,... | collective-permute-start | bytes 1505288 | tf_op jit(solution)/shard_map/ppermute | solution.py:359
  118.7 4.5 %own.2 = (f32[432,384]{1,0:T(8,128)S(1)}, f32[432,384]{1,0:T(8,128)S(1)}) custom-call(bf16[2240,256]{1,0:T(8,128)(2,1)S(1)} %attend.2.n_own, bf16[2240,256]{1,0:T(8,128)(2,1)S(1)} %collective-permute-done.7.n_other, bf16[2240,128]{1,0:T(8,128)(2,1)} %attend.3.z_own, bf16[2240,128]{1,0:T(8,128)(2,1)} %collective-permute-done.8.z_other, ...), custom_call_target="tpu_custom_call" | custom-call | tf_op jit(solution)/shard_map/own/pallas_call | solution.py:459
  123.9 6.0 %collective-permute-done.23.refs_0_ = bf16[112,2240]{1,0:T(8,128)(2,1)S(1)} collective-permute-done((bf16[112,2240]{1,0:T(8,128)(2,1)S(1)}, bf16[112,2240]{1,0:T(8,128)(2,1)S(1)}, u32[]{:S(2)}, u32[]{:S(2)}) %collective-permute-start.23) | collective-permute-done | bytes 501792 | tf_op jit(solution)/shard_map/ppermute | solution.py:359
  129.8 8.7 %collective-permute-done.24.refs_1_ = bf16[112,2240]{1,0:T(8,128)(2,1)S(1)} collective-permute-done((bf16[112,2240]{1,0:T(8,128)(2,1)S(1)}, bf16[112,2240]{1,0:T(8,128)(2,1)S(1)}, u32[]{:S(2)}, u32[]{:S(2)}) %collective-permute-start.24) | collective-permute-done | bytes 501792 | tf_op jit(solution)/shard_map/ppermute | solution.py:359
  138.6 1.9 %rim.3 = (bf16[144,512]{1,0:T(8,128)(2,1)S(1)}, bf16[3,144,2240]{2,1,0:T(8,128)(2,1)S(1)}) custom-call(s32[1]{0:T(128)} %bitcast.code, bf16[2240,256]{1,0:T(8,128)(2,1)S(1)} %attend.2.n_own, bf16[2240,256]{1,0:T(8,128)(2,1)S(1)} %collective-permute-done.7.n_other, bf16[112,2240]{1,0:T(8,128)(2,1)S(1)} %collective-permute-done.23.refs_0_, ...), custom_call_target="tpu_custom_call" | custom-call | tf_op jit(solution)/shard_map/rim/pallas_call | solution.py:446
  140.5 4.5 %collective-permute-start.30 = (bf16[144,512]{1,0:T(8,128)(2,1)S(1)}, bf16[144,512]{1,0:T(8,128)(2,1)S(1)}, u32[]{:S(2)}, u32[]{:S(2)}) collective-permute-start(bf16[144,512]{1,0:T(8,128)(2,1)S(1)} %get-tuple-element.24), channel_id=1, source_target_pairs={{0,4},{1,5},{2,6},{3,7},{4,8},{5,9},{6,10},{7,11},{8,12},{9,13},{1... | collective-permute-start | bytes 442376 | tf_op jit(solution)/shard_map/ppermute | solution.py:359
  145.0 2.5 %own.3 = (f32[144,384]{1,0:T(8,128)S(1)}, f32[144,384]{1,0:T(8,128)S(1)}) custom-call(bf16[2240,256]{1,0:T(8,128)(2,1)S(1)} %attend.2.n_own, bf16[2240,256]{1,0:T(8,128)(2,1)S(1)} %collective-permute-done.7.n_other, bf16[2240,128]{1,0:T(8,128)(2,1)} %attend.3.z_own, bf16[2240,128]{1,0:T(8,128)(2,1)} %collective-permute-done.8.z_other, ...), custom_call_target="tpu_custom_call" | custom-call | tf_op jit(solution)/shard_map/own/pallas_call | solution.py:459
  149.2 1.5 %out.1 = bf16[3,128,1152]{2,1,0:T(8,128)(2,1)} custom-call(s32[1]{0:T(128)} %bitcast.code, f32[432,384]{1,0:T(8,128)S(1)} %get-tuple-element.18.refs_0_, f32[432,384]{1,0:T(8,128)S(1)} %collective-permute-done.22.refs_1_, f32[144,384]{1,0:T(8,128)S(1)} %get-tuple-element.21.refs_2_, f32[144,384]{1,0:T(8,128)S(1)} %collective-permute-done.27.refs_3_, ...), custom_call_target="tpu_custom_call" | custom-call | tf_op jit(solution)/shard_map/out/pallas_call | solution.py:469
  (99 shorter events, 40.7 us)
Async XLA Ops:
  13.3 20.9 %collective-permute-start.11 = (bf16[112,2240]{1,0:T(8,128)(2,1)S(1)}, bf16[112,2240]{1,0:T(8,128)(2,1)}, u32[]{:S(2)}, u32[]{:S(2)}) collective-permute-start(bf16[112,2240]{1,0:T(8,128)(2,1)S(1)} %half_of.2), channel_id=1, source_target_pairs={{0,4},{1,5},{2,6},{3,7},{4,0},{5,1},{6,2},{7,3},{8,12},{9,13},{10,... | collective-permute-start | bytes 1505288 | tf_op jit(solution)/shard_map/ppermute | solution.py:359
  16.3 12.8 %collective-permute-start.2 = (bf16[560,128]{1,0:T(8,128)(2,1)S(1)}, bf16[560,128]{1,0:T(8,128)(2,1)S(1)}, u32[]{:S(2)}, u32[]{:S(2)}) collective-permute-start(bf16[560,128]{1,0:T(8,128)(2,1)S(1)} %add_convert_fusion.3), channel_id=1, source_target_pairs={{0,4},{1,5},{2,6},{3,7},{4,8},{5,9},{6,10},{7,11},{8,12},{9,13},{1... | collective-permute-start | bytes 430088 | tf_op jit(solution)/shard_map/ppermute | solution.py:359
  33.6 12.4 %collective-permute-start.9 = (bf16[112,2240]{1,0:T(8,128)(2,1)S(1)}, bf16[112,2240]{1,0:T(8,128)(2,1)S(1)}, u32[]{:S(2)}, u32[]{:S(2)}) collective-permute-start(bf16[112,2240]{1,0:T(8,128)(2,1)S(1)} %half_of.2), channel_id=1, source_target_pairs={{0,2},{1,3},{2,0},{3,1},{4,6},{5,7},{6,4},{7,5},{8,10},{9,11},{10,... | collective-permute-start | bytes 1505288 | tf_op jit(solution)/shard_map/ppermute | solution.py:359
  34.2 13.9 %collective-permute-start.19 = (bf16[112,2240]{1,0:T(8,128)(2,1)}, bf16[112,2240]{1,0:T(8,128)(2,1)S(1)}, u32[]{:S(2)}, u32[]{:S(2)}) collective-permute-start(bf16[112,2240]{1,0:T(8,128)(2,1)} %collective-permute-done.11.refs_3_), channel_id=1, source_target_pairs={{4,8},{5,9},{6,10},{7,11},{8,4},{9,5},{10,6},{11,7},{20,24},{21,25... | collective-permute-start | bytes 1505288 | tf_op jit(solution)/shard_map/ppermute | solution.py:359
  36.3 10.3 %collective-permute-start.4 = (bf16[560,128]{1,0:T(8,128)(2,1)S(1)}, bf16[560,128]{1,0:T(8,128)(2,1)S(1)}, u32[]{:S(2)}, u32[]{:S(2)}) collective-permute-start(bf16[560,128]{1,0:T(8,128)(2,1)S(1)} %add_convert_fusion.1.s0), channel_id=1, source_target_pairs={{0,1},{1,0},{2,3},{3,2},{4,5},{5,4},{6,7},{7,6},{8,9},{9,8},{10,11... | collective-permute-start | bytes 430088 | tf_op jit(solution)/shard_map/ppermute | solution.py:359
  36.4 17.6 %collective-permute-start.15 = (bf16[112,2240]{1,0:T(8,128)(2,1)S(1)}, bf16[112,2240]{1,0:T(8,128)(2,1)}, u32[]{:S(2)}, u32[]{:S(2)}) collective-permute-start(bf16[112,2240]{1,0:T(8,128)(2,1)S(1)} %half_of.2), channel_id=1, source_target_pairs={{4,8},{5,9},{6,10},{7,11},{8,4},{9,5},{10,6},{11,7},{20,24},{21,25... | collective-permute-start | bytes 1505288 | tf_op jit(solution)/shard_map/ppermute | solution.py:359
  39.0 15.6 %collective-permute-start.17 = (bf16[112,2240]{1,0:T(8,128)(2,1)S(1)}, bf16[112,2240]{1,0:T(8,128)(2,1)}, u32[]{:S(2)}, u32[]{:S(2)}) collective-permute-start(bf16[112,2240]{1,0:T(8,128)(2,1)S(1)} %half_of.3), channel_id=1, source_target_pairs={{4,8},{5,9},{6,10},{7,11},{8,4},{9,5},{10,6},{11,7},{20,24},{21,25... | collective-permute-start | bytes 1505288 | tf_op jit(solution)/shard_map/ppermute | solution.py:359
  46.6 11.7 %collective-permute-start.10 = (bf16[112,2240]{1,0:T(8,128)(2,1)S(1)}, bf16[112,2240]{1,0:T(8,128)(2,1)S(1)}, u32[]{:S(2)}, u32[]{:S(2)}) collective-permute-start(bf16[112,2240]{1,0:T(8,128)(2,1)S(1)} %collective-permute-done.9.refs_1_), channel_id=1, source_target_pairs={{0,16},{1,17},{2,18},{3,19},{4,20},{5,21},{6,22},{7,23},{8,24},{9,... | collective-permute-start | bytes 1505288 | tf_op jit(solution)/shard_map/ppermute | solution.py:359
  48.1 16.3 %collective-permute-start.20 = (bf16[112,2240]{1,0:T(8,128)(2,1)S(1)}, bf16[112,2240]{1,0:T(8,128)(2,1)S(1)}, u32[]{:S(2)}, u32[]{:S(2)}) collective-permute-start(bf16[112,2240]{1,0:T(8,128)(2,1)S(1)} %collective-permute-done.19.b), channel_id=1, source_target_pairs={{4,0},{5,1},{6,2},{7,3},{8,12},{9,13},{10,14},{11,15},{20,16},{21,... | collective-permute-start | bytes 1505288 | tf_op jit(solution)/shard_map/ppermute | solution.py:359
  53.8 48.6 %collective-permute-start.7 = (bf16[2240,256]{1,0:T(8,128)(2,1)S(1)}, bf16[2240,256]{1,0:T(8,128)(2,1)S(1)}, u32[]{:S(2)}, u32[]{:S(2)}) collective-permute-start(bf16[2240,256]{1,0:T(8,128)(2,1)S(1)} %attend.2.n_own), channel_id=1, source_target_pairs={{0,1},{1,0},{2,3},{3,2},{4,5},{5,4},{6,7},{7,6},{8,9},{9,8},{10,11... | collective-permute-start | bytes 3440648 | tf_op jit(solution)/shard_map/ppermute | solution.py:359
  54.0 15.3 %collective-permute-start.13 = (bf16[112,2240]{1,0:T(8,128)(2,1)}, bf16[112,2240]{1,0:T(8,128)(2,1)}, u32[]{:S(2)}, u32[]{:S(2)}) collective-permute-start(bf16[112,2240]{1,0:T(8,128)(2,1)} %collective-permute-done.11.refs_3_), channel_id=1, source_target_pairs={{0,2},{1,3},{2,0},{3,1},{4,6},{5,7},{6,4},{7,5},{8,10},{9,11},{10,... | collective-permute-start | bytes 1505288 | tf_op jit(solution)/shard_map/ppermute | solution.py:359
  54.5 16.3 %collective-permute-start.12 = (bf16[112,2240]{1,0:T(8,128)(2,1)}, bf16[112,2240]{1,0:T(8,128)(2,1)}, u32[]{:S(2)}, u32[]{:S(2)}) collective-permute-start(bf16[112,2240]{1,0:T(8,128)(2,1)} %collective-permute-done.11.refs_3_), channel_id=1, source_target_pairs={{0,16},{1,17},{2,18},{3,19},{4,20},{5,21},{6,22},{7,23},{8,24},{9,... | collective-permute-start | bytes 1505288 | tf_op jit(solution)/shard_map/ppermute | solution.py:359
  59.0 30.9 %collective-permute-start.16 = (bf16[112,2240]{1,0:T(8,128)(2,1)}, bf16[112,2240]{1,0:T(8,128)(2,1)}, u32[]{:S(2)}, u32[]{:S(2)}) collective-permute-start(bf16[112,2240]{1,0:T(8,128)(2,1)} %collective-permute-done.15.b), channel_id=1, source_target_pairs={{4,0},{5,1},{6,2},{7,3},{8,12},{9,13},{10,14},{11,15},{20,16},{21,... | collective-permute-start | bytes 1505288 | tf_op jit(solution)/shard_map/ppermute | solution.py:359
  65.1 34.6 %collective-permute-start.18 = (bf16[112,2240]{1,0:T(8,128)(2,1)}, bf16[112,2240]{1,0:T(8,128)(2,1)}, u32[]{:S(2)}, u32[]{:S(2)}) collective-permute-start(bf16[112,2240]{1,0:T(8,128)(2,1)} %collective-permute-done.17.b), channel_id=1, source_target_pairs={{4,0},{5,1},{6,2},{7,3},{8,12},{9,13},{10,14},{11,15},{20,16},{21,... | collective-permute-start | bytes 1505288 | tf_op jit(solution)/shard_map/ppermute | solution.py:359
  69.4 33.0 %collective-permute-start.14 = (bf16[112,2240]{1,0:T(8,128)(2,1)}, bf16[112,2240]{1,0:T(8,128)(2,1)}, u32[]{:S(2)}, u32[]{:S(2)}) collective-permute-start(bf16[112,2240]{1,0:T(8,128)(2,1)} %collective-permute-done.13.refs_5_), channel_id=1, source_target_pairs={{0,16},{1,17},{2,18},{3,19},{4,20},{5,21},{6,22},{7,23},{8,24},{9,... | collective-permute-start | bytes 1505288 | tf_op jit(solution)/shard_map/ppermute | solution.py:359
  70.8 31.5 %collective-permute-start.21 = (bf16[112,2240]{1,0:T(8,128)(2,1)}, bf16[112,2240]{1,0:T(8,128)(2,1)}, u32[]{:S(2)}, u32[]{:S(2)}) collective-permute-start(bf16[112,2240]{1,0:T(8,128)(2,1)} %pick.5.refs_9_), channel_id=1, source_target_pairs={{0,16},{1,17},{2,18},{3,19},{4,20},{5,21},{6,22},{7,23},{8,24},{9,... | collective-permute-start | bytes 1505288 | tf_op jit(solution)/shard_map/ppermute | solution.py:359
  90.0 27.3 %collective-permute-start.25 = (bf16[112,2240]{1,0:T(8,128)(2,1)}, bf16[112,2240]{1,0:T(8,128)(2,1)}, u32[]{:S(2)}, u32[]{:S(2)}) collective-permute-start(bf16[112,2240]{1,0:T(8,128)(2,1)} %pick.5.refs_9_), channel_id=1, source_target_pairs={{0,2},{1,3},{2,0},{3,1},{4,6},{5,7},{6,4},{7,5},{8,10},{9,11},{10,... | collective-permute-start | bytes 1505288 | tf_op jit(solution)/shard_map/ppermute | solution.py:359
  99.7 19.0 %collective-permute-start.8 = (bf16[2240,128]{1,0:T(8,128)(2,1)}, bf16[2240,128]{1,0:T(8,128)(2,1)}, u32[]{:S(2)}, u32[]{:S(2)}) collective-permute-start(bf16[2240,128]{1,0:T(8,128)(2,1)} %attend.3.z_own), channel_id=1, source_target_pairs={{0,1},{1,0},{2,3},{3,2},{4,5},{5,4},{6,7},{7,6},{8,9},{9,8},{10,11... | collective-permute-start | bytes 1720328 | tf_op jit(solution)/shard_map/ppermute | solution.py:359
  106.3 17.3 %collective-permute-start.28 = (bf16[432,512]{1,0:T(8,128)(2,1)S(1)}, bf16[432,512]{1,0:T(8,128)(2,1)S(1)}, u32[]{:S(2)}, u32[]{:S(2)}) collective-permute-start(bf16[432,512]{1,0:T(8,128)(2,1)S(1)} %get-tuple-element.23), channel_id=1, source_target_pairs={{0,4},{1,5},{2,6},{3,7},{4,8},{5,9},{6,10},{7,11},{8,12},{9,13},{1... | collective-permute-start | bytes 1327112 | tf_op jit(solution)/shard_map/ppermute | solution.py:359
  115.2 14.7 %collective-permute-start.23 = (bf16[112,2240]{1,0:T(8,128)(2,1)S(1)}, bf16[112,2240]{1,0:T(8,128)(2,1)S(1)}, u32[]{:S(2)}, u32[]{:S(2)}) collective-permute-start(bf16[112,2240]{1,0:T(8,128)(2,1)S(1)} %pick.3.refs_7_), channel_id=1, source_target_pairs={{0,2},{1,3},{2,0},{3,1},{4,6},{5,7},{6,4},{7,5},{8,10},{9,11},{10,... | collective-permute-start | bytes 1505288 | tf_op jit(solution)/shard_map/ppermute | solution.py:359
  115.6 23.0 %collective-permute-start.24 = (bf16[112,2240]{1,0:T(8,128)(2,1)S(1)}, bf16[112,2240]{1,0:T(8,128)(2,1)S(1)}, u32[]{:S(2)}, u32[]{:S(2)}) collective-permute-start(bf16[112,2240]{1,0:T(8,128)(2,1)S(1)} %pick.4.refs_8_), channel_id=1, source_target_pairs={{0,2},{1,3},{2,0},{3,1},{4,6},{5,7},{6,4},{7,5},{8,10},{9,11},{10,... | collective-permute-start | bytes 1505288 | tf_op jit(solution)/shard_map/ppermute | solution.py:359
  117.3 21.3 %collective-permute-start.26 = (bf16[112,2240]{1,0:T(8,128)(2,1)}, bf16[112,2240]{1,0:T(8,128)(2,1)S(1)}, u32[]{:S(2)}, u32[]{:S(2)}) collective-permute-start(bf16[112,2240]{1,0:T(8,128)(2,1)} %collective-permute-done.25.refs_2_), channel_id=1, source_target_pairs={{0,16},{1,17},{2,18},{3,19},{4,20},{5,21},{6,22},{7,23},{8,24},{9,... | collective-permute-start | bytes 1505288 | tf_op jit(solution)/shard_map/ppermute | solution.py:359
  123.3 25.9 %collective-permute-start.22 = (f32[432,384]{1,0:T(8,128)S(1)}, f32[432,384]{1,0:T(8,128)S(1)}, u32[]{:S(2)}, u32[]{:S(2)}) collective-permute-start(f32[432,384]{1,0:T(8,128)S(1)} %get-tuple-element.19), channel_id=1, source_target_pairs={{0,1},{1,0},{2,3},{3,2},{4,5},{5,4},{6,7},{7,6},{8,9},{9,8},{10,11... | collective-permute-start | bytes 1990664 | tf_op jit(solution)/shard_map/ppermute | solution.py:359
  123.6 25.6 %collective-permute-start.29 = (bf16[432,512]{1,0:T(8,128)(2,1)S(1)}, bf16[432,512]{1,0:T(8,128)(2,1)S(1)}, u32[]{:S(2)}, u32[]{:S(2)}) collective-permute-start(bf16[432,512]{1,0:T(8,128)(2,1)S(1)} %collective-permute-done.28.refs_4_), channel_id=1, source_target_pairs={{0,1},{1,0},{2,3},{3,2},{4,5},{5,4},{6,7},{7,6},{8,9},{9,8},{10,11... | collective-permute-start | bytes 1327112 | tf_op jit(solution)/shard_map/ppermute | solution.py:359
  (28 other events, 168.5 us)

commit v5 on v4

--- a/solution.py
+++ b/solution.py
@@ -106,10 +106,10 @@
         copy.wait()
 
 
-def half_of(x, whole, half):
-    rows, width = whole.shape
+def half_of(x, whole, half, step):
+    width = whole.shape[1]
     return pl.pallas_call(
-        functools.partial(slice_kernel, rows - half),
+        functools.partial(slice_kernel, step),
         in_specs=[SMEM, ANY],
         out_specs=VMEM,
         out_shape=pltpu.VMEM((half, width), whole.dtype),
@@ -229,7 +229,7 @@
     )(mine, queries, *states, gain)
 
 
-def place(x, cols, half, tap, shards, w):
+def place(x, cols, tap, shards, w):
     rows = 3 * cols
     lo_tap, hi_tap = tap * cols, (tap + 1) * cols
 
@@ -250,11 +250,10 @@
         def _(flag=flag):
             for slot, shard in enumerate(shards):
                 if len(shard) == 2:
-                    for ref, top in ((shard[0], flag), (shard[1], not flag)):
-                        if top:
-                            put(ref, slot, 0, half, 0)
-                        else:
-                            put(ref, slot, half, rows, rows - half)
+                    top, bottom = shard if flag else shard[::-1]
+                    count = bottom.shape[0]
+                    put(top, slot, 0, top.shape[0], 0)
+                    put(bottom, slot, rows - count, rows, rows - count)
 
 
 def dot(a, b):
@@ -279,7 +278,7 @@
     return jnp.concatenate([own[:, at], other[:, at]], axis=1)
 
 
-def rim_kernel(cols, half, part, code, n_own, n_other, *refs):
+def rim_kernel(cols, part, code, n_own, n_other, *refs):
     pieces, (out, w) = refs[:-2], refs[-2:]
     x, _, _, _ = where_of(code[0])
     shards = []
@@ -287,7 +286,7 @@
         shards, pieces = [pieces[:1]], pieces[1:]
     shards += [pieces[i : i + 2] for i in range(0, len(pieces), 2)]
     for tap in (2, 1, 0):
-        place(x, cols, half, tap, shards, w.at[tap])
+        place(x, cols, tap, shards, w.at[tap])
     p = n_own.shape[1] // 2
     first = both_cores(n_own, n_other, pl.ds(0, p))
     last = both_cores(n_own, n_other, pl.ds(p, p))
@@ -389,8 +388,8 @@
     rows = 3 * cols
     half = -(-rows // 16) * 8
     whole = conv_weight.transpose(0, 2, 1).reshape(rows, width)
-    piece = half_of(side, whole, half)
-    rest = half_of(1 - side, whole, half)
+    piece = half_of(side, whole, half, rows - half)
+    rest = half_of(1 - side, whole, rows - half, half)
     zp1 = send(piece, along(z0=1, z1=0, z2=3, z3=2))
     zp2 = send(piece, along(z1=2, z2=1))
     zp3 = send(zp1, along(z1=2, z2=1))
@@ -444,7 +443,7 @@
     for name, pieces in (("a", early_pieces), ("b", late_pieces)):
         count = cols * len(blocks_of("ab".index(name), z, y))
         rim, w = pl.pallas_call(
-            functools.partial(rim_kernel, cols, half, "ab".index(name)),
+            functools.partial(rim_kernel, cols, "ab".index(name)),
             in_specs=[SMEM] + [VMEM] * (2 + len(pieces)),
             out_specs=[VMEM] * 2,
             out_shape=[

time: 152 us -> 161 us (1.059)
  the two profiles are of different devices: /device:TPU:0 before, /device:TPU:18 now
where the time goes in v5:
time: 161 us; the launch traced here: 158 us
  waiting for transfers between devices  79.2 us (49%)
  starting transfers between devices  38.8 us (24%)
  Pallas kernels  27.4 us (17%)
  local copies, waits for them, and re-layouts  11.2 us (7%)
    ppermute x32, waiting for transfers between devices, send(): moved = lax.ppermute(block, axes, route)  79.2 us
    ppermute x32, starting transfers between devices, send(): moved = lax.ppermute(block, axes, route)  38.8 us
    unnamed x40, local copies, waits for them, and re-layouts  10.9 us
    pallas_call x2, Pallas kernels, tuned(): pl.pallas_call(own_kernel, in_specs=[VMEM] * 5, out_specs=[VMEM] * 2, out...  7.04 us
    pallas_call x1, Pallas kernels, local_state(): pl.pallas_call(state_kernel, grid_spec=pltpu.PrefetchScalarGridSpec(num_s...  6.29 us
    pallas_call x2, Pallas kernels, tuned(): pl.pallas_call(functools.partial(rim_kernel, cols, 'ab'.index(name)), in_...  6.11 us
  transfers between devices with their start and end apart: 32, of which 15 were waited for; matrix products, arithmetic and copies ran while one was open for 0% of the time, Pallas kernels for 12%

profile of v5, /device:TPU:18, one launch (start us, length us, event | category | flops | bytes accessed | tf_op | source)
XLA Modules:
  0.0 158.3 jit_solution(12925855887605471279)
XLA Ops:
  0.0 6.3 %local_state.1 = (bf16[1120,128]{1,0:T(8,128)(2,1)}, bf16[1120,128]{1,0:T(8,128)(2,1)}) custom-call(s32[1]{0:T(128)} %bitcast.1.mine, bf16[3,2240,128]{2,1,0:T(8,128)(2,1)} %bitcast.22, bf16[3,2240,128]{2,1,0:T(8,128)(2,1)} %bitcast.23), custom_call_target="tpu_custom_call" | custom-call | tf_op jit(solution)/shard_map/local_state/pallas_call | solution.py:171
  6.3 1.8 %collective-permute-done = bf16[1120,128]{1,0:T(8,128)(2,1)S(1)} collective-permute-done((bf16[1120,128]{1,0:T(8,128)(2,1)}, bf16[1120,128]{1,0:T(8,128)(2,1)S(1)}, u32[]{:S(2)}, u32[]{:S(2)}) %collective-permute-start) | collective-permute-done | bytes 286752 | tf_op jit(solution)/shard_map/ppermute | solution.py:358
  11.9 1.6 %collective-permute-start.11 = (bf16[112,2240]{1,0:T(8,128)(2,1)S(1)}, bf16[112,2240]{1,0:T(8,128)(2,1)}, u32[]{:S(2)}, u32[]{:S(2)}) collective-permute-start(bf16[112,2240]{1,0:T(8,128)(2,1)S(1)} %half_of.2), channel_id=1, source_target_pairs={{0,4},{1,5},{2,6},{3,7},{4,0},{5,1},{6,2},{7,3},{8,12},{9,13},{10,... | collective-permute-start | bytes 1505288 | tf_op jit(solution)/shard_map/ppermute | solution.py:358
  15.1 3.6 %collective-permute-start.2 = (bf16[560,128]{1,0:T(8,128)(2,1)S(1)}, bf16[560,128]{1,0:T(8,128)(2,1)S(1)}, u32[]{:S(2)}, u32[]{:S(2)}) collective-permute-start(bf16[560,128]{1,0:T(8,128)(2,1)S(1)} %add_convert_fusion.3), channel_id=1, source_target_pairs={{0,4},{1,5},{2,6},{3,7},{4,8},{5,9},{6,10},{7,11},{8,12},{9,13},{1... | collective-permute-start | bytes 430088 | tf_op jit(solution)/shard_map/ppermute | solution.py:358
  18.7 8.9 %collective-permute-done.2 = bf16[560,128]{1,0:T(8,128)(2,1)S(1)} collective-permute-done((bf16[560,128]{1,0:T(8,128)(2,1)S(1)}, bf16[560,128]{1,0:T(8,128)(2,1)S(1)}, u32[]{:S(2)}, u32[]{:S(2)}) %collective-permute-start.2) | collective-permute-done | bytes 143392 | tf_op jit(solution)/shard_map/ppermute | solution.py:358
  30.1 6.5 %collective-permute-start.17 = (bf16[104,2240]{1,0:T(8,128)(2,1)S(1)}, bf16[104,2240]{1,0:T(8,128)(2,1)S(1)}, u32[]{:S(2)}, u32[]{:S(2)}) collective-permute-start(bf16[104,2240]{1,0:T(8,128)(2,1)S(1)} %half_of.3), channel_id=1, source_target_pairs={{4,8},{5,9},{6,10},{7,11},{8,4},{9,5},{10,6},{11,7},{20,24},{21,25... | collective-permute-start | bytes 1397768 | tf_op jit(solution)/shard_map/ppermute | solution.py:358
  36.5 1.9 %collective-permute-start.19 = (bf16[112,2240]{1,0:T(8,128)(2,1)}, bf16[112,2240]{1,0:T(8,128)(2,1)S(1)}, u32[]{:S(2)}, u32[]{:S(2)}) collective-permute-start(bf16[112,2240]{1,0:T(8,128)(2,1)} %collective-permute-done.11.refs_3_), channel_id=1, source_target_pairs={{4,8},{5,9},{6,10},{7,11},{8,4},{9,5},{10,6},{11,7},{20,24},{21,25... | collective-permute-start | bytes 1505288 | tf_op jit(solution)/shard_map/ppermute | solution.py:358
  39.2 3.9 %collective-permute-start.15 = (bf16[112,2240]{1,0:T(8,128)(2,1)S(1)}, bf16[112,2240]{1,0:T(8,128)(2,1)}, u32[]{:S(2)}, u32[]{:S(2)}) collective-permute-start(bf16[112,2240]{1,0:T(8,128)(2,1)S(1)} %half_of.2), channel_id=1, source_target_pairs={{4,8},{5,9},{6,10},{7,11},{8,4},{9,5},{10,6},{11,7},{20,24},{21,25... | collective-permute-start | bytes 1505288 | tf_op jit(solution)/shard_map/ppermute | solution.py:358
  43.1 5.8 %collective-permute-done.17.b = bf16[104,2240]{1,0:T(8,128)(2,1)S(1)} collective-permute-done((bf16[104,2240]{1,0:T(8,128)(2,1)S(1)}, bf16[104,2240]{1,0:T(8,128)(2,1)S(1)}, u32[]{:S(2)}, u32[]{:S(2)}) %collective-permute-start.17) | collective-permute-done | bytes 465952 | tf_op jit(solution)/shard_map/ppermute | solution.py:358
  50.7 9.2 %collective-permute-done.19.b = bf16[112,2240]{1,0:T(8,128)(2,1)S(1)} collective-permute-done((bf16[112,2240]{1,0:T(8,128)(2,1)}, bf16[112,2240]{1,0:T(8,128)(2,1)S(1)}, u32[]{:S(2)}, u32[]{:S(2)}) %collective-permute-start.19) | collective-permute-done | bytes 501792 | tf_op jit(solution)/shard_map/ppermute | solution.py:358
  64.7 6.0 %collective-permute-done.15.b = bf16[112,2240]{1,0:T(8,128)(2,1)} collective-permute-done((bf16[112,2240]{1,0:T(8,128)(2,1)S(1)}, bf16[112,2240]{1,0:T(8,128)(2,1)}, u32[]{:S(2)}, u32[]{:S(2)}) %collective-permute-start.15) | collective-permute-done | bytes 501792 | tf_op jit(solution)/shard_map/ppermute | solution.py:358
  74.3 3.6 %collective-permute-start.16 = (bf16[112,2240]{1,0:T(8,128)(2,1)}, bf16[112,2240]{1,0:T(8,128)(2,1)}, u32[]{:S(2)}, u32[]{:S(2)}) collective-permute-start(bf16[112,2240]{1,0:T(8,128)(2,1)} %collective-permute-done.15.b), channel_id=1, source_target_pairs={{4,0},{5,1},{6,2},{7,3},{8,12},{9,13},{10,14},{11,15},{20,16},{21,... | collective-permute-start | bytes 1505288 | tf_op jit(solution)/shard_map/ppermute | solution.py:358
  81.3 4.3 %collective-permute-done.10.refs_2_ = bf16[112,2240]{1,0:T(8,128)(2,1)} collective-permute-done((bf16[112,2240]{1,0:T(8,128)(2,1)}, bf16[112,2240]{1,0:T(8,128)(2,1)}, u32[]{:S(2)}, u32[]{:S(2)}) %collective-permute-start.10) | collective-permute-done | bytes 501792 | tf_op jit(solution)/shard_map/ppermute | solution.py:358
  86.1 10.5 %collective-permute-done.12.refs_4_ = bf16[112,2240]{1,0:T(8,128)(2,1)} collective-permute-done((bf16[112,2240]{1,0:T(8,128)(2,1)}, bf16[112,2240]{1,0:T(8,128)(2,1)}, u32[]{:S(2)}, u32[]{:S(2)}) %collective-permute-start.12) | collective-permute-done | bytes 501792 | tf_op jit(solution)/shard_map/ppermute | solution.py:358
  107.7 9.8 %collective-permute-done.21.refs_10_ = bf16[112,2240]{1,0:T(8,128)(2,1)} collective-permute-done((bf16[112,2240]{1,0:T(8,128)(2,1)}, bf16[112,2240]{1,0:T(8,128)(2,1)}, u32[]{:S(2)}, u32[]{:S(2)}) %collective-permute-start.21) | collective-permute-done | bytes 501792 | tf_op jit(solution)/shard_map/ppermute | solution.py:358
  117.5 4.2 %rim.2 = (bf16[432,512]{1,0:T(8,128)(2,1)S(1)}, bf16[3,432,2240]{2,1,0:T(8,128)(2,1)S(1)}) custom-call(s32[1]{0:T(128)} %bitcast.code, bf16[2240,256]{1,0:T(8,128)(2,1)S(1)} %attend.2.n_own, bf16[2240,256]{1,0:T(8,128)(2,1)S(1)} %collective-permute-done.7.n_other, bf16[216,2240]{1,0:T(8,128)(2,1)S(1)} %bitcast.19, ...), custom_call_target="tpu_custom_call" | custom-call | tf_op jit(solution)/shard_map/rim/pallas_call | solution.py:445
  121.7 1.9 %collective-permute-start.28 = (bf16[432,512]{1,0:T(8,128)(2,1)S(1)}, bf16[432,512]{1,0:T(8,128)(2,1)S(1)}, u32[]{:S(2)}, u32[]{:S(2)}) collective-permute-start(bf16[432,512]{1,0:T(8,128)(2,1)S(1)} %get-tuple-element.23), channel_id=1, source_target_pairs={{0,4},{1,5},{2,6},{3,7},{4,8},{5,9},{6,10},{7,11},{8,12},{9,13},{1... | collective-permute-start | bytes 1327112 | tf_op jit(solution)/shard_map/ppermute | solution.py:358
  126.3 4.5 %own.2 = (f32[432,384]{1,0:T(8,128)S(1)}, f32[432,384]{1,0:T(8,128)S(1)}) custom-call(bf16[2240,256]{1,0:T(8,128)(2,1)S(1)} %attend.2.n_own, bf16[2240,256]{1,0:T(8,128)(2,1)S(1)} %collective-permute-done.7.n_other, bf16[2240,128]{1,0:T(8,128)(2,1)} %attend.3.z_own, bf16[2240,128]{1,0:T(8,128)(2,1)} %collective-permute-done.8.z_other, ...), custom_call_target="tpu_custom_call" | custom-call | tf_op jit(solution)/shard_map/own/pallas_call | solution.py:458
  130.9 3.6 %collective-permute-done.28.refs_4_ = bf16[432,512]{1,0:T(8,128)(2,1)S(1)} collective-permute-done((bf16[432,512]{1,0:T(8,128)(2,1)S(1)}, bf16[432,512]{1,0:T(8,128)(2,1)S(1)}, u32[]{:S(2)}, u32[]{:S(2)}) %collective-permute-start.28) | collective-permute-done | bytes 442400 | tf_op jit(solution)/shard_map/ppermute | solution.py:358
  134.5 11.9 %collective-permute-done.24.refs_1_ = bf16[104,2240]{1,0:T(8,128)(2,1)S(1)} collective-permute-done((bf16[104,2240]{1,0:T(8,128)(2,1)S(1)}, bf16[104,2240]{1,0:T(8,128)(2,1)S(1)}, u32[]{:S(2)}, u32[]{:S(2)}) %collective-permute-start.24) | collective-permute-done | bytes 465952 | tf_op jit(solution)/shard_map/ppermute | solution.py:358
  146.5 1.9 %rim.3 = (bf16[144,512]{1,0:T(8,128)(2,1)S(1)}, bf16[3,144,2240]{2,1,0:T(8,128)(2,1)S(1)}) custom-call(s32[1]{0:T(128)} %bitcast.code, bf16[2240,256]{1,0:T(8,128)(2,1)S(1)} %attend.2.n_own, bf16[2240,256]{1,0:T(8,128)(2,1)S(1)} %collective-permute-done.7.n_other, bf16[112,2240]{1,0:T(8,128)(2,1)S(1)} %collective-permute-done.23.refs_0_, ...), custom_call_target="tpu_custom_call" | custom-call | tf_op jit(solution)/shard_map/rim/pallas_call | solution.py:445
  148.4 1.9 %collective-permute-start.30 = (bf16[144,512]{1,0:T(8,128)(2,1)S(1)}, bf16[144,512]{1,0:T(8,128)(2,1)S(1)}, u32[]{:S(2)}, u32[]{:S(2)}) collective-permute-start(bf16[144,512]{1,0:T(8,128)(2,1)S(1)} %get-tuple-element.24), channel_id=1, source_target_pairs={{0,4},{1,5},{2,6},{3,7},{4,8},{5,9},{6,10},{7,11},{8,12},{9,13},{1... | collective-permute-start | bytes 442376 | tf_op jit(solution)/shard_map/ppermute | solution.py:358
  150.3 2.5 %own.3 = (f32[144,384]{1,0:T(8,128)S(1)}, f32[144,384]{1,0:T(8,128)S(1)}) custom-call(bf16[2240,256]{1,0:T(8,128)(2,1)S(1)} %attend.2.n_own, bf16[2240,256]{1,0:T(8,128)(2,1)S(1)} %collective-permute-done.7.n_other, bf16[2240,128]{1,0:T(8,128)(2,1)} %attend.3.z_own, bf16[2240,128]{1,0:T(8,128)(2,1)} %collective-permute-done.8.z_other, ...), custom_call_target="tpu_custom_call" | custom-call | tf_op jit(solution)/shard_map/own/pallas_call | solution.py:458
  152.9 2.5 %collective-permute-done.30.refs_6_ = bf16[144,512]{1,0:T(8,128)(2,1)S(1)} collective-permute-done((bf16[144,512]{1,0:T(8,128)(2,1)S(1)}, bf16[144,512]{1,0:T(8,128)(2,1)S(1)}, u32[]{:S(2)}, u32[]{:S(2)}) %collective-permute-start.30) | collective-permute-done | bytes 147488 | tf_op jit(solution)/shard_map/ppermute | solution.py:358
  (99 shorter events, 39.2 us)
Async XLA Ops:
  11.9 24.7 %collective-permute-start.11 = (bf16[112,2240]{1,0:T(8,128)(2,1)S(1)}, bf16[112,2240]{1,0:T(8,128)(2,1)}, u32[]{:S(2)}, u32[]{:S(2)}) collective-permute-start(bf16[112,2240]{1,0:T(8,128)(2,1)S(1)} %half_of.2), channel_id=1, source_target_pairs={{0,4},{1,5},{2,6},{3,7},{4,0},{5,1},{6,2},{7,3},{8,12},{9,13},{10,... | collective-permute-start | bytes 1505288 | tf_op jit(solution)/shard_map/ppermute | solution.py:358
  15.1 12.5 %collective-permute-start.2 = (bf16[560,128]{1,0:T(8,128)(2,1)S(1)}, bf16[560,128]{1,0:T(8,128)(2,1)S(1)}, u32[]{:S(2)}, u32[]{:S(2)}) collective-permute-start(bf16[560,128]{1,0:T(8,128)(2,1)S(1)} %add_convert_fusion.3), channel_id=1, source_target_pairs={{0,4},{1,5},{2,6},{3,7},{4,8},{5,9},{6,10},{7,11},{8,12},{9,13},{1... | collective-permute-start | bytes 430088 | tf_op jit(solution)/shard_map/ppermute | solution.py:358
  30.1 18.8 %collective-permute-start.17 = (bf16[104,2240]{1,0:T(8,128)(2,1)S(1)}, bf16[104,2240]{1,0:T(8,128)(2,1)S(1)}, u32[]{:S(2)}, u32[]{:S(2)}) collective-permute-start(bf16[104,2240]{1,0:T(8,128)(2,1)S(1)} %half_of.3), channel_id=1, source_target_pairs={{4,8},{5,9},{6,10},{7,11},{8,4},{9,5},{10,6},{11,7},{20,24},{21,25... | collective-permute-start | bytes 1397768 | tf_op jit(solution)/shard_map/ppermute | solution.py:358
  36.5 23.4 %collective-permute-start.19 = (bf16[112,2240]{1,0:T(8,128)(2,1)}, bf16[112,2240]{1,0:T(8,128)(2,1)S(1)}, u32[]{:S(2)}, u32[]{:S(2)}) collective-permute-start(bf16[112,2240]{1,0:T(8,128)(2,1)} %collective-permute-done.11.refs_3_), channel_id=1, source_target_pairs={{4,8},{5,9},{6,10},{7,11},{8,4},{9,5},{10,6},{11,7},{20,24},{21,25... | collective-permute-start | bytes 1505288 | tf_op jit(solution)/shard_map/ppermute | solution.py:358
  38.6 25.5 %collective-permute-start.9 = (bf16[112,2240]{1,0:T(8,128)(2,1)S(1)}, bf16[112,2240]{1,0:T(8,128)(2,1)}, u32[]{:S(2)}, u32[]{:S(2)}) collective-permute-start(bf16[112,2240]{1,0:T(8,128)(2,1)S(1)} %half_of.2), channel_id=1, source_target_pairs={{0,2},{1,3},{2,0},{3,1},{4,6},{5,7},{6,4},{7,5},{8,10},{9,11},{10,... | collective-permute-start | bytes 1505288 | tf_op jit(solution)/shard_map/ppermute | solution.py:358
  39.2 31.5 %collective-permute-start.15 = (bf16[112,2240]{1,0:T(8,128)(2,1)S(1)}, bf16[112,2240]{1,0:T(8,128)(2,1)}, u32[]{:S(2)}, u32[]{:S(2)}) collective-permute-start(bf16[112,2240]{1,0:T(8,128)(2,1)S(1)} %half_of.2), channel_id=1, source_target_pairs={{4,8},{5,9},{6,10},{7,11},{8,4},{9,5},{10,6},{11,7},{20,24},{21,25... | collective-permute-start | bytes 1505288 | tf_op jit(solution)/shard_map/ppermute | solution.py:358
  48.9 12.4 %collective-permute-start.5 = (bf16[560,128]{1,0:T(8,128)(2,1)S(1)}, bf16[560,128]{1,0:T(8,128)(2,1)S(1)}, u32[]{:S(2)}, u32[]{:S(2)}) collective-permute-start(bf16[560,128]{1,0:T(8,128)(2,1)S(1)} %add_convert_fusion.1.s0), channel_id=1, source_target_pairs={{0,2},{1,3},{2,0},{3,1},{4,6},{5,7},{6,4},{7,5},{8,10},{9,11},{10,... | collective-permute-start | bytes 430088 | tf_op jit(solution)/shard_map/ppermute | solution.py:358
  49.4 21.8 %collective-permute-start.18 = (bf16[104,2240]{1,0:T(8,128)(2,1)S(1)}, bf16[104,2240]{1,0:T(8,128)(2,1)S(1)}, u32[]{:S(2)}, u32[]{:S(2)}) collective-permute-start(bf16[104,2240]{1,0:T(8,128)(2,1)S(1)} %collective-permute-done.17.b), channel_id=1, source_target_pairs={{4,0},{5,1},{6,2},{7,3},{8,12},{9,13},{10,14},{11,15},{20,16},{21,... | collective-permute-start | bytes 1397768 | tf_op jit(solution)/shard_map/ppermute | solution.py:358
  59.9 13.5 %collective-permute-start.20 = (bf16[112,2240]{1,0:T(8,128)(2,1)S(1)}, bf16[112,2240]{1,0:T(8,128)(2,1)S(1)}, u32[]{:S(2)}, u32[]{:S(2)}) collective-permute-start(bf16[112,2240]{1,0:T(8,128)(2,1)S(1)} %collective-permute-done.19.b), channel_id=1, source_target_pairs={{4,0},{5,1},{6,2},{7,3},{8,12},{9,13},{10,14},{11,15},{20,16},{21,... | collective-permute-start | bytes 1505288 | tf_op jit(solution)/shard_map/ppermute | solution.py:358
  64.0 53.5 %collective-permute-start.7 = (bf16[2240,256]{1,0:T(8,128)(2,1)S(1)}, bf16[2240,256]{1,0:T(8,128)(2,1)S(1)}, u32[]{:S(2)}, u32[]{:S(2)}) collective-permute-start(bf16[2240,256]{1,0:T(8,128)(2,1)S(1)} %attend.2.n_own), channel_id=1, source_target_pairs={{0,1},{1,0},{2,3},{3,2},{4,5},{5,4},{6,7},{7,6},{8,9},{9,8},{10,11... | collective-permute-start | bytes 3440648 | tf_op jit(solution)/shard_map/ppermute | solution.py:358
  64.2 16.6 %collective-permute-start.13 = (bf16[112,2240]{1,0:T(8,128)(2,1)}, bf16[112,2240]{1,0:T(8,128)(2,1)}, u32[]{:S(2)}, u32[]{:S(2)}) collective-permute-start(bf16[112,2240]{1,0:T(8,128)(2,1)} %collective-permute-done.11.refs_3_), channel_id=1, source_target_pairs={{0,2},{1,3},{2,0},{3,1},{4,6},{5,7},{6,4},{7,5},{8,10},{9,11},{10,... | collective-permute-start | bytes 1505288 | tf_op jit(solution)/shard_map/ppermute | solution.py:358
  70.7 14.9 %collective-permute-start.10 = (bf16[112,2240]{1,0:T(8,128)(2,1)}, bf16[112,2240]{1,0:T(8,128)(2,1)}, u32[]{:S(2)}, u32[]{:S(2)}) collective-permute-start(bf16[112,2240]{1,0:T(8,128)(2,1)} %collective-permute-done.9.refs_1_), channel_id=1, source_target_pairs={{0,16},{1,17},{2,18},{3,19},{4,20},{5,21},{6,22},{7,23},{8,24},{9,... | collective-permute-start | bytes 1505288 | tf_op jit(solution)/shard_map/ppermute | solution.py:358
  72.0 24.7 %collective-permute-start.12 = (bf16[112,2240]{1,0:T(8,128)(2,1)}, bf16[112,2240]{1,0:T(8,128)(2,1)}, u32[]{:S(2)}, u32[]{:S(2)}) collective-permute-start(bf16[112,2240]{1,0:T(8,128)(2,1)} %collective-permute-done.11.refs_3_), channel_id=1, source_target_pairs={{0,16},{1,17},{2,18},{3,19},{4,20},{5,21},{6,22},{7,23},{8,24},{9,... | collective-permute-start | bytes 1505288 | tf_op jit(solution)/shard_map/ppermute | solution.py:358
  74.3 29.3 %collective-permute-start.16 = (bf16[112,2240]{1,0:T(8,128)(2,1)}, bf16[112,2240]{1,0:T(8,128)(2,1)}, u32[]{:S(2)}, u32[]{:S(2)}) collective-permute-start(bf16[112,2240]{1,0:T(8,128)(2,1)} %collective-permute-done.15.b), channel_id=1, source_target_pairs={{4,0},{5,1},{6,2},{7,3},{8,12},{9,13},{10,14},{11,15},{20,16},{21,... | collective-permute-start | bytes 1505288 | tf_op jit(solution)/shard_map/ppermute | solution.py:358
  80.8 27.0 %collective-permute-start.14 = (bf16[112,2240]{1,0:T(8,128)(2,1)}, bf16[112,2240]{1,0:T(8,128)(2,1)}, u32[]{:S(2)}, u32[]{:S(2)}) collective-permute-start(bf16[112,2240]{1,0:T(8,128)(2,1)} %collective-permute-done.13.refs_5_), channel_id=1, source_target_pairs={{0,16},{1,17},{2,18},{3,19},{4,20},{5,21},{6,22},{7,23},{8,24},{9,... | collective-permute-start | bytes 1505288 | tf_op jit(solution)/shard_map/ppermute | solution.py:358
  85.6 31.9 %collective-permute-start.21 = (bf16[112,2240]{1,0:T(8,128)(2,1)}, bf16[112,2240]{1,0:T(8,128)(2,1)}, u32[]{:S(2)}, u32[]{:S(2)}) collective-permute-start(bf16[112,2240]{1,0:T(8,128)(2,1)} %pick.5.refs_9_), channel_id=1, source_target_pairs={{0,16},{1,17},{2,18},{3,19},{4,20},{5,21},{6,22},{7,23},{8,24},{9,... | collective-permute-start | bytes 1505288 | tf_op jit(solution)/shard_map/ppermute | solution.py:358
  96.7 27.6 %collective-permute-start.25 = (bf16[112,2240]{1,0:T(8,128)(2,1)}, bf16[112,2240]{1,0:T(8,128)(2,1)}, u32[]{:S(2)}, u32[]{:S(2)}) collective-permute-start(bf16[112,2240]{1,0:T(8,128)(2,1)} %pick.5.refs_9_), channel_id=1, source_target_pairs={{0,2},{1,3},{2,0},{3,1},{4,6},{5,7},{6,4},{7,5},{8,10},{9,11},{10,... | collective-permute-start | bytes 1505288 | tf_op jit(solution)/shard_map/ppermute | solution.py:358
  103.6 22.7 %collective-permute-start.8 = (bf16[2240,128]{1,0:T(8,128)(2,1)}, bf16[2240,128]{1,0:T(8,128)(2,1)}, u32[]{:S(2)}, u32[]{:S(2)}) collective-permute-start(bf16[2240,128]{1,0:T(8,128)(2,1)} %attend.3.z_own), channel_id=1, source_target_pairs={{0,1},{1,0},{2,3},{3,2},{4,5},{5,4},{6,7},{7,6},{8,9},{9,8},{10,11... | collective-permute-start | bytes 1720328 | tf_op jit(solution)/shard_map/ppermute | solution.py:358
  121.7 12.8 %collective-permute-start.28 = (bf16[432,512]{1,0:T(8,128)(2,1)S(1)}, bf16[432,512]{1,0:T(8,128)(2,1)S(1)}, u32[]{:S(2)}, u32[]{:S(2)}) collective-permute-start(bf16[432,512]{1,0:T(8,128)(2,1)S(1)} %get-tuple-element.23), channel_id=1, source_target_pairs={{0,4},{1,5},{2,6},{3,7},{4,8},{5,9},{6,10},{7,11},{8,12},{9,13},{1... | collective-permute-start | bytes 1327112 | tf_op jit(solution)/shard_map/ppermute | solution.py:358
  123.7 22.8 %collective-permute-start.23 = (bf16[112,2240]{1,0:T(8,128)(2,1)S(1)}, bf16[112,2240]{1,0:T(8,128)(2,1)S(1)}, u32[]{:S(2)}, u32[]{:S(2)}) collective-permute-start(bf16[112,2240]{1,0:T(8,128)(2,1)S(1)} %pick.3.refs_7_), channel_id=1, source_target_pairs={{0,2},{1,3},{2,0},{3,1},{4,6},{5,7},{6,4},{7,5},{8,10},{9,11},{10,... | collective-permute-start | bytes 1505288 | tf_op jit(solution)/shard_map/ppermute | solution.py:358
  124.2 22.2 %collective-permute-start.26 = (bf16[112,2240]{1,0:T(8,128)(2,1)}, bf16[112,2240]{1,0:T(8,128)(2,1)S(1)}, u32[]{:S(2)}, u32[]{:S(2)}) collective-permute-start(bf16[112,2240]{1,0:T(8,128)(2,1)} %collective-permute-done.25.refs_2_), channel_id=1, source_target_pairs={{0,16},{1,17},{2,18},{3,19},{4,20},{5,21},{6,22},{7,23},{8,24},{9,... | collective-permute-start | bytes 1505288 | tf_op jit(solution)/shard_map/ppermute | solution.py:358
  124.8 21.7 %collective-permute-start.24 = (bf16[104,2240]{1,0:T(8,128)(2,1)S(1)}, bf16[104,2240]{1,0:T(8,128)(2,1)S(1)}, u32[]{:S(2)}, u32[]{:S(2)}) collective-permute-start(bf16[104,2240]{1,0:T(8,128)(2,1)S(1)} %pick.4.refs_8_), channel_id=1, source_target_pairs={{0,2},{1,3},{2,0},{3,1},{4,6},{5,7},{6,4},{7,5},{8,10},{9,11},{10,... | collective-permute-start | bytes 1397768 | tf_op jit(solution)/shard_map/ppermute | solution.py:358
  130.8 25.9 %collective-permute-start.22 = (f32[432,384]{1,0:T(8,128)S(1)}, f32[432,384]{1,0:T(8,128)S(1)}, u32[]{:S(2)}, u32[]{:S(2)}) collective-permute-start(f32[432,384]{1,0:T(8,128)S(1)} %get-tuple-element.19), channel_id=1, source_target_pairs={{0,1},{1,0},{2,3},{3,2},{4,5},{5,4},{6,7},{7,6},{8,9},{9,8},{10,11... | collective-permute-start | bytes 1990664 | tf_op jit(solution)/shard_map/ppermute | solution.py:358
  134.5 22.3 %collective-permute-start.29 = (bf16[432,512]{1,0:T(8,128)(2,1)S(1)}, bf16[432,512]{1,0:T(8,128)(2,1)S(1)}, u32[]{:S(2)}, u32[]{:S(2)}) collective-permute-start(bf16[432,512]{1,0:T(8,128)(2,1)S(1)} %collective-permute-done.28.refs_4_), channel_id=1, source_target_pairs={{0,1},{1,0},{2,3},{3,2},{4,5},{5,4},{6,7},{7,6},{8,9},{9,8},{10,11... | collective-permute-start | bytes 1327112 | tf_op jit(solution)/shard_map/ppermute | solution.py:358
  (28 other events, 227.4 us)
